TPU v7x, 256 devices: a whole 4x4x8 slice. The times are simulated.
256 devices in a mesh: rad: 8 (over z), azi: 8 (over y, core), ax: 4 (over x).
Axes of the slice: x: 4, y: 4, z: 8, core: 2. Of those that a mesh axis runs over, the one named last changes fastest.
Arguments:
- primal: float32 [5, 128, 256, 512], P(None, 'rad', 'azi', 'ax'), may hold values from -1 to 4, as said below
- adjoint: float32 [5, 128, 256, 512], P(None, 'rad', 'azi', 'ax'), may hold values from -6 to 6
- refine_flag: int32 [8, 16, 32], P('rad', 'azi', 'ax'), may hold values 0 or 1
- owner_map: int32 [8, 16, 32], P('rad', 'azi', 'ax'), may hold values from 0 to 255
- migrate_weight: int32 [8, 16, 32], P('rad', 'azi', 'ax'), may hold values from 1 to 16
- neighbor_list: int32 [8, 16, 32, 6], P('rad', 'azi', 'ax'), may hold values from 0 to 4095
Outputs:
- indicator: float32 [128, 256, 512], P('rad', 'azi', 'ax')
- block_cost: float32 [8, 16, 32], P('rad', 'azi', 'ax')
- owner_load: float32 [8, 8, 4], P('rad', 'azi', 'ax')
Inputs may be any that keep to these rules, and one draw needn't show every extreme that they name: `primal`: density (field 0) lies in [0.5, 2], momenta (fields 1 to 3) in [-1, 1], energy (field 4) in [2, 4].
All inputs are finite; a program needn't handle non-finite values. No bound on the sum of `refine_flag` on one device may be relied on, other than what follows from the above.
Results may differ from a plain program's by a relative error of at most 0.00002.
Values sent between devices are 32-bit elements; how exact they have to be, the bound alone decides.
A program may use at most 64 MiB of HBM per device.

v0:
```python
import jax
import jax.numpy as jnp
from jax import lax
from jax.sharding import PartitionSpec as P

BLK = 16


def with_halo(block, sides, width, periodic):
    for axis, dim in sides:
        count = lax.axis_size(axis)
        forward = [(i, i + 1) for i in range(count - 1)]
        if periodic:
            forward.append((count - 1, 0))
        backward = [(target, source) for source, target in forward]
        low = lax.ppermute(
            lax.slice_in_dim(block, block.shape[dim] - width, None, axis=dim), axis, forward
        )
        high = lax.ppermute(lax.slice_in_dim(block, 0, width, axis=dim), axis, backward)
        block = jnp.concatenate([low, block, high], axis=dim)
    return block


def euler_flux(face_state, along):
    density = face_state[0]
    momenta = face_state[1:4]
    energy = face_state[4]
    velocity = momenta[along] / density
    kinetic = (
        0.5
        * (momenta[0] * momenta[0] + momenta[1] * momenta[1] + momenta[2] * momenta[2])
        / density
    )
    pressure = 0.4 * (energy - kinetic)
    columns = [
        momenta[along],
        momenta[0] * velocity,
        momenta[1] * velocity,
        momenta[2] * velocity,
        (energy + pressure) * velocity,
    ]
    columns[1 + along] = columns[1 + along] + pressure
    return jnp.stack(columns)


def window(extended, along, start, count, padded_axes):
    pieces = [slice(None)] * 4
    for spatial in padded_axes:
        pieces[spatial] = slice(2, extended.shape[spatial] - 2)
    pieces[along] = slice(start, start + count)
    return extended[tuple(pieces)]


def axis_terms(ext_primal, ext_adjoint, along, padded_axes):
    length = ext_primal.shape[along] - 4
    high = (
        7.0 * window(ext_primal, along, 1, length + 1, padded_axes)
        - window(ext_primal, along, 0, length + 1, padded_axes)
    ) / 12.0
    low = (
        7.0 * window(ext_primal, along, 2, length + 1, padded_axes)
        - window(ext_primal, along, 3, length + 1, padded_axes)
    ) / 12.0
    fluxes = euler_flux(high + low, along - 1)
    balance = lax.slice_in_dim(fluxes, 1, length + 1, axis=along) - lax.slice_in_dim(
        fluxes, 0, length, axis=along
    )
    fourth = (
        window(ext_adjoint, along, 0, length, padded_axes)
        - 4.0 * window(ext_adjoint, along, 1, length, padded_axes)
        + 6.0 * window(ext_adjoint, along, 2, length, padded_axes)
        - 4.0 * window(ext_adjoint, along, 3, length, padded_axes)
        + window(ext_adjoint, along, 4, length, padded_axes)
    ) / 12.0
    return (balance, fourth)


def on_device(primal, adjoint, refine_flag, owner_map, migrate_weight, neighbor_list):
    wrap_primal, wrap_adjoint = (
        with_halo(primal, (("azi", 2),), 2, True),
        with_halo(adjoint, (("azi", 2),), 2, True),
    )
    full_primal, full_adjoint = (
        with_halo(wrap_primal, (("rad", 1), ("ax", 3)), 2, False),
        with_halo(wrap_adjoint, (("rad", 1), ("ax", 3)), 2, False),
    )
    sources = [(full_primal, full_adjoint, (1, 2, 3))] * 3
    balance = jnp.zeros(primal.shape, jnp.float32)
    weight = jnp.zeros(primal.shape, jnp.float32)
    for along in (1, 2, 3):
        ext_primal, ext_adjoint, padded_axes = sources[along - 1]
        part_balance, part_weight = axis_terms(ext_primal, ext_adjoint, along, padded_axes)
        balance = balance + part_balance
        weight = weight + part_weight
    indicator = jnp.abs(jnp.sum(weight * balance, axis=0))
    rows_rad, rows_azi, rows_ax = indicator.shape
    per_rad = rows_rad // BLK
    per_azi = rows_azi // BLK
    per_ax = rows_ax // BLK
    block_mean = indicator.reshape(per_rad, BLK, per_azi, BLK, per_ax, BLK).mean(axis=(1, 3, 5))
    all_means = lax.all_gather(block_mean.reshape(-1), ("rad", "azi", "ax"), axis=0, tiled=True)
    size_rad = lax.axis_size("rad")
    size_azi = lax.axis_size("azi")
    size_ax = lax.axis_size("ax")
    blocks_azi = per_azi * size_azi
    blocks_ax = per_ax * size_ax
    block_rad = neighbor_list // (blocks_azi * blocks_ax)
    block_azi = neighbor_list // blocks_ax % blocks_azi
    block_ax = neighbor_list % blocks_ax
    owner_dev = (
        block_rad // per_rad * size_azi + block_azi // per_azi
    ) * size_ax + block_ax // per_ax
    local_pos = (block_rad % per_rad * per_azi + block_azi % per_azi) * per_ax + block_ax % per_ax
    position = owner_dev * (per_rad * per_azi * per_ax) + local_pos
    beside_all = jnp.mean(jnp.take(all_means, position), axis=-1)
    smooth = 0.5 * block_mean + 0.5 * beside_all
    own_index = (
        lax.axis_index("rad") * size_azi + lax.axis_index("azi")
    ) * size_ax + lax.axis_index("ax")
    moved = (owner_map != own_index).astype(jnp.float32)
    block_cost = (
        smooth * (1.0 + 7.0 * refine_flag.astype(jnp.float32))
        + 0.25 * migrate_weight.astype(jnp.float32) * moved
    )
    devices = size_rad * size_azi * size_ax
    owner_flat = owner_map.reshape(-1)
    one_hot = (owner_flat[:, None] == jnp.arange(devices, dtype=jnp.int32)[None, :]).astype(
        jnp.float32
    )
    partial_load = jnp.sum(one_hot * block_cost.reshape(-1)[:, None], axis=0)
    mine = lax.psum_scatter(partial_load, ("rad", "azi", "ax"), scatter_dimension=0, tiled=True)
    owner_load = (mine / (per_rad * per_azi * per_ax)).reshape(1, 1, 1)
    return (indicator, block_cost, owner_load)


def solution(mesh):
    return jax.shard_map(
        on_device,
        mesh=mesh,
        in_specs=(
            P(None, "rad", "azi", "ax"),
            P(None, "rad", "azi", "ax"),
            P("rad", "azi", "ax"),
            P("rad", "azi", "ax"),
            P("rad", "azi", "ax"),
            P("rad", "azi", "ax", None),
        ),
        out_specs=(P("rad", "azi", "ax"), P("rad", "azi", "ax"), P("rad", "azi", "ax")),
        check_vma=False,
    )
```

profile of v0, /device:TPU:1, one launch (start us, length us, event | category | flops | bytes accessed | tf_op | source)
XLA Modules:
  0.0 265.6 jit_solution(4792332652920569260)
XLA Ops:
  0.6 1.2 fusion.52
  1.9 2.7 %collective-permute-start.6 = (f32[5,16,2,128]{3,1,2,0:T(8,128)S(1)}, f32[5,16,2,128]{3,1,2,0:T(8,128)S(1)}, u32[]{:S(2)}, u32[]{:S(2)}) collective-permute-start(f32[5,16,2,128]{3,1,2,0:T(8,128)S(1)} %copy.199), channel_id=1, source_target_pairs={{0,4},{4,8},{8,12},{12,16},{16,20},{20,24},{24,28},{28,0},{1,5},{5... | collective-permute-start | bytes 245768 | tf_op jit(solution)/shard_map/ppermute | solution.py:16
  4.6 0.6 collective-permute-start.7
  5.2 1.1 fusion.51
  6.4 2.9 %collective-permute-start.1 = (f32[5,16,2,128]{3,1,2,0:T(8,128)S(1)}, f32[5,16,2,128]{3,1,2,0:T(8,128)}, u32[]{:S(2)}, u32[]{:S(2)}) collective-permute-start(f32[5,16,2,128]{3,1,2,0:T(8,128)S(1)} %copy.184), channel_id=1, source_target_pairs={{4,0},{8,4},{12,8},{16,12},{20,16},{24,20},{28,24},{0,28},{5,1},{9... | collective-permute-start | bytes 245768 | tf_op jit(solution)/shard_map/ppermute | solution.py:19
  9.3 0.6 copy.183
  9.9 1.2 constant_dynamic-update-slice_fusion.1
  11.2 0.1 copy.177
  11.6 0.1 copy-done.1
  11.8 1.8 collective-permute-start.8
  13.6 1.3 collective-permute-start.9
  14.9 0.8 constant_dynamic-update-slice_fusion.2
  15.7 0.3 fusion.5
  16.1 0.1 add_dynamic-update-slice_fusion.2
  16.3 0.9 copy.155
  17.2 1.6 constant_dynamic-update-slice_fusion
  18.8 0.8 pad_maximum_fusion.21
  19.6 4.8 %collective-permute-start.2 = (f32[5,2,36,128]{3,2,1,0:T(8,128)}, f32[5,2,36,128]{3,2,1,0:T(8,128)}, u32[]{:S(2)}, u32[]{:S(2)}) collective-permute-start(f32[5,2,36,128]{3,2,1,0:T(8,128)} %get-tuple-element.34), channel_id=1, source_target_pairs={{0,32},{32,64},{64,96},{96,128},{128,160},{160,192},{192,224},{1,3... | collective-permute-start | bytes 552968 | tf_op jit(solution)/shard_map/ppermute | solution.py:16
  24.5 1.3 collective-permute-start.3
  25.8 1.7 fusion.50
  27.5 0.3 maximum_maximum_fusion.2
  27.8 0.6 fusion.3
  28.4 0.8 slice_dynamic-update-slice_fusion.1
  29.2 0.4 copy-done.2
  29.7 1.0 add_dynamic-update-slice_fusion.1
  30.6 0.3 pad_maximum_fusion.2
  30.9 2.6 fusion.49
  33.5 3.2 %copy.171 = f32[5,20,36,2]{2,1,3,0:T(8,128)} copy(f32[5,20,36,2]{3,2,1,0:T(8,128)} %get-tuple-element.28) | data formatting | bytes 57600 | tf_op jit(solution)/shard_map/slice | solution.py:17
  36.7 3.8 %collective-permute-start.10 = (f32[5,20,36,2]{2,1,3,0:T(8,128)}, f32[5,20,36,2]{2,1,3,0:T(8,128)}, u32[]{:S(2)}, u32[]{:S(2)}) collective-permute-start(f32[5,20,36,2]{2,1,3,0:T(8,128)} %copy.171), channel_id=1, source_target_pairs={{0,1},{1,2},{2,3},{4,5},{5,6},{6,7},{8,9},{9,10},{10,11},{12,13},{... | collective-permute-start | bytes 86408 | tf_op jit(solution)/shard_map/ppermute | solution.py:16
  40.4 3.2 %copy.173 = f32[5,20,36,2]{2,1,3,0:T(8,128)} copy(f32[5,20,36,2]{3,2,1,0:T(8,128)} %get-tuple-element.29) | data formatting | bytes 57600 | tf_op jit(solution)/shard_map/slice | solution.py:19
  43.6 1.3 collective-permute-start.11
  44.9 1.7 multiply_dynamic-update-slice_fusion.5
  46.6 1.7 multiply_dynamic-update-slice_fusion.4
  48.3 1.3 pad_maximum_fusion.1
  49.6 2.6 fusion.48
  52.2 3.2 %copy.159 = f32[5,20,36,2]{2,1,3,0:T(8,128)} copy(f32[5,20,36,2]{3,2,1,0:T(8,128)} %get-tuple-element.26) | data formatting | bytes 57600 | tf_op jit(solution)/shard_map/slice | solution.py:17
  55.3 4.6 %collective-permute-start.4 = (f32[5,20,36,2]{2,1,3,0:T(8,128)}, f32[5,20,36,2]{2,1,3,0:T(8,128)}, u32[]{:S(2)}, u32[]{:S(2)}) collective-permute-start(f32[5,20,36,2]{2,1,3,0:T(8,128)} %copy.159), channel_id=1, source_target_pairs={{0,1},{1,2},{2,3},{4,5},{5,6},{6,7},{8,9},{9,10},{10,11},{12,13},{... | collective-permute-start | bytes 86408 | tf_op jit(solution)/shard_map/ppermute | solution.py:16
  60.0 3.2 %copy.161 = f32[5,20,36,2]{2,1,3,0:T(8,128)} copy(f32[5,20,36,2]{3,2,1,0:T(8,128)} %get-tuple-element.27) | data formatting | bytes 57600 | tf_op jit(solution)/shard_map/slice | solution.py:19
  63.1 1.5 collective-permute-start.5
  64.6 1.8 multiply_dynamic-update-slice_fusion.3
  66.4 3.2 %maximum_maximum_fusion.1 = (f32[5,18,36,128]{3,2,1,0:T(8,128)}, f32[5,18,36,128]{3,2,1,0:T(8,128)}) fusion(f32[5,16,2,128]{3,2,1,0:T(2,128)S(1)} %get-tuple-element.51, f32[5,16,32,128]{3,2,1,0:T(8,128)S(1)} %copy-done, f32[5,16,2,128]{3,2,1,0:T(2,128)S(1)} %copy.155, f32[5,2,36,128]{3,2,1,0:T(8,128)} %collective-permute-done.2, ...), kind=kLoop, calls=%fused_computation.11 | loop fusion | flops 2488320 | bytes 5160960 | tf_op jit(solution)/shard_map/concatenate | solution.py:20
  69.6 3.0 %copy.172 = f32[5,20,36,2]{3,2,1,0:T(8,128)} copy(f32[5,20,36,2]{2,1,3,0:T(8,128)} %collective-permute-done.10) | data formatting | bytes 57600 | tf_op jit(solution)/shard_map/ppermute | solution.py:16
  72.7 3.1 %copy.174 = f32[5,20,36,2]{3,2,1,0:T(8,128)} copy(f32[5,20,36,2]{2,1,3,0:T(8,128)} %collective-permute-done.11) | data formatting | bytes 57600 | tf_op jit(solution)/shard_map/ppermute | solution.py:19
  75.7 5.5 %maximum_maximum_fusion = (f32[5,20,36,130]{3,2,1,0:T(8,128)S(1)}, f32[5,20,36,130]{3,2,1,0:T(8,128)S(1)}) fusion(f32[5,2,36,128]{3,2,1,0:T(8,128)S(1)} %copy-done.6, f32[5,16,2,128]{3,2,1,0:T(2,128)S(1)} %copy.166, f32[5,16,32,128]{3,2,1,0:T(8,128)S(1)} %copy-done.1, f32[5,16,2,128]{3,2,1,0:T(2,128)S(1)} %copy.165, ...), kind=kLoop, calls=%fused_computation.1 | loop fusion | flops 4680000 | bytes 5644800 | tf_op jit(solution)/shard_map/concatenate | solution.py:20
  81.3 1.8 fusion.1
  83.1 0.1 multiply_dynamic-update-slice_fusion.2
  83.3 0.3 add_dynamic-update-slice_fusion
  83.6 0.1 multiply_dynamic-update-slice_fusion
  83.7 1.5 copy-done.4
  85.2 3.0 %copy.160 = f32[5,20,36,2]{3,2,1,0:T(8,128)} copy(f32[5,20,36,2]{2,1,3,0:T(8,128)} %collective-permute-done.4) | data formatting | bytes 57600 | tf_op jit(solution)/shard_map/ppermute | solution.py:16
  88.3 3.2 %copy.162 = f32[5,20,36,2]{3,2,1,0:T(8,128)} copy(f32[5,20,36,2]{2,1,3,0:T(8,128)} %collective-permute-done.5) | data formatting | bytes 57600 | tf_op jit(solution)/shard_map/ppermute | solution.py:19
  91.5 11.0 %fusion.26 = f32[16,32,128]{2,1,0:T(8,128)} fusion(f32[5,16,32,129]{3,2,1,0:T(8,128)} %copy-done.4, f32[5,16,32,128]{3,1,2,0:T(8,128)} %get-tuple-element.41, f32[5,16,32,128]{3,1,2,0:T(8,128)} %get-tuple-element.40, f32[5,17,32,128]{3,2,1,0:T(8,128)} %multiply_dynamic-update-slice_fusion.3, f32[5,20,36,2]{3,2,1,0:T(8,128)} %copy.162, ...), kind=kLoop, calls=%fused_computation.68 | loop fusion | flops 16646144 | bytes 17891584 | tf_op jit(solution)/shard_map/reduce_sum | solution.py:95
  102.5 1.4 copy.182
  103.9 0.3 abs_reduce_fusion
  104.2 0.1 reduce_sum.45
  104.4 0.1 reduce_sum.46
  104.6 0.2 dynamic-update-slice
  104.8 81.5 %all-reduce = f32[4096]{0:T(1024)S(1)} all-reduce(f32[4096]{0:T(1024)S(1)} %dynamic-update-slice), channel_id=1, replica_groups=mesh['rad'=8,'azi'=8,'ax'=4] {'rad','azi','ax'}, use_global_device_ids=true, to_apply=%add | all-reduce | flops 4096 | bytes 32768
  186.3 1.1 gather_fusion
  187.5 0.1 select_reduce_fusion.1
  187.7 0.1 select_reduce_fusion
  187.8 74.3 %all-reduce.1 = f32[256]{0:T(256)S(1)} all-reduce(f32[256]{0:T(256)S(1)} %select_reduce_fusion), channel_id=2, replica_groups=mesh['rad'=8,'azi'=8,'ax'=4] {'rad','azi','ax'}, use_global_device_ids=true, to_apply=%region_5.6.clone | all-reduce | flops 256 | bytes 2048
  262.1 1.1 copy.181
  263.2 0.6 dynamic-slice
  (59 shorter events, 1.1 us)
Async XLA Ops:
  0.6 9.3 %copy-start = (f32[5,16,32,128]{3,2,1,0:T(8,128)S(1)}, f32[5,16,32,128]{3,2,1,0:T(8,128)}, u32[]{:S(2)}) copy-start(f32[5,16,32,128]{3,2,1,0:T(8,128)} %param.7) | copy-start | bytes 3932164
  1.9 9.6 %collective-permute-start.6 = (f32[5,16,2,128]{3,1,2,0:T(8,128)S(1)}, f32[5,16,2,128]{3,1,2,0:T(8,128)S(1)}, u32[]{:S(2)}, u32[]{:S(2)}) collective-permute-start(f32[5,16,2,128]{3,1,2,0:T(8,128)S(1)} %copy.199), channel_id=1, source_target_pairs={{0,4},{4,8},{8,12},{12,16},{16,20},{20,24},{24,28},{28,0},{1,5},{5... | collective-permute-start | bytes 245768 | tf_op jit(solution)/shard_map/ppermute | solution.py:16
  4.6 6.9 %collective-permute-start.7 = (f32[5,16,2,128]{3,1,2,0:T(8,128)S(1)}, f32[5,16,2,128]{3,1,2,0:T(8,128)S(1)}, u32[]{:S(2)}, u32[]{:S(2)}) collective-permute-start(f32[5,16,2,128]{3,1,2,0:T(8,128)S(1)} %copy.198), channel_id=1, source_target_pairs={{4,0},{8,4},{12,8},{16,12},{20,16},{24,20},{28,24},{0,28},{5,1},{9... | collective-permute-start | bytes 245768 | tf_op jit(solution)/shard_map/ppermute | solution.py:19
  6.4 10.8 %collective-permute-start.1 = (f32[5,16,2,128]{3,1,2,0:T(8,128)S(1)}, f32[5,16,2,128]{3,1,2,0:T(8,128)}, u32[]{:S(2)}, u32[]{:S(2)}) collective-permute-start(f32[5,16,2,128]{3,1,2,0:T(8,128)S(1)} %copy.184), channel_id=1, source_target_pairs={{4,0},{8,4},{12,8},{16,12},{20,16},{24,20},{28,24},{0,28},{5,1},{9... | collective-permute-start | bytes 245768 | tf_op jit(solution)/shard_map/ppermute | solution.py:19
  9.3 1.9 copy-start.7
  9.3 2.1 copy-start.8
  9.9 1.8 copy-start.1
  9.9 6.3 %collective-permute-start = (f32[5,16,2,128]{3,1,2,0:T(8,128)}, f32[5,16,2,128]{3,1,2,0:T(8,128)}, u32[]{:S(2)}, u32[]{:S(2)}) collective-permute-start(f32[5,16,2,128]{3,1,2,0:T(8,128)} %copy.183), channel_id=1, source_target_pairs={{0,4},{4,8},{8,12},{12,16},{16,20},{20,24},{24,28},{28,0},{1,5},{5... | collective-permute-start | bytes 245768 | tf_op jit(solution)/shard_map/ppermute | solution.py:16
  11.8 15.7 %collective-permute-start.8 = (f32[5,2,36,128]{3,2,1,0:T(8,128)S(1)}, f32[5,2,36,128]{3,2,1,0:T(8,128)S(1)}, u32[]{:S(2)}, u32[]{:S(2)}) collective-permute-start(f32[5,2,36,128]{3,2,1,0:T(8,128)S(1)} %get-tuple-element.38), channel_id=1, source_target_pairs={{0,32},{32,64},{64,96},{96,128},{128,160},{160,192},{192,224},{1,3... | collective-permute-start | bytes 552968 | tf_op jit(solution)/shard_map/ppermute | solution.py:16
  13.6 13.9 %collective-permute-start.9 = (f32[5,2,36,128]{3,2,1,0:T(8,128)S(1)}, f32[5,2,36,128]{3,2,1,0:T(8,128)S(1)}, u32[]{:S(2)}, u32[]{:S(2)}) collective-permute-start(f32[5,2,36,128]{3,2,1,0:T(8,128)S(1)} %get-tuple-element.39), channel_id=1, source_target_pairs={{32,0},{64,32},{96,64},{128,96},{160,128},{192,160},{224,192},{33,... | collective-permute-start | bytes 552968 | tf_op jit(solution)/shard_map/ppermute | solution.py:19
  19.6 28.7 %collective-permute-start.2 = (f32[5,2,36,128]{3,2,1,0:T(8,128)}, f32[5,2,36,128]{3,2,1,0:T(8,128)}, u32[]{:S(2)}, u32[]{:S(2)}) collective-permute-start(f32[5,2,36,128]{3,2,1,0:T(8,128)} %get-tuple-element.34), channel_id=1, source_target_pairs={{0,32},{32,64},{64,96},{96,128},{128,160},{160,192},{192,224},{1,3... | collective-permute-start | bytes 552968 | tf_op jit(solution)/shard_map/ppermute | solution.py:16
  24.5 23.8 %collective-permute-start.3 = (f32[5,2,36,128]{3,2,1,0:T(8,128)}, f32[5,2,36,128]{3,2,1,0:T(8,128)}, u32[]{:S(2)}, u32[]{:S(2)}) collective-permute-start(f32[5,2,36,128]{3,2,1,0:T(8,128)} %get-tuple-element.35), channel_id=1, source_target_pairs={{32,0},{64,32},{96,64},{128,96},{160,128},{192,160},{224,192},{33,... | collective-permute-start | bytes 552968 | tf_op jit(solution)/shard_map/ppermute | solution.py:19
  27.5 3.1 %copy-start.5 = (f32[5,2,36,128]{3,2,1,0:T(8,128)}, f32[5,2,36,128]{3,2,1,0:T(8,128)S(1)}, u32[]{:S(2)}) copy-start(f32[5,2,36,128]{3,2,1,0:T(8,128)S(1)} %collective-permute-done.9) | copy-start | bytes 552964
  28.4 1.2 copy-start.2
  36.7 33.0 %collective-permute-start.10 = (f32[5,20,36,2]{2,1,3,0:T(8,128)}, f32[5,20,36,2]{2,1,3,0:T(8,128)}, u32[]{:S(2)}, u32[]{:S(2)}) collective-permute-start(f32[5,20,36,2]{2,1,3,0:T(8,128)} %copy.171), channel_id=1, source_target_pairs={{0,1},{1,2},{2,3},{4,5},{5,6},{6,7},{8,9},{9,10},{10,11},{12,13},{... | collective-permute-start | bytes 86408 | tf_op jit(solution)/shard_map/ppermute | solution.py:16
  43.6 29.1 %collective-permute-start.11 = (f32[5,20,36,2]{2,1,3,0:T(8,128)}, f32[5,20,36,2]{2,1,3,0:T(8,128)}, u32[]{:S(2)}, u32[]{:S(2)}) collective-permute-start(f32[5,20,36,2]{2,1,3,0:T(8,128)} %copy.173), channel_id=1, source_target_pairs={{1,0},{2,1},{3,2},{5,4},{6,5},{7,6},{9,8},{10,9},{11,10},{13,12},{... | collective-permute-start | bytes 86408 | tf_op jit(solution)/shard_map/ppermute | solution.py:19
  55.3 29.9 %collective-permute-start.4 = (f32[5,20,36,2]{2,1,3,0:T(8,128)}, f32[5,20,36,2]{2,1,3,0:T(8,128)}, u32[]{:S(2)}, u32[]{:S(2)}) collective-permute-start(f32[5,20,36,2]{2,1,3,0:T(8,128)} %copy.159), channel_id=1, source_target_pairs={{0,1},{1,2},{2,3},{4,5},{5,6},{6,7},{8,9},{9,10},{10,11},{12,13},{... | collective-permute-start | bytes 86408 | tf_op jit(solution)/shard_map/ppermute | solution.py:16
  63.1 25.1 %collective-permute-start.5 = (f32[5,20,36,2]{2,1,3,0:T(8,128)}, f32[5,20,36,2]{2,1,3,0:T(8,128)}, u32[]{:S(2)}, u32[]{:S(2)}) collective-permute-start(f32[5,20,36,2]{2,1,3,0:T(8,128)} %copy.161), channel_id=1, source_target_pairs={{1,0},{2,1},{3,2},{5,4},{6,5},{7,6},{9,8},{10,9},{11,10},{13,12},{... | collective-permute-start | bytes 86408 | tf_op jit(solution)/shard_map/ppermute | solution.py:19
  72.7 3.1 %copy-start.6 = (f32[5,2,36,128]{3,2,1,0:T(8,128)S(1)}, f32[5,2,36,128]{3,2,1,0:T(8,128)}, u32[]{:S(2)}) copy-start(f32[5,2,36,128]{3,2,1,0:T(8,128)} %copy-done.5) | copy-start | bytes 552964
  83.7 1.5 copy-start.4
  88.2 3.2 %copy-start.3 = (f32[5,18,36,128]{3,2,1,0:T(8,128)S(1)}, f32[5,18,36,128]{3,2,1,0:T(8,128)}, u32[]{:S(2)}) copy-start(f32[5,18,36,128]{3,2,1,0:T(8,128)} %get-tuple-element.32) | copy-start | bytes 4976644
  186.3 1.4 copy-start.9
  186.3 1.4 copy-start.10
  187.6 76.8 %copy-start.11 = (f32[1,2,8]{2,1,0:T(2,128)}, f32[1,2,8]{2,1,0:T(2,128)S(1)}, u32[]{:S(2)}) copy-start(f32[1,2,8]{2,1,0:T(2,128)S(1)} %fusion.47) | copy-start | bytes 196
where the time goes:
time: 267 us; the launch traced here: 266 us
  blocking collectives  156 us (58%)
  local copies, waits for them, and re-layouts  47.5 us (18%)
  other arithmetic  32.9 us (12%)
  starting transfers between devices  26.6 us (10%)
  between operations  2.79 us (1%)
    unnamed x2, blocking collectives  156 us
    ppermute x6, starting transfers between devices, with_halo(): lax.ppermute(lax.slice_in_dim(block, block.shape[dim] - width, None, axis...  17.8 us
    slice x6, local copies, waits for them, and re-layouts, with_halo(): lax.slice_in_dim(block, block.shape[dim] - width, None, axis=dim)  13.8 us
    reduce_sum x1, other arithmetic, on_device(): indicator = jnp.abs(jnp.sum(weight * balance, axis=0))  11 us
    concatenate x5, other arithmetic, with_halo(): block = jnp.concatenate([low, block, high], axis=dim)  10.6 us
    ppermute x6, starting transfers between devices, with_halo(): lax.ppermute(lax.slice_in_dim(block, 0, width, axis=dim), axis, backward)  8.84 us
    unnamed x39, local copies, waits for them, and re-layouts  8.24 us
    ppermute x4, local copies, waits for them, and re-layouts, with_halo(): lax.ppermute(lax.slice_in_dim(block, block.shape[dim] - width, None, axis...  7.04 us
  transfers between devices with their start and end apart: 12, of which 0 were waited for; matrix products, arithmetic and copies ran while one was open for 22% of the time, Pallas kernels for 0%

commit v1 on v0

v1 whole, which is shorter than its diff:
```python
import functools
import jax
import jax.numpy as jnp
from jax import lax
from jax.experimental import pallas as pl
from jax.experimental.pallas import tpu as pltpu
from jax.sharding import PartitionSpec as P

BLK = 16
AXES = ("rad", "azi", "ax")
MESH = pl.DeviceIdType.MESH


def gather_kernel(sizes, x_ref, o_ref, lsem, ssem, rsem):
    n_r, n_a, n_x = sizes
    r = lax.axis_index("rad")
    a = lax.axis_index("azi")
    x = lax.axis_index("ax")

    def at(rr, aa, xx):
        return (rr, aa, xx)

    stages = [
        (n_x, lambda k: at(r, a, lax.rem(x + k, n_x)), lambda k: at(r, a, lax.rem(x + n_x - k, n_x))),
        (n_a, lambda k: at(r, lax.rem(a + k, n_a), x), lambda k: at(r, lax.rem(a + n_a - k, n_a), x)),
        (n_r, lambda k: at(lax.rem(r + k, n_r), a, x), lambda k: at(lax.rem(r + n_r - k, n_r), a, x)),
    ]
    barrier = pltpu.get_barrier_semaphore()
    count = 0
    for n, to, _ in stages:
        for k in range(1, n):
            pl.semaphore_signal(barrier, 1, device_id=to(k), device_id_type=MESH)
            count += 1
    pl.semaphore_wait(barrier, count)

    def region(stage, dev):
        rr, aa, xx = dev
        if stage == 0:
            return o_ref.at[pl.ds(rr, 1), pl.ds(aa, 1), pl.ds(xx, 1)]
        if stage == 1:
            return o_ref.at[pl.ds(rr, 1), pl.ds(aa, 1)]
        return o_ref.at[pl.ds(rr, 1)]

    local = pltpu.make_async_copy(x_ref, region(0, (r, a, x)), lsem)
    local.start()
    sends = []
    slot = 0
    for stage, (n, to, frm) in enumerate(stages):
        src = x_ref if stage == 0 else region(stage, (r, a, x))
        first = slot
        for k in range(1, n):
            copy = pltpu.make_async_remote_copy(
                src_ref=src,
                dst_ref=region(stage, (r, a, x)),
                send_sem=ssem.at[slot],
                recv_sem=rsem.at[slot],
                device_id=to(k),
                device_id_type=MESH,
            )
            copy.start()
            sends.append(copy)
            slot += 1
        slot = first
        for k in range(1, n):
            incoming = pltpu.make_async_remote_copy(
                src_ref=src,
                dst_ref=region(stage, frm(k)),
                send_sem=ssem.at[slot],
                recv_sem=rsem.at[slot],
                device_id=frm(k),
                device_id_type=MESH,
            )
            incoming.wait_recv()
            slot += 1
        if stage == 0:
            local.wait()
    for copy in sends:
        copy.wait_send()


def gather_all(values, cid):
    n_r, n_a, n_x = (lax.axis_size(ax) for ax in AXES)
    width = values.shape[0]
    links = (n_r - 1) + (n_a - 1) + (n_x - 1)
    out = pl.pallas_call(
        functools.partial(gather_kernel, (n_r, n_a, n_x)),
        out_shape=jax.ShapeDtypeStruct((n_r, n_a, n_x, width), jnp.float32),
        in_specs=[pl.BlockSpec(memory_space=pltpu.VMEM)],
        out_specs=pl.BlockSpec(memory_space=pltpu.VMEM),
        scratch_shapes=[
            pltpu.SemaphoreType.DMA(()),
            pltpu.SemaphoreType.DMA((links,)),
            pltpu.SemaphoreType.DMA((links,)),
        ],
        compiler_params=pltpu.CompilerParams(collective_id=cid, has_side_effects=True),
    )(values.reshape(1, 1, 1, width))
    return out.reshape(-1)


def halo_pair(parts, axis, dim, periodic):
    count = lax.axis_size(axis)
    forward = [(i, i + 1) for i in range(count - 1)]
    if periodic:
        forward.append((count - 1, 0))
    backward = [(target, source) for source, target in forward]
    tails = tuple(lax.slice_in_dim(p, p.shape[dim] - 2, None, axis=dim) for p in parts)
    heads = tuple(lax.slice_in_dim(p, 0, 2, axis=dim) for p in parts)
    low = lax.ppermute(tails, axis, forward)
    high = lax.ppermute(heads, axis, backward)
    return tuple(jnp.concatenate([lo, p, hi], axis=dim) for lo, p, hi in zip(low, parts, high))


def euler_flux(face_state, along):
    density = face_state[0]
    momenta = face_state[1:4]
    energy = face_state[4]
    velocity = momenta[along] / density
    kinetic = (
        0.5
        * (momenta[0] * momenta[0] + momenta[1] * momenta[1] + momenta[2] * momenta[2])
        / density
    )
    pressure = 0.4 * (energy - kinetic)
    columns = [
        momenta[along],
        momenta[0] * velocity,
        momenta[1] * velocity,
        momenta[2] * velocity,
        (energy + pressure) * velocity,
    ]
    columns[1 + along] = columns[1 + along] + pressure
    return jnp.stack(columns)


def axis_terms(ext_p, ext_a, dim):
    length = ext_p.shape[dim] - 4
    win = lambda e, s, c: lax.slice_in_dim(e, s, s + c, axis=dim)
    high = (7.0 * win(ext_p, 1, length + 1) - win(ext_p, 0, length + 1)) / 12.0
    low = (7.0 * win(ext_p, 2, length + 1) - win(ext_p, 3, length + 1)) / 12.0
    fluxes = euler_flux(high + low, dim - 1)
    balance = win(fluxes, 1, length) - win(fluxes, 0, length)
    fourth = (
        win(ext_a, 0, length)
        - 4.0 * win(ext_a, 1, length)
        + 6.0 * win(ext_a, 2, length)
        - 4.0 * win(ext_a, 3, length)
        + win(ext_a, 4, length)
    ) / 12.0
    return balance, fourth


def on_device(primal, adjoint, refine_flag, owner_map, migrate_weight, neighbor_list):
    ext = {
        1: halo_pair((primal, adjoint), "rad", 1, False),
        2: halo_pair((primal, adjoint), "azi", 2, True),
        3: halo_pair((primal, adjoint), "ax", 3, False),
    }
    balance = None
    weight = None
    for along in (1, 2, 3):
        part_balance, part_weight = axis_terms(ext[along][0], ext[along][1], along)
        balance = part_balance if balance is None else balance + part_balance
        weight = part_weight if weight is None else weight + part_weight
    indicator = jnp.abs(jnp.sum(weight * balance, axis=0))
    rows_rad, rows_azi, rows_ax = indicator.shape
    per_rad = rows_rad // BLK
    per_azi = rows_azi // BLK
    per_ax = rows_ax // BLK
    block_mean = indicator.reshape(per_rad, BLK, per_azi, BLK, per_ax, BLK).mean(axis=(1, 3, 5))
    all_means = gather_all(block_mean.reshape(-1), 0)
    size_rad = lax.axis_size("rad")
    size_azi = lax.axis_size("azi")
    size_ax = lax.axis_size("ax")
    blocks_azi = per_azi * size_azi
    blocks_ax = per_ax * size_ax
    block_rad = neighbor_list // (blocks_azi * blocks_ax)
    block_azi = neighbor_list // blocks_ax % blocks_azi
    block_ax = neighbor_list % blocks_ax
    owner_dev = (
        block_rad // per_rad * size_azi + block_azi // per_azi
    ) * size_ax + block_ax // per_ax
    local_pos = (block_rad % per_rad * per_azi + block_azi % per_azi) * per_ax + block_ax % per_ax
    position = owner_dev * (per_rad * per_azi * per_ax) + local_pos
    beside_all = jnp.mean(jnp.take(all_means, position), axis=-1)
    smooth = 0.5 * block_mean + 0.5 * beside_all
    own_index = (
        lax.axis_index("rad") * size_azi + lax.axis_index("azi")
    ) * size_ax + lax.axis_index("ax")
    moved = (owner_map != own_index).astype(jnp.float32)
    block_cost = (
        smooth * (1.0 + 7.0 * refine_flag.astype(jnp.float32))
        + 0.25 * migrate_weight.astype(jnp.float32) * moved
    )
    width = block_cost.size
    payload = jnp.concatenate([block_cost.reshape(-1), owner_map.reshape(-1).astype(jnp.float32)])
    gathered = gather_all(payload, 1).reshape(-1, 2 * width)
    cost_all = gathered[:, :width]
    owner_all = gathered[:, width:]
    total = jnp.sum(jnp.where(owner_all == own_index.astype(jnp.float32), cost_all, 0.0))
    owner_load = (total / (per_rad * per_azi * per_ax)).reshape(1, 1, 1)
    return (indicator, block_cost, owner_load)


def solution(mesh):
    return jax.shard_map(
        on_device,
        mesh=mesh,
        in_specs=(
            P(None, "rad", "azi", "ax"),
            P(None, "rad", "azi", "ax"),
            P("rad", "azi", "ax"),
            P("rad", "azi", "ax"),
            P("rad", "azi", "ax"),
            P("rad", "azi", "ax", None),
        ),
        out_specs=(P("rad", "azi", "ax"), P("rad", "azi", "ax"), P("rad", "azi", "ax")),
        check_vma=False,
    )
```

time: 267 us -> 130 us (0.49)
  blocking collectives: 156 us -> 0 us
  Pallas kernels: 0 us -> 44.2 us
  other arithmetic: 32.9 us -> 17.5 us
  local copies, waits for them, and re-layouts: 47.5 us -> 37.3 us
    unnamed x2 -> x0, blocking collectives: 156 us -> none
    pallas_call x0 -> x2, Pallas kernels: none -> 44.2 us  [gather_all(): pl.pallas_call(functools.partial(gather_kernel, (n_r, n_a, n_x)), out_sha...]
    slice x9 -> x6, local copies, waits for them, and re-layouts: 21.8 us -> 9.13 us  [halo_pair(): lax.slice_in_dim(p, p.shape[dim] - 2, None, axis=dim)]
    concatenate x5 -> x0, other arithmetic: 10.6 us -> none  [with_halo(): block = jnp.concatenate([low, block, high], axis=dim)]
    reduce_sum x1, other arithmetic: 11 us -> 2.96 us  [on_device(): indicator = jnp.abs(jnp.sum(weight * balance, axis=0))]
    unnamed x39 -> x46, local copies, waits for them, and re-layouts: 8.24 us -> 13.5 us
    ppermute x7 -> x4, local copies, waits for them, and re-layouts: 13.3 us -> 8.25 us  [the longest x2 4.13 us: halo_pair(): low = lax.ppermute(tails, axis, forward)]
    add x3, other arithmetic: 2.63 us -> 6.59 us  [axis_terms(): fluxes = euler_flux(high + low, dim - 1)]
  transfers between devices with their start and end apart: 12 -> 12, of which waited for: 0 -> 0; matrix products, arithmetic and copies ran while one was open for 22% -> 30% of each run, Pallas kernels for 0% -> 0%
where the time goes in v1:
time: 130 us
  Pallas kernels  44.2 us (34%)
  local copies, waits for them, and re-layouts  37.3 us (29%)
  starting transfers between devices  27.7 us (21%)
  other arithmetic  17.5 us (13%)
  between operations  2.86 us (2%)
    pallas_call x2, Pallas kernels, gather_all(): pl.pallas_call(functools.partial(gather_kernel, (n_r, n_a, n_x)), out_sha...  44.2 us
    ppermute x6, starting transfers between devices, halo_pair(): low = lax.ppermute(tails, axis, forward)  20.5 us
    unnamed x46, local copies, waits for them, and re-layouts  13.5 us
    slice x6, local copies, waits for them, and re-layouts, halo_pair(): lax.slice_in_dim(p, p.shape[dim] - 2, None, axis=dim)  9.13 us
    ppermute x6, starting transfers between devices, halo_pair(): high = lax.ppermute(heads, axis, backward)  7.26 us
    add x3, other arithmetic, axis_terms(): fluxes = euler_flux(high + low, dim - 1)  6.59 us
    ppermute x2, local copies, waits for them, and re-layouts, halo_pair(): low = lax.ppermute(tails, axis, forward)  4.13 us
    ppermute x2, local copies, waits for them, and re-layouts, halo_pair(): high = lax.ppermute(heads, axis, backward)  4.13 us
  transfers between devices with their start and end apart: 12, of which 0 were waited for; matrix products, arithmetic and copies ran while one was open for 30% of the time, Pallas kernels for 0%

profile of v1, /device:TPU:1, one launch (start us, length us, event | category | flops | bytes accessed | tf_op | source)
XLA Modules:
  0.0 129.6 jit_solution(14149112517564747129)
XLA Ops:
  0.6 1.7 %fusion.59 = (f32[5,2,32,128]{3,2,1,0:T(8,128)}, f32[5,2,32,128]{3,2,1,0:T(8,128)}) fusion(f32[5,16,32,128]{3,2,1,0:T(8,128)} %param.6), kind=kLoop, calls=%fused_computation.154 | loop fusion | bytes 655360 | tf_op jit(solution)/shard_map/slice | solution.py:106
  2.4 5.0 %collective-permute-start.6 = (f32[5,2,32,128]{3,2,1,0:T(8,128)}, f32[5,2,32,128]{3,2,1,0:T(8,128)}, u32[]{:S(2)}, u32[]{:S(2)}) collective-permute-start(f32[5,2,32,128]{3,2,1,0:T(8,128)} %get-tuple-element.28), channel_id=1, source_target_pairs={{0,32},{32,64},{64,96},{96,128},{128,160},{160,192},{192,224},{1,3... | collective-permute-start | bytes 491528 | tf_op jit(solution)/shard_map/ppermute | solution.py:108
  7.4 1.3 collective-permute-start.7
  8.7 1.8 %fusion.60 = (f32[5,16,2,128]{3,2,1,0:T(2,128)}, f32[5,16,2,128]{3,2,1,0:T(2,128)}) fusion(f32[5,16,32,128]{3,2,1,0:T(8,128)} %param.6), kind=kLoop, calls=%fused_computation.155 | loop fusion | bytes 327680 | tf_op jit(solution)/shard_map/slice | solution.py:106
  10.5 1.0 collective-permute-start.9
  11.5 3.3 %fusion.61 = (f32[5,16,32,2]{3,2,1,0:T(8,128)}, f32[5,16,32,2]{3,2,1,0:T(8,128)S(1)}) fusion(f32[5,16,32,128]{3,2,1,0:T(8,128)} %param.6), kind=kLoop, calls=%fused_computation.156 | loop fusion | bytes 81920 | tf_op jit(solution)/shard_map/slice | solution.py:106
  14.8 1.9 %copy.43 = f32[5,16,32,2]{2,1,3,0:T(8,128)S(1)} copy(f32[5,16,32,2]{3,2,1,0:T(8,128)} %get-tuple-element.32) | data formatting | bytes 40960
  16.7 3.1 %collective-permute-start.10 = (f32[5,16,32,2]{2,1,3,0:T(8,128)S(1)}, f32[5,16,32,2]{2,1,3,0:T(8,128)S(1)}, u32[]{:S(2)}, u32[]{:S(2)}) collective-permute-start(f32[5,16,32,2]{2,1,3,0:T(8,128)S(1)} %copy.43), channel_id=1, source_target_pairs={{0,1},{1,2},{2,3},{4,5},{5,6},{6,7},{8,9},{9,10},{10,11},{12,13},{... | collective-permute-start | bytes 61448 | tf_op jit(solution)/shard_map/ppermute | solution.py:108
  19.9 0.5 copy.44
  20.4 1.3 collective-permute-start.11
  21.7 0.7 fusion.57
  22.4 1.6 %fusion.58 = (f32[5,16,32,2]{3,2,1,0:T(8,128)}, f32[5,16,32,2]{3,2,1,0:T(8,128)S(1)}) fusion(f32[5,16,32,128]{3,2,1,0:T(8,128)S(1)} %copy-done.2), kind=kLoop, calls=%fused_computation.153 | loop fusion | bytes 81920 | tf_op jit(solution)/shard_map/slice | solution.py:106
  24.0 0.1 copy.37
  24.1 0.1 reshape.87
  24.2 0.6 pad_clamp_fusion
  24.8 2.5 %copy.41 = f32[5,16,32,2]{2,1,3,0:T(8,128)} copy(f32[5,16,32,2]{3,2,1,0:T(8,128)} %get-tuple-element.23) | data formatting | bytes 40960
  27.3 1.2 copy.42
  28.5 0.6 convert_element_type.19
  29.1 4.6 %collective-permute-start.4 = (f32[5,16,32,2]{2,1,3,0:T(8,128)}, f32[5,16,32,2]{2,1,3,0:T(8,128)}, u32[]{:S(2)}, u32[]{:S(2)}) collective-permute-start(f32[5,16,32,2]{2,1,3,0:T(8,128)} %copy.41), channel_id=1, source_target_pairs={{0,1},{1,2},{2,3},{4,5},{5,6},{6,7},{8,9},{9,10},{10,11},{12,13},{... | collective-permute-start | bytes 61448 | tf_op jit(solution)/shard_map/ppermute | solution.py:108
  33.7 1.6 %copy.34 = f32[5,16,32,2]{3,2,1,0:T(8,128)} copy(f32[5,16,32,2]{2,1,3,0:T(8,128)S(1)} %collective-permute-done.10) | data formatting | bytes 40960 | tf_op jit(solution)/shard_map/ppermute | solution.py:108
  35.3 1.3 collective-permute-start.5
  36.6 1.6 %copy.36 = f32[5,16,32,2]{3,2,1,0:T(8,128)} copy(f32[5,16,32,2]{2,1,3,0:T(8,128)S(1)} %collective-permute-done.11) | data formatting | bytes 40960 | tf_op jit(solution)/shard_map/ppermute | solution.py:109
  38.2 4.6 %fusion.2 = f32[5,16,32,129]{3,2,1,0:T(8,128)S(1)} fusion(f32[5,16,32,2]{3,2,1,0:T(8,128)} %copy.36, f32[5,16,32,128]{3,2,1,0:T(8,128)S(1)} %copy-done, f32[5,16,32,2]{3,2,1,0:T(8,128)} %copy.34), kind=kLoop, calls=%fused_computation.4 | loop fusion | flops 3302400 | bytes 2672640 | tf_op jit(solution)/shard_map/add | solution.py:140
  42.8 0.1 multiply_dynamic-update-slice_fusion.2
  43.0 0.1 multiply_dynamic-update-slice_fusion.1
  43.0 1.3 copy-done.1
  44.3 1.2 add_dynamic-update-slice_fusion
  45.5 1.5 %copy-done.5 = f32[5,16,32,129]{3,2,1,0:T(8,128)} copy-done((f32[5,16,32,129]{3,2,1,0:T(8,128)}, f32[5,16,32,129]{3,2,1,0:T(8,128)S(1)}, u32[]{:S(2)}) %copy-start.5) | copy-done | bytes 1320984
  47.0 2.0 %collective-permute-start.8 = (f32[5,16,2,128]{3,2,1,0:T(2,128)}, f32[5,16,2,128]{3,2,1,0:T(2,128)}, u32[]{:S(2)}, u32[]{:S(2)}) collective-permute-start(f32[5,16,2,128]{3,2,1,0:T(2,128)} %get-tuple-element.30), channel_id=1, source_target_pairs={{0,4},{4,8},{8,12},{12,16},{16,20},{20,24},{24,28},{28,0},{1,5},{5... | collective-permute-start | bytes 245768 | tf_op jit(solution)/shard_map/ppermute | solution.py:108
  49.0 2.5 %copy.30 = f32[5,16,32,2]{3,2,1,0:T(8,128)} copy(f32[5,16,32,2]{2,1,3,0:T(8,128)} %collective-permute-done.4) | data formatting | bytes 40960 | tf_op jit(solution)/shard_map/ppermute | solution.py:108
  51.6 4.9 %collective-permute-start = (f32[5,2,32,128]{3,2,1,0:T(8,128)S(1)}, f32[5,2,32,128]{3,2,1,0:T(8,128)}, u32[]{:S(2)}, u32[]{:S(2)}) collective-permute-start(f32[5,2,32,128]{3,2,1,0:T(8,128)S(1)} %get-tuple-element.19), channel_id=1, source_target_pairs={{0,32},{32,64},{64,96},{96,128},{128,160},{160,192},{192,224},{1,3... | collective-permute-start | bytes 491528 | tf_op jit(solution)/shard_map/ppermute | solution.py:108
  56.5 2.5 %copy.32 = f32[5,16,32,2]{3,2,1,0:T(8,128)} copy(f32[5,16,32,2]{2,1,3,0:T(8,128)} %collective-permute-done.5) | data formatting | bytes 40960 | tf_op jit(solution)/shard_map/ppermute | solution.py:109
  59.0 2.1 %multiply_dynamic-update-slice_fusion = f32[5,16,32,129]{3,2,1,0:T(8,128)} fusion(f32[5,16,32,129]{3,2,1,0:T(8,128)} %copy-done.5, f32[1,16,32,129]{3,2,1,0:T(8,128)S(1)} %get-tuple-element.15, f32[1,16,32,129]{3,2,1,0:T(8,128)} %get-tuple-element.13, f32[5,16,32,129]{3,2,1,0:T(8,128)} %copy-done.1), kind=kLoop, calls=%fused_computation.62 | loop fusion | flops 132096 | bytes 1837056 | tf_op jit(solution)/shard_map/stack | solution.py:132
  61.1 1.5 %collective-permute-start.1 = (f32[5,2,32,128]{3,2,1,0:T(8,128)S(1)}, f32[5,2,32,128]{3,2,1,0:T(8,128)S(1)}, u32[]{:S(2)}, u32[]{:S(2)}) collective-permute-start(f32[5,2,32,128]{3,2,1,0:T(8,128)S(1)} %get-tuple-element.20), channel_id=1, source_target_pairs={{32,0},{64,32},{96,64},{128,96},{160,128},{192,160},{224,192},{33,... | collective-permute-start | bytes 491528 | tf_op jit(solution)/shard_map/ppermute | solution.py:109
  62.6 0.9 constant_dynamic-update-slice_fusion.7
  63.5 0.4 constant_dynamic-update-slice_fusion.6
  64.0 0.4 copy-done.7
  64.4 1.0 collective-permute-start.3
  65.4 0.9 constant_dynamic-update-slice_fusion.8
  66.3 0.4 fusion.8
  66.7 0.2 add_dynamic-update-slice_fusion.2
  67.0 0.8 collective-permute-start.2
  67.7 0.9 constant_dynamic-update-slice_fusion.10
  68.7 1.7 %fusion.5 = f32[5,16,33,128]{3,2,1,0:T(8,128)S(1)} fusion(f32[5,16,34,128]{3,2,1,0:T(8,128)S(1)} %constant_dynamic-update-slice_fusion.10, f32[5,16,32,128]{3,2,1,0:T(8,128)S(1)} %copy-done, f32[5,16,2,128]{3,2,1,0:T(2,128)} %collective-permute-done.8), kind=kLoop, calls=%fused_computation.15 | loop fusion | flops 2703360 | bytes 5447680 | tf_op jit(solution)/shard_map/add | solution.py:140
  70.4 0.1 add_dynamic-update-slice_fusion.1
  70.8 0.9 constant_dynamic-update-slice_fusion.1
  71.7 0.4 constant_dynamic-update-slice_fusion
  72.2 0.8 copy-done.3
  73.0 0.4 copy-done.4
  73.4 0.8 copy-done.6
  74.2 3.0 %fusion.32 = f32[16,32,128]{2,1,0:T(8,128)S(1)} fusion(f32[5,16,32,129]{3,2,1,0:T(8,128)S(1)} %copy-done.6, f32[5,16,33,128]{3,2,1,0:T(8,128)S(1)} %multiply_dynamic-update-slice_fusion.3, f32[5,17,32,128]{3,2,1,0:T(8,128)S(1)} %multiply_dynamic-update-slice_fusion.6, f32[5,16,32,2]{3,2,1,0:T(8,128)S(1)} %copy-done.4, f32[5,16,32,128]{3,2,1,0:T(8,128)S(1)} %copy-done.2, ...), kind=kLoop, calls=%fused_computation.61 | loop fusion | flops 11403264 | bytes 17424384 | tf_op jit(solution)/shard_map/reduce_sum | solution.py:164
  77.2 0.7 fusion.55
  77.9 0.1 reduce_sum.45
  78.0 0.1 reduce_sum.46
  78.1 0.6 div.145.x_ref
  78.7 26.3 %shard_map.85 = f32[8,8,4,16]{3,2,1,0:T(4,128)} custom-call(f32[1,1,1,16]{3,2,1,0:T(1,128)} %div.145.x_ref), custom_call_target="tpu_custom_call" | custom-call | tf_op jit(solution)/shard_map/pallas_call | solution.py:85
  105.0 1.0 reshape.81
  106.1 1.1 gather_fusion
  107.3 0.1 reshape.86
  107.4 0.1 select_reduce_fusion
  107.5 0.1 reshape.82
  107.6 0.6 maximum_bitcast_fusion.x_ref
  108.2 17.9 %shard_map.86 = f32[8,8,4,32]{3,2,1,0:T(4,128)} custom-call(f32[1,1,1,32]{3,2,1,0:T(1,128)} %maximum_bitcast_fusion.x_ref), custom_call_target="tpu_custom_call" | custom-call | tf_op jit(solution)/shard_map/pallas_call | solution.py:85
  126.2 1.7 %fusion.33 = f32[]{:T(128)} fusion(f32[256,32]{1,0:T(8,128)} %bitcast.10, f32[]{:T(128)S(6)} %convert_element_type.20), kind=kLoop, calls=%fused_computation.84 | loop fusion | flops 12287 | bytes 32776 | tf_op jit(solution)/shard_map/reduce_sum | solution.py:199
  (58 shorter events, 0.6 us)
Async XLA Ops:
  2.4 58.7 %collective-permute-start.6 = (f32[5,2,32,128]{3,2,1,0:T(8,128)}, f32[5,2,32,128]{3,2,1,0:T(8,128)}, u32[]{:S(2)}, u32[]{:S(2)}) collective-permute-start(f32[5,2,32,128]{3,2,1,0:T(8,128)} %get-tuple-element.28), channel_id=1, source_target_pairs={{0,32},{32,64},{64,96},{96,128},{128,160},{160,192},{192,224},{1,3... | collective-permute-start | bytes 491528 | tf_op jit(solution)/shard_map/ppermute | solution.py:108
  7.4 56.5 %collective-permute-start.7 = (f32[5,2,32,128]{3,2,1,0:T(8,128)}, f32[5,2,32,128]{3,2,1,0:T(8,128)}, u32[]{:S(2)}, u32[]{:S(2)}) collective-permute-start(f32[5,2,32,128]{3,2,1,0:T(8,128)} %get-tuple-element.29), channel_id=1, source_target_pairs={{32,0},{64,32},{96,64},{128,96},{160,128},{192,160},{224,192},{33,... | collective-permute-start | bytes 491528 | tf_op jit(solution)/shard_map/ppermute | solution.py:109
  10.5 56.5 %collective-permute-start.9 = (f32[5,16,2,128]{3,2,1,0:T(2,128)}, f32[5,16,2,128]{3,2,1,0:T(2,128)}, u32[]{:S(2)}, u32[]{:S(2)}) collective-permute-start(f32[5,16,2,128]{3,2,1,0:T(2,128)} %get-tuple-element.31), channel_id=1, source_target_pairs={{4,0},{8,4},{12,8},{16,12},{20,16},{24,20},{28,24},{0,28},{5,1},{9... | collective-permute-start | bytes 245768 | tf_op jit(solution)/shard_map/ppermute | solution.py:109
  14.8 6.9 %copy-start.2 = (f32[5,16,32,128]{3,2,1,0:T(8,128)S(1)}, f32[5,16,32,128]{3,2,1,0:T(8,128)}, u32[]{:S(2)}) copy-start(f32[5,16,32,128]{3,2,1,0:T(8,128)} %param.7) | copy-start | bytes 3932164
  16.7 12.3 %collective-permute-start.10 = (f32[5,16,32,2]{2,1,3,0:T(8,128)S(1)}, f32[5,16,32,2]{2,1,3,0:T(8,128)S(1)}, u32[]{:S(2)}, u32[]{:S(2)}) collective-permute-start(f32[5,16,32,2]{2,1,3,0:T(8,128)S(1)} %copy.43), channel_id=1, source_target_pairs={{0,1},{1,2},{2,3},{4,5},{5,6},{6,7},{8,9},{9,10},{10,11},{12,13},{... | collective-permute-start | bytes 61448 | tf_op jit(solution)/shard_map/ppermute | solution.py:108
  20.4 14.9 %collective-permute-start.11 = (f32[5,16,32,2]{2,1,3,0:T(8,128)S(1)}, f32[5,16,32,2]{2,1,3,0:T(8,128)S(1)}, u32[]{:S(2)}, u32[]{:S(2)}) collective-permute-start(f32[5,16,32,2]{2,1,3,0:T(8,128)S(1)} %copy.44), channel_id=1, source_target_pairs={{1,0},{2,1},{3,2},{5,4},{6,5},{7,6},{9,8},{10,9},{11,10},{13,12},{... | collective-permute-start | bytes 61448 | tf_op jit(solution)/shard_map/ppermute | solution.py:109
  22.4 1.6 %copy-start.11 = (s32[1,2,8,6]{2,1,3,0:T(2,128)S(1)}, s32[1,2,8,6]{2,1,3,0:T(2,128)}, u32[]{:S(2)}) copy-start(s32[1,2,8,6]{2,1,3,0:T(2,128)} %param.11) | copy-start | bytes 1156
  24.0 4.5 %copy-start.12 = (s32[1,2,8]{2,1,0:T(2,128)S(1)}, s32[1,2,8]{2,1,0:T(2,128)}, u32[]{:S(2)}) copy-start(s32[1,2,8]{2,1,0:T(2,128)} %param.9) | copy-start | bytes 196
  24.1 11.2 %copy-start.8 = (s32[1,2,8,6]{3,2,1,0:T(8,128)}, s32[1,2,8,6]{3,2,1,0:T(8,128)S(1)}, u32[]{:S(2)}) copy-start(s32[1,2,8,6]{3,2,1,0:T(8,128)S(1)} %copy.37) | copy-start | bytes 1156
  28.5 9.8 %copy-start = (f32[5,16,32,128]{3,2,1,0:T(8,128)S(1)}, f32[5,16,32,128]{3,2,1,0:T(8,128)}, u32[]{:S(2)}) copy-start(f32[5,16,32,128]{3,2,1,0:T(8,128)} %param.6) | copy-start | bytes 3932164
  29.1 18.0 %collective-permute-start.4 = (f32[5,16,32,2]{2,1,3,0:T(8,128)}, f32[5,16,32,2]{2,1,3,0:T(8,128)}, u32[]{:S(2)}, u32[]{:S(2)}) collective-permute-start(f32[5,16,32,2]{2,1,3,0:T(8,128)} %copy.41), channel_id=1, source_target_pairs={{0,1},{1,2},{2,3},{4,5},{5,6},{6,7},{8,9},{9,10},{10,11},{12,13},{... | collective-permute-start | bytes 61448 | tf_op jit(solution)/shard_map/ppermute | solution.py:108
  35.3 16.3 %collective-permute-start.5 = (f32[5,16,32,2]{2,1,3,0:T(8,128)}, f32[5,16,32,2]{2,1,3,0:T(8,128)}, u32[]{:S(2)}, u32[]{:S(2)}) collective-permute-start(f32[5,16,32,2]{2,1,3,0:T(8,128)} %copy.42), channel_id=1, source_target_pairs={{1,0},{2,1},{3,2},{5,4},{6,5},{7,6},{9,8},{10,9},{11,10},{13,12},{... | collective-permute-start | bytes 61448 | tf_op jit(solution)/shard_map/ppermute | solution.py:109
  42.8 1.5 %copy-start.1 = (f32[5,16,32,129]{3,2,1,0:T(8,128)}, f32[5,16,32,129]{3,2,1,0:T(8,128)S(1)}, u32[]{:S(2)}) copy-start(f32[5,16,32,129]{3,2,1,0:T(8,128)S(1)} %fusion.2) | copy-start | bytes 3962884
  45.5 1.5 %copy-start.5 = (f32[5,16,32,129]{3,2,1,0:T(8,128)}, f32[5,16,32,129]{3,2,1,0:T(8,128)S(1)}, u32[]{:S(2)}) copy-start(f32[5,16,32,129]{3,2,1,0:T(8,128)S(1)} %get-tuple-element.12) | copy-start | bytes 3962884
  47.0 21.6 %collective-permute-start.8 = (f32[5,16,2,128]{3,2,1,0:T(2,128)}, f32[5,16,2,128]{3,2,1,0:T(2,128)}, u32[]{:S(2)}, u32[]{:S(2)}) collective-permute-start(f32[5,16,2,128]{3,2,1,0:T(2,128)} %get-tuple-element.30), channel_id=1, source_target_pairs={{0,4},{4,8},{8,12},{12,16},{16,20},{20,24},{24,28},{28,0},{1,5},{5... | collective-permute-start | bytes 245768 | tf_op jit(solution)/shard_map/ppermute | solution.py:108
  51.6 19.2 %collective-permute-start = (f32[5,2,32,128]{3,2,1,0:T(8,128)S(1)}, f32[5,2,32,128]{3,2,1,0:T(8,128)}, u32[]{:S(2)}, u32[]{:S(2)}) collective-permute-start(f32[5,2,32,128]{3,2,1,0:T(8,128)S(1)} %get-tuple-element.19), channel_id=1, source_target_pairs={{0,32},{32,64},{64,96},{96,128},{128,160},{160,192},{192,224},{1,3... | collective-permute-start | bytes 491528 | tf_op jit(solution)/shard_map/ppermute | solution.py:108
  61.1 11.0 %collective-permute-start.1 = (f32[5,2,32,128]{3,2,1,0:T(8,128)S(1)}, f32[5,2,32,128]{3,2,1,0:T(8,128)S(1)}, u32[]{:S(2)}, u32[]{:S(2)}) collective-permute-start(f32[5,2,32,128]{3,2,1,0:T(8,128)S(1)} %get-tuple-element.20), channel_id=1, source_target_pairs={{32,0},{64,32},{96,64},{128,96},{160,128},{192,160},{224,192},{33,... | collective-permute-start | bytes 491528 | tf_op jit(solution)/shard_map/ppermute | solution.py:109
  63.5 0.9 copy-start.7
  64.4 7.8 %collective-permute-start.3 = (f32[5,16,2,128]{3,2,1,0:T(2,128)S(1)}, f32[5,16,2,128]{3,2,1,0:T(2,128)S(1)}, u32[]{:S(2)}, u32[]{:S(2)}) collective-permute-start(f32[5,16,2,128]{3,2,1,0:T(2,128)S(1)} %copy-done.7), channel_id=1, source_target_pairs={{4,0},{8,4},{12,8},{16,12},{20,16},{24,20},{28,24},{0,28},{5,1},{9... | collective-permute-start | bytes 245768 | tf_op jit(solution)/shard_map/ppermute | solution.py:109
  67.0 5.2 %collective-permute-start.2 = (f32[5,16,2,128]{3,2,1,0:T(2,128)S(1)}, f32[5,16,2,128]{3,2,1,0:T(2,128)S(1)}, u32[]{:S(2)}, u32[]{:S(2)}) collective-permute-start(f32[5,16,2,128]{3,2,1,0:T(2,128)S(1)} %get-tuple-element.21), channel_id=1, source_target_pairs={{0,4},{4,8},{8,12},{12,16},{16,20},{20,24},{24,28},{28,0},{1,5},{5... | collective-permute-start | bytes 245768 | tf_op jit(solution)/shard_map/ppermute | solution.py:108
  71.7 1.3 %copy-start.3 = (f32[5,16,32,2]{3,2,1,0:T(8,128)S(1)}, f32[5,16,32,2]{3,2,1,0:T(8,128)}, u32[]{:S(2)}) copy-start(f32[5,16,32,2]{3,2,1,0:T(8,128)} %copy.30) | copy-start | bytes 61444
  71.7 1.7 %copy-start.4 = (f32[5,16,32,2]{3,2,1,0:T(8,128)S(1)}, f32[5,16,32,2]{3,2,1,0:T(8,128)}, u32[]{:S(2)}) copy-start(f32[5,16,32,2]{3,2,1,0:T(8,128)} %copy.32) | copy-start | bytes 61444
  71.7 2.5 %copy-start.6 = (f32[5,16,32,129]{3,2,1,0:T(8,128)S(1)}, f32[5,16,32,129]{3,2,1,0:T(8,128)}, u32[]{:S(2)}) copy-start(f32[5,16,32,129]{3,2,1,0:T(8,128)} %multiply_dynamic-update-slice_fusion) | copy-start | bytes 3962884
  74.2 31.8 %copy-start.10 = (s32[1024]{0:T(1024)S(1)}, s32[1024]{0:T(1024)}, u32[]{:S(2)}) copy-start(s32[1024]{0:T(1024)} %pad_clamp_fusion) | copy-start | bytes 12292
  106.1 1.3 copy-start.9
  106.1 1.4 %copy-start.13 = (s32[1,2,8]{2,1,0:T(2,128)S(1)}, s32[1,2,8]{2,1,0:T(2,128)}, u32[]{:S(2)}) copy-start(s32[1,2,8]{2,1,0:T(2,128)} %param.9) | copy-start | bytes 196
  106.1 1.4 %copy-start.14 = (s32[1,2,8]{2,1,0:T(2,128)S(1)}, s32[1,2,8]{2,1,0:T(2,128)}, u32[]{:S(2)}) copy-start(s32[1,2,8]{2,1,0:T(2,128)} %param.10) | copy-start | bytes 196
  106.1 1.4 %copy-start.15 = (s32[1,2,8]{2,1,0:T(2,128)S(1)}, s32[1,2,8]{2,1,0:T(2,128)}, u32[]{:S(2)}) copy-start(s32[1,2,8]{2,1,0:T(2,128)} %param.8) | copy-start | bytes 196
  106.1 1.5 %copy-start.17 = (f32[16]{0:T(128)S(1)}, f32[16]{0:T(128)}, u32[]{:S(2)}) copy-start(f32[16]{0:T(128)} %convert_element_type.19) | copy-start | bytes 196
  107.5 21.0 %copy-start.16 = (f32[1,2,8]{2,1,0:T(2,128)}, f32[1,2,8]{2,1,0:T(2,128)S(1)}, u32[]{:S(2)}) copy-start(f32[1,2,8]{2,1,0:T(2,128)S(1)} %fusion.54) | copy-start | bytes 196

commit v2 on v1

--- a/solution.py
+++ b/solution.py
@@ -97,71 +97,150 @@
     return out.reshape(-1)
 
 
-def halo_pair(parts, axis, dim, periodic):
+def dense(x):
+    return x.reshape(-1, 128)
+
+
+def exchange(tail, head, axis, periodic):
     count = lax.axis_size(axis)
     forward = [(i, i + 1) for i in range(count - 1)]
     if periodic:
         forward.append((count - 1, 0))
     backward = [(target, source) for source, target in forward]
-    tails = tuple(lax.slice_in_dim(p, p.shape[dim] - 2, None, axis=dim) for p in parts)
-    heads = tuple(lax.slice_in_dim(p, 0, 2, axis=dim) for p in parts)
-    low = lax.ppermute(tails, axis, forward)
-    high = lax.ppermute(heads, axis, backward)
-    return tuple(jnp.concatenate([lo, p, hi], axis=dim) for lo, p, hi in zip(low, parts, high))
-
-
-def euler_flux(face_state, along):
-    density = face_state[0]
-    momenta = face_state[1:4]
-    energy = face_state[4]
-    velocity = momenta[along] / density
-    kinetic = (
-        0.5
-        * (momenta[0] * momenta[0] + momenta[1] * momenta[1] + momenta[2] * momenta[2])
-        / density
+    low = lax.ppermute(dense(tail), axis, forward).reshape(tail.shape)
+    high = lax.ppermute(dense(head), axis, backward).reshape(head.shape)
+    return low, high
+
+
+def flux_pair(state_lo, state_hi, along):
+    return [h - l for h, l in zip(euler_flux(state_hi, along), euler_flux(state_lo, along))]
+
+
+def euler_flux(s, along):
+    density, m0, m1, m2, energy = s
+    momenta = (m0, m1, m2)
+    inv = 1.0 / density
+    velocity = momenta[along] * inv
+    kinetic = 0.5 * (m0 * m0 + m1 * m1 + m2 * m2) * inv
+    pressure = 0.4 * (energy - kinetic)
+    columns = [momenta[along], m0 * velocity, m1 * velocity, m2 * velocity, (energy + pressure) * velocity]
+    columns[1 + along] = columns[1 + along] + pressure
+    return columns
+
+
+def faces(um2, um1, u, up1, up2):
+    lower = (7.0 * um1 - um2) / 12.0 + (7.0 * u - up1) / 12.0
+    upper = (7.0 * u - um1) / 12.0 + (7.0 * up1 - up2) / 12.0
+    return lower, upper
+
+
+def fourth(zm2, zm1, z, zp1, zp2):
+    return (zm2 - 4.0 * zm1 + 6.0 * z - 4.0 * zp1 + zp2) / 12.0
+
+
+def stencil_kernel(p_hbm, a_hbm, rl, rh, al, ah, xl, xh, out_ref, ep, ea, sems):
+    fields, rows = ep.shape[0], ep.shape[1] - 4
+    copies = [
+        pltpu.make_async_copy(p_hbm, ep.at[:, pl.ds(2, rows)], sems.at[0]),
+        pltpu.make_async_copy(a_hbm, ea.at[:, pl.ds(2, rows)], sems.at[1]),
+    ]
+    for c in copies:
+        c.start()
+    ep[:, 0:2] = rl[0]
+    ea[:, 0:2] = rl[1]
+    ep[:, rows + 2:rows + 4] = rh[0]
+    ea[:, rows + 2:rows + 4] = rh[1]
+    for c in copies:
+        c.wait()
+    n_a, n_x = ep.shape[2], ep.shape[3]
+    sub = lax.broadcasted_iota(jnp.int32, (n_a, n_x), 0)
+    lane = lax.broadcasted_iota(jnp.int32, (n_a, n_x), 1)
+
+    def shifted_azi(u, lo, hi):
+        um1 = jnp.where(sub == 0, jnp.broadcast_to(lo[1:2], u.shape), pltpu.roll(u, 1, 0))
+        um2 = jnp.where(sub == 0, jnp.broadcast_to(lo[0:1], u.shape),
+                        jnp.where(sub == 1, jnp.broadcast_to(lo[1:2], u.shape), pltpu.roll(u, 2, 0)))
+        up1 = jnp.where(sub == n_a - 1, jnp.broadcast_to(hi[0:1], u.shape), pltpu.roll(u, n_a - 1, 0))
+        up2 = jnp.where(sub == n_a - 1, jnp.broadcast_to(hi[1:2], u.shape),
+                        jnp.where(sub == n_a - 2, jnp.broadcast_to(hi[0:1], u.shape), pltpu.roll(u, n_a - 2, 0)))
+        return um2, um1, u, up1, up2
+
+    def shifted_ax(u, lo, hi):
+        um1 = jnp.where(lane == 0, jnp.broadcast_to(lo[:, 1:2], u.shape), pltpu.roll(u, 1, 1))
+        um2 = jnp.where(lane == 0, jnp.broadcast_to(lo[:, 0:1], u.shape),
+                        jnp.where(lane == 1, jnp.broadcast_to(lo[:, 1:2], u.shape), pltpu.roll(u, 2, 1)))
+        up1 = jnp.where(lane == n_x - 1, jnp.broadcast_to(hi[:, 0:1], u.shape), pltpu.roll(u, n_x - 1, 1))
+        up2 = jnp.where(lane == n_x - 1, jnp.broadcast_to(hi[:, 1:2], u.shape),
+                        jnp.where(lane == n_x - 2, jnp.broadcast_to(hi[:, 0:1], u.shape), pltpu.roll(u, n_x - 2, 1)))
+        return um2, um1, u, up1, up2
+
+    def row(r, carry):
+        balance = None
+        weight = None
+        lo_s, hi_s = [], []
+        w = []
+        for f in range(fields):
+            e = [ep[f, r + k] for k in range(5)]
+            lo, hi = faces(*e)
+            lo_s.append(lo)
+            hi_s.append(hi)
+            w.append(fourth(*[ea[f, r + k] for k in range(5)]))
+        balance = flux_pair(lo_s, hi_s, 0)
+        weight = w
+        lo_s, hi_s, w = [], [], []
+        for f in range(fields):
+            lo, hi = faces(*shifted_azi(ep[f, r + 2], al[0, f, r], ah[0, f, r]))
+            lo_s.append(lo)
+            hi_s.append(hi)
+            w.append(fourth(*shifted_azi(ea[f, r + 2], al[1, f, r], ah[1, f, r])))
+        part = flux_pair(lo_s, hi_s, 1)
+        balance = [b + p for b, p in zip(balance, part)]
+        weight = [a + b for a, b in zip(weight, w)]
+        lo_s, hi_s, w = [], [], []
+        for f in range(fields):
+            lo, hi = faces(*shifted_ax(ep[f, r + 2], xl[0, f, r], xh[0, f, r]))
+            lo_s.append(lo)
+            hi_s.append(hi)
+            w.append(fourth(*shifted_ax(ea[f, r + 2], xl[1, f, r], xh[1, f, r])))
+        part = flux_pair(lo_s, hi_s, 2)
+        balance = [b + p for b, p in zip(balance, part)]
+        weight = [a + b for a, b in zip(weight, w)]
+        total = weight[0] * balance[0]
+        for f in range(1, fields):
+            total = total + weight[f] * balance[f]
+        out_ref[r] = jnp.abs(total)
+        return carry
+
+    lax.fori_loop(0, rows, row, 0)
+
+
+def stencil(primal, adjoint, rl, rh, al, ah, xl, xh):
+    fields, rows, n_a, n_x = primal.shape
+    vmem = pl.BlockSpec(memory_space=pltpu.VMEM)
+    anywhere = pl.BlockSpec(memory_space=pl.ANY)
+    return pl.pallas_call(
+        stencil_kernel,
+        out_shape=jax.ShapeDtypeStruct((rows, n_a, n_x), jnp.float32),
+        in_specs=[anywhere, anywhere] + [vmem] * 6,
+        out_specs=vmem,
+        scratch_shapes=[
+            pltpu.VMEM((fields, rows + 4, n_a, n_x), jnp.float32),
+            pltpu.VMEM((fields, rows + 4, n_a, n_x), jnp.float32),
+            pltpu.SemaphoreType.DMA((2,)),
+        ],
+        compiler_params=pltpu.CompilerParams(vmem_limit_bytes=48 * 1024 * 1024),
+    )(primal, adjoint, rl, rh, al, ah, xl, xh)
+
+
+def on_device(primal, adjoint, refine_flag, owner_map, migrate_weight, neighbor_list):
+    both = jnp.stack([primal, adjoint])
+    rl, rh = exchange(both[:, :, -2:], both[:, :, :2], "rad", False)
+    al, ah = exchange(both[:, :, :, -2:], both[:, :, :, :2], "azi", True)
+    xl, xh = exchange(
+        jnp.swapaxes(both[..., -2:], -1, -2), jnp.swapaxes(both[..., :2], -1, -2), "ax", False
     )
-    pressure = 0.4 * (energy - kinetic)
-    columns = [
-        momenta[along],
-        momenta[0] * velocity,
-        momenta[1] * velocity,
-        momenta[2] * velocity,
-        (energy + pressure) * velocity,
-    ]
-    columns[1 + along] = columns[1 + along] + pressure
-    return jnp.stack(columns)
-
-
-def axis_terms(ext_p, ext_a, dim):
-    length = ext_p.shape[dim] - 4
-    win = lambda e, s, c: lax.slice_in_dim(e, s, s + c, axis=dim)
-    high = (7.0 * win(ext_p, 1, length + 1) - win(ext_p, 0, length + 1)) / 12.0
-    low = (7.0 * win(ext_p, 2, length + 1) - win(ext_p, 3, length + 1)) / 12.0
-    fluxes = euler_flux(high + low, dim - 1)
-    balance = win(fluxes, 1, length) - win(fluxes, 0, length)
-    fourth = (
-        win(ext_a, 0, length)
-        - 4.0 * win(ext_a, 1, length)
-        + 6.0 * win(ext_a, 2, length)
-        - 4.0 * win(ext_a, 3, length)
-        + win(ext_a, 4, length)
-    ) / 12.0
-    return balance, fourth
-
-
-def on_device(primal, adjoint, refine_flag, owner_map, migrate_weight, neighbor_list):
-    ext = {
-        1: halo_pair((primal, adjoint), "rad", 1, False),
-        2: halo_pair((primal, adjoint), "azi", 2, True),
-        3: halo_pair((primal, adjoint), "ax", 3, False),
-    }
-    balance = None
-    weight = None
-    for along in (1, 2, 3):
-        part_balance, part_weight = axis_terms(ext[along][0], ext[along][1], along)
-        balance = part_balance if balance is None else balance + part_balance
-        weight = part_weight if weight is None else weight + part_weight
-    indicator = jnp.abs(jnp.sum(weight * balance, axis=0))
+    xl, xh = jnp.swapaxes(xl, -1, -2), jnp.swapaxes(xh, -1, -2)
+    indicator = stencil(primal, adjoint, rl, rh, al, ah, xl, xh)
     rows_rad, rows_azi, rows_ax = indicator.shape
     per_rad = rows_rad // BLK
     per_azi = rows_azi // BLK

time: 130 us -> 103 us (0.79)
  local copies, waits for them, and re-layouts: 37.3 us -> 21.1 us
  starting transfers between devices: 27.7 us -> 12.6 us
  Pallas kernels: 44.2 us -> 55.5 us
  other arithmetic: 17.5 us -> 11 us
    ppermute x12 -> x6, starting transfers between devices: 27.7 us -> 12.6 us  [the longest x3 10 us: exchange(): low = lax.ppermute(dense(tail), axis, forward).reshape(tail.shape)]
    pallas_call x0 -> x1, Pallas kernels: none -> 12.1 us  [stencil(): pl.pallas_call(stencil_kernel, out_shape=jax.ShapeDtypeStruct((rows, n_a,...]
    unnamed x46 -> x17, local copies, waits for them, and re-layouts: 13.5 us -> 1.85 us
    reshape x0 -> x6, local copies, waits for them, and re-layouts: none -> 10.4 us  [the longest x2 4.66 us: exchange(): high = lax.ppermute(dense(head), axis, backward).reshape(head.shape)]
    slice x6 -> x0, local copies, waits for them, and re-layouts: 9.13 us -> none  [halo_pair(): lax.slice_in_dim(p, p.shape[dim] - 2, None, axis=dim)]
    ppermute x4 -> x0, local copies, waits for them, and re-layouts: 8.25 us -> none  [the longest x2 4.13 us: halo_pair(): low = lax.ppermute(tails, axis, forward)]
    add x3 -> x0, other arithmetic: 6.59 us -> none  [axis_terms(): fluxes = euler_flux(high + low, dim - 1)]
    transpose x0 -> x1, other arithmetic: none -> 5.68 us  [on_device(): jnp.swapaxes(both[..., :2], -1, -2)]
  transfers between devices with their start and end apart: 12 -> 6, of which waited for: 0 -> 0; matrix products, arithmetic and copies ran while one was open for 30% -> 14% of each run, Pallas kernels for 0% -> 0%
where the time goes in v2:
time: 103 us
  Pallas kernels  55.5 us (54%)
  local copies, waits for them, and re-layouts  21.1 us (20%)
  starting transfers between devices  12.6 us (12%)
  other arithmetic  11 us (11%)
  between operations  2.62 us (3%)
    pallas_call x2, Pallas kernels, gather_all(): pl.pallas_call(functools.partial(gather_kernel, (n_r, n_a, n_x)), out_sha...  43.4 us
    pallas_call x1, Pallas kernels, stencil(): pl.pallas_call(stencil_kernel, out_shape=jax.ShapeDtypeStruct((rows, n_a,...  12.1 us
    ppermute x3, starting transfers between devices, exchange(): low = lax.ppermute(dense(tail), axis, forward).reshape(tail.shape)  10 us
    transpose x1, other arithmetic, on_device(): jnp.swapaxes(both[..., :2], -1, -2)  5.68 us
    reshape x2, local copies, waits for them, and re-layouts, exchange(): high = lax.ppermute(dense(head), axis, backward).reshape(head.shape)  4.66 us
    reshape x2, local copies, waits for them, and re-layouts, exchange(): low = lax.ppermute(dense(tail), axis, forward).reshape(tail.shape)  3.9 us
    transpose x1, local copies, waits for them, and re-layouts, on_device(): jnp.swapaxes(both[..., :2], -1, -2)  3.03 us
    ppermute x3, starting transfers between devices, exchange(): high = lax.ppermute(dense(head), axis, backward).reshape(head.shape)  2.59 us
  transfers between devices with their start and end apart: 6, of which 0 were waited for; matrix products, arithmetic and copies ran while one was open for 14% of the time, Pallas kernels for 0%

profile of v2, /device:TPU:1, one launch (start us, length us, event | category | flops | bytes accessed | tf_op | source)
XLA Modules:
  0.0 102.8 jit_solution(5873599915390060030)
XLA Ops:
  0.6 5.7 %fusion = (f32[2,5,16,2,32]{3,4,2,1,0:T(8,128)}, f32[2,5,16,2,32]{3,4,2,1,0:T(8,128)}) fusion(f32[1,5,16,32,128]{4,3,2,1,0:T(8,128)} %bitcast.29, f32[1,5,16,32,128]{4,3,2,1,0:T(8,128)} %bitcast.26), kind=kLoop, calls=%fused_computation.2 | loop fusion | flops 20480 | bytes 2703360 | tf_op jit(solution)/shard_map/transpose | solution.py:240
  6.3 0.0 copy-start
  6.3 0.0 copy-start.1
  6.3 2.6 %copy.21 = f32[2,5,16,2,32]{4,3,2,1,0:T(2,128)S(1)} copy(f32[2,5,16,2,32]{3,4,2,1,0:T(8,128)} %get-tuple-element.4) | data formatting | bytes 81920 | tf_op jit(solution)/shard_map/transpose | solution.py:240
  8.9 0.8 reshape.124
  9.7 0.0 copy-start.3
  9.7 4.1 %collective-permute-start.4 = (f32[80,128]{1,0:T(8,128)}, f32[80,128]{1,0:T(8,128)S(1)}, u32[]{:S(2)}, u32[]{:S(2)}) collective-permute-start(f32[80,128]{1,0:T(8,128)} %reshape.124), channel_id=1, source_target_pairs={{0,1},{1,2},{2,3},{4,5},{5,6},{6,7},{8,9},{9,10},{10,11},{12,13},{... | collective-permute-start | bytes 122888 | tf_op jit(solution)/shard_map/ppermute | solution.py:110
  13.8 0.0 copy-done
  13.8 0.0 copy-done.1
  13.8 0.9 pad_maximum_fusion.1
  14.7 3.5 %collective-permute-start = (f32[640,128]{1,0:T(8,128)}, f32[640,128]{1,0:T(8,128)S(1)}, u32[]{:S(2)}, u32[]{:S(2)}) collective-permute-start(f32[640,128]{1,0:T(8,128)} %bitcast.2), channel_id=1, source_target_pairs={{0,32},{32,64},{64,96},{96,128},{128,160},{160,192},{192,224},{1,3... | collective-permute-start | bytes 983048 | tf_op jit(solution)/shard_map/ppermute | solution.py:110
  18.3 0.0 copy-start.4
  18.3 1.3 %collective-permute-start.1 = (f32[640,128]{1,0:T(8,128)}, f32[640,128]{1,0:T(8,128)S(1)}, u32[]{:S(2)}, u32[]{:S(2)}) collective-permute-start(f32[640,128]{1,0:T(8,128)} %bitcast.4), channel_id=1, source_target_pairs={{32,0},{64,32},{96,64},{128,96},{160,128},{192,160},{224,192},{33,... | collective-permute-start | bytes 983048 | tf_op jit(solution)/shard_map/ppermute | solution.py:111
  19.6 0.9 pad_maximum_fusion.3
  20.4 2.4 %collective-permute-start.2 = (f32[320,128]{1,0:T(8,128)}, f32[320,128]{1,0:T(8,128)S(1)}, u32[]{:S(2)}, u32[]{:S(2)}) collective-permute-start(f32[320,128]{1,0:T(8,128)} %bitcast.6), channel_id=1, source_target_pairs={{0,4},{4,8},{8,12},{12,16},{16,20},{20,24},{24,28},{28,0},{1,5},{5... | collective-permute-start | bytes 491528 | tf_op jit(solution)/shard_map/ppermute | solution.py:110
  22.9 0.0 collective-permute-start.3
  22.9 0.0 copy-done.3
  22.9 0.1 copy.25
  23.0 3.0 %copy.23 = f32[2,5,16,2,32]{4,3,2,1,0:T(2,128)} copy(f32[2,5,16,2,32]{3,4,2,1,0:T(8,128)} %get-tuple-element.3) | data formatting | bytes 81920 | tf_op jit(solution)/shard_map/transpose | solution.py:240
  26.0 1.1 %reshape.126 = f32[80,128]{1,0:T(8,128)S(1)} reshape(f32[2,5,16,2,32]{4,3,2,1,0:T(2,128)} %copy.23) | data formatting | bytes 81920 | tf_op jit(solution)/shard_map/reshape | solution.py:101
  27.1 0.1 reshape.134
  27.2 0.0 collective-permute-done.4
  27.2 1.3 %collective-permute-start.5 = (f32[80,128]{1,0:T(8,128)S(1)}, f32[80,128]{1,0:T(8,128)}, u32[]{:S(2)}, u32[]{:S(2)}) collective-permute-start(f32[80,128]{1,0:T(8,128)S(1)} %reshape.126), channel_id=1, source_target_pairs={{1,0},{2,1},{3,2},{5,4},{6,5},{7,6},{9,8},{10,9},{11,10},{13,12},{... | collective-permute-start | bytes 122888 | tf_op jit(solution)/shard_map/ppermute | solution.py:111
  28.5 0.0 copy-done.4
  28.5 0.1 convert_element_type.19
  28.6 0.8 reshape.125
  29.5 3.0 %copy.22 = f32[2,5,16,2,32]{3,4,2,1,0:T(8,128)} copy(f32[2,5,16,2,32]{4,3,2,1,0:T(2,128)} %reshape.125) | data formatting | bytes 81920 | tf_op jit(solution)/shard_map/reshape | solution.py:110
  32.5 0.0 collective-permute-done.5
  32.5 1.6 %reshape.127 = f32[2,5,16,2,32]{4,3,2,1,0:T(2,128)} reshape(f32[80,128]{1,0:T(8,128)} %collective-permute-done.5) | data formatting | bytes 81920 | tf_op jit(solution)/shard_map/reshape | solution.py:111
  34.1 3.0 %copy.24 = f32[2,5,16,2,32]{3,4,2,1,0:T(8,128)} copy(f32[2,5,16,2,32]{4,3,2,1,0:T(2,128)} %reshape.127) | data formatting | bytes 81920 | tf_op jit(solution)/shard_map/reshape | solution.py:111
  37.2 0.0 collective-permute-done.2
  37.2 0.0 collective-permute-done.3
  37.2 0.0 collective-permute-done
  37.2 0.0 collective-permute-done.1
  37.2 0.0 copy-start.2
  37.2 1.7 %copy-done.2 = f32[2,5,16,2,32]{3,4,2,1,0:T(8,128)S(1)} copy-done((f32[2,5,16,2,32]{3,4,2,1,0:T(8,128)S(1)}, f32[2,5,16,2,32]{3,4,2,1,0:T(8,128)}, u32[]{:S(2)}) %copy-start.2) | copy-done | bytes 40984
  39.0 12.1 %shard_map.85 = f32[16,32,128]{2,1,0:T(8,128)} custom-call(f32[5,16,32,128]{3,2,1,0:T(8,128)S(1)} %copy-done, f32[5,16,32,128]{3,2,1,0:T(8,128)S(1)} %copy-done.1, f32[2,5,2,32,128]{4,3,2,1,0:T(8,128)S(1)} %bitcast.33, f32[2,5,2,32,128]{4,3,2,1,0:T(8,128)S(1)} %bitcast.34, f32[2,5,16,2,128]{4,3,2,1,0:T(2,128)S(1)} %bitcast.35, ...), custom_call_target="tpu_custom_call" | custom-call | tf_op jit(solution)/shard_map/pallas_call | solution.py:221
  51.0 1.0 reduce_sum.34
  52.0 0.1 reduce_sum.35
  52.1 0.1 reduce_sum.36
  52.2 0.6 div.67.x_ref
  52.8 26.0 %shard_map.86 = f32[8,8,4,16]{3,2,1,0:T(4,128)} custom-call(f32[1,1,1,16]{3,2,1,0:T(1,128)} %div.67.x_ref), custom_call_target="tpu_custom_call" | custom-call | tf_op jit(solution)/shard_map/pallas_call | solution.py:85
  78.8 1.0 %reshape.128 = f32[4096]{0:T(1024)S(1)} reshape(f32[8,8,4,16]{3,2,1,0:T(4,128)} %shard_map.86) | data formatting | bytes 32768 | tf_op jit(solution)/shard_map/reshape | solution.py:97
  79.8 0.0 copy-start.5
  79.8 0.0 copy-start.6
  79.9 1.1 %gather_fusion = f32[96]{0:T(128)S(1)} fusion(f32[4096]{0:T(1024)S(1)} %reshape.128, s32[1024]{0:T(1024)S(1)} %pad_clamp_fusion), kind=kCustom, calls=%fused_computation | custom fusion | bytes 1152 | tf_op jit(solution)/shard_map/jit(_take)/gather | solution.py:263
  81.0 0.1 reshape.133
  81.1 0.1 select_reduce_fusion
  81.2 0.0 copy-done.5
  81.2 0.0 copy-done.6
  81.2 0.0 copy-start.7
  81.2 0.1 reshape.129
  81.3 0.6 maximum_bitcast_fusion.1.x_ref
  81.9 17.4 %shard_map.87 = f32[8,8,4,32]{3,2,1,0:T(4,128)} custom-call(f32[1,1,1,32]{3,2,1,0:T(1,128)} %maximum_bitcast_fusion.1.x_ref), custom_call_target="tpu_custom_call" | custom-call | tf_op jit(solution)/shard_map/pallas_call | solution.py:85
  99.3 1.7 %fusion.1 = f32[]{:T(128)} fusion(f32[256,32]{1,0:T(8,128)} %bitcast.37, f32[]{:T(128)S(6)} %convert_element_type.20), kind=kLoop, calls=%fused_computation.9 | loop fusion | flops 12287 | bytes 32776 | tf_op jit(solution)/shard_map/reduce_sum | solution.py:278
  101.7 0.0 copy-done.7
  (5 shorter events, 0.1 us)
Async XLA Ops:
  6.3 7.4 %copy-start = (f32[5,16,32,128]{3,2,1,0:T(8,128)S(1)}, f32[5,16,32,128]{3,2,1,0:T(8,128)}, u32[]{:S(2)}) copy-start(f32[5,16,32,128]{3,2,1,0:T(8,128)} %p_hbm.1) | copy-start | bytes 3932164
  6.3 7.5 %copy-start.1 = (f32[5,16,32,128]{3,2,1,0:T(8,128)S(1)}, f32[5,16,32,128]{3,2,1,0:T(8,128)}, u32[]{:S(2)}) copy-start(f32[5,16,32,128]{3,2,1,0:T(8,128)} %a_hbm.1) | copy-start | bytes 3932164
  9.7 13.2 %copy-start.3 = (s32[1,2,8,6]{2,1,3,0:T(2,128)S(1)}, s32[1,2,8,6]{2,1,3,0:T(2,128)}, u32[]{:S(2)}) copy-start(s32[1,2,8,6]{2,1,3,0:T(2,128)} %param.11) | copy-start | bytes 1156
  9.7 17.5 %collective-permute-start.4 = (f32[80,128]{1,0:T(8,128)}, f32[80,128]{1,0:T(8,128)S(1)}, u32[]{:S(2)}, u32[]{:S(2)}) collective-permute-start(f32[80,128]{1,0:T(8,128)} %reshape.124), channel_id=1, source_target_pairs={{0,1},{1,2},{2,3},{4,5},{5,6},{6,7},{8,9},{9,10},{10,11},{12,13},{... | collective-permute-start | bytes 122888 | tf_op jit(solution)/shard_map/ppermute | solution.py:110
  14.7 22.5 %collective-permute-start = (f32[640,128]{1,0:T(8,128)}, f32[640,128]{1,0:T(8,128)S(1)}, u32[]{:S(2)}, u32[]{:S(2)}) collective-permute-start(f32[640,128]{1,0:T(8,128)} %bitcast.2), channel_id=1, source_target_pairs={{0,32},{32,64},{64,96},{96,128},{128,160},{160,192},{192,224},{1,3... | collective-permute-start | bytes 983048 | tf_op jit(solution)/shard_map/ppermute | solution.py:110
  18.3 10.3 %copy-start.4 = (s32[1,2,8]{2,1,0:T(2,128)S(1)}, s32[1,2,8]{2,1,0:T(2,128)}, u32[]{:S(2)}) copy-start(s32[1,2,8]{2,1,0:T(2,128)} %param.9) | copy-start | bytes 196
  18.3 18.9 %collective-permute-start.1 = (f32[640,128]{1,0:T(8,128)}, f32[640,128]{1,0:T(8,128)S(1)}, u32[]{:S(2)}, u32[]{:S(2)}) collective-permute-start(f32[640,128]{1,0:T(8,128)} %bitcast.4), channel_id=1, source_target_pairs={{32,0},{64,32},{96,64},{128,96},{160,128},{192,160},{224,192},{33,... | collective-permute-start | bytes 983048 | tf_op jit(solution)/shard_map/ppermute | solution.py:111
  20.4 16.8 %collective-permute-start.2 = (f32[320,128]{1,0:T(8,128)}, f32[320,128]{1,0:T(8,128)S(1)}, u32[]{:S(2)}, u32[]{:S(2)}) collective-permute-start(f32[320,128]{1,0:T(8,128)} %bitcast.6), channel_id=1, source_target_pairs={{0,4},{4,8},{8,12},{12,16},{16,20},{20,24},{24,28},{28,0},{1,5},{5... | collective-permute-start | bytes 491528 | tf_op jit(solution)/shard_map/ppermute | solution.py:110
  22.9 14.3 %collective-permute-start.3 = (f32[320,128]{1,0:T(8,128)}, f32[320,128]{1,0:T(8,128)}, u32[]{:S(2)}, u32[]{:S(2)}) collective-permute-start(f32[320,128]{1,0:T(8,128)} %bitcast.8), channel_id=1, source_target_pairs={{4,0},{8,4},{12,8},{16,12},{20,16},{24,20},{28,24},{0,28},{5,1},{9... | collective-permute-start | bytes 491528 | tf_op jit(solution)/shard_map/ppermute | solution.py:111
  27.2 5.3 %collective-permute-start.5 = (f32[80,128]{1,0:T(8,128)S(1)}, f32[80,128]{1,0:T(8,128)}, u32[]{:S(2)}, u32[]{:S(2)}) collective-permute-start(f32[80,128]{1,0:T(8,128)S(1)} %reshape.126), channel_id=1, source_target_pairs={{1,0},{2,1},{3,2},{5,4},{6,5},{7,6},{9,8},{10,9},{11,10},{13,12},{... | collective-permute-start | bytes 122888 | tf_op jit(solution)/shard_map/ppermute | solution.py:111
  37.2 1.7 %copy-start.2 = (f32[2,5,16,2,32]{3,4,2,1,0:T(8,128)S(1)}, f32[2,5,16,2,32]{3,4,2,1,0:T(8,128)}, u32[]{:S(2)}) copy-start(f32[2,5,16,2,32]{3,4,2,1,0:T(8,128)} %copy.22) | copy-start | bytes 122884
  79.8 1.4 %copy-start.5 = (s32[1,2,8]{2,1,0:T(2,128)S(1)}, s32[1,2,8]{2,1,0:T(2,128)}, u32[]{:S(2)}) copy-start(s32[1,2,8]{2,1,0:T(2,128)} %param.10) | copy-start | bytes 196
  79.8 1.4 %copy-start.6 = (s32[1,2,8]{2,1,0:T(2,128)S(1)}, s32[1,2,8]{2,1,0:T(2,128)}, u32[]{:S(2)}) copy-start(s32[1,2,8]{2,1,0:T(2,128)} %param.8) | copy-start | bytes 196
  81.2 20.5 %copy-start.7 = (f32[1,2,8]{2,1,0:T(2,128)}, f32[1,2,8]{2,1,0:T(2,128)S(1)}, u32[]{:S(2)}) copy-start(f32[1,2,8]{2,1,0:T(2,128)S(1)} %fusion.22) | copy-start | bytes 196

commit v3 on v2

--- a/solution.py
+++ b/solution.py
@@ -138,21 +138,112 @@
     return (zm2 - 4.0 * zm1 + 6.0 * z - 4.0 * zp1 + zp2) / 12.0
 
 
-def stencil_kernel(p_hbm, a_hbm, rl, rh, al, ah, xl, xh, out_ref, ep, ea, sems):
-    fields, rows = ep.shape[0], ep.shape[1] - 4
-    copies = [
-        pltpu.make_async_copy(p_hbm, ep.at[:, pl.ds(2, rows)], sems.at[0]),
-        pltpu.make_async_copy(a_hbm, ea.at[:, pl.ds(2, rows)], sems.at[1]),
+def stencil_kernel(p_hbm, a_hbm, out_ref, e, az_send, az_recv, az_exp, x_send, x_recv, xt, sems, ssem, rsem):
+    _, fields, ext_rows, n_a, n_x = e.shape
+    rows = ext_rows - 4
+    n_r_dev, n_a_dev, n_x_dev = (lax.axis_size(ax) for ax in AXES)
+    me_r, me_a, me_x = (lax.axis_index(ax) for ax in AXES)
+    has_r_lo, has_r_hi = me_r > 0, me_r < n_r_dev - 1
+    has_x_lo, has_x_hi = me_x > 0, me_x < n_x_dev - 1
+    r_lo, r_hi = (me_r - 1, me_a, me_x), (me_r + 1, me_a, me_x)
+    a_lo = (me_r, lax.rem(me_a + n_a_dev - 1, n_a_dev), me_x)
+    a_hi = (me_r, lax.rem(me_a + 1, n_a_dev), me_x)
+    x_lo, x_hi = (me_r, me_a, me_x - 1), (me_r, me_a, me_x + 1)
+
+    loads = [
+        pltpu.make_async_copy(p_hbm, e.at[0, :, pl.ds(2, rows)], sems.at[0]),
+        pltpu.make_async_copy(a_hbm, e.at[1, :, pl.ds(2, rows)], sems.at[1]),
     ]
-    for c in copies:
+    for c in loads:
         c.start()
-    ep[:, 0:2] = rl[0]
-    ea[:, 0:2] = rl[1]
-    ep[:, rows + 2:rows + 4] = rh[0]
-    ea[:, rows + 2:rows + 4] = rh[1]
-    for c in copies:
+
+    barrier = pltpu.get_barrier_semaphore()
+    for cond, dev in ((has_r_lo, r_lo), (has_r_hi, r_hi), (has_x_lo, x_lo), (has_x_hi, x_hi)):
+        @pl.when(cond)
+        def _():
+            pl.semaphore_signal(barrier, 1, device_id=dev, device_id_type=MESH)
+    pl.semaphore_signal(barrier, 1, device_id=a_lo, device_id_type=MESH)
+    pl.semaphore_signal(barrier, 1, device_id=a_hi, device_id_type=MESH)
+    count = 2 + sum(c.astype(jnp.int32) for c in (has_r_lo, has_r_hi, has_x_lo, has_x_hi))
+    pl.semaphore_wait(barrier, count)
+
+    x_recv[:, x_send.shape[1]:, :] = jnp.zeros((2, x_recv.shape[1] - x_send.shape[1], x_recv.shape[2]), jnp.float32)
+    x_send[:, 4 * fields:, :] = jnp.zeros((2, x_send.shape[1] - 4 * fields, x_send.shape[2]), jnp.float32)
+    for c in loads:
         c.wait()
-    n_a, n_x = ep.shape[2], ep.shape[3]
+
+    for k in range(2):
+        for f in range(fields):
+            for r in range(rows):
+                row = ((k * fields + f) * rows + r) * 2
+                az_send[0, row:row + 2, :] = e[k, f, 2 + r, 0:2, :]
+                az_send[1, row:row + 2, :] = e[k, f, 2 + r, n_a - 2:n_a, :]
+            plane = e[k, f, 2:2 + rows].reshape(rows * n_a, n_x)
+            cols = plane.T
+            row = (k * fields + f) * 2
+            x_send[0, row:row + 2, :] = cols[0:2]
+            x_send[1, row:row + 2, :] = cols[n_x - 2:n_x]
+
+    def remote(src, dst, i, dev):
+        return pltpu.make_async_remote_copy(
+            src_ref=src, dst_ref=dst, send_sem=ssem.at[i], recv_sem=rsem.at[i],
+            device_id=dev, device_id_type=MESH,
+        )
+
+    n_kx = x_send.shape[1]
+    sends = [
+        (has_r_hi, remote(e.at[:, :, pl.ds(rows, 2)], e.at[:, :, pl.ds(0, 2)], 0, r_hi)),
+        (has_r_lo, remote(e.at[:, :, pl.ds(2, 2)], e.at[:, :, pl.ds(rows + 2, 2)], 1, r_lo)),
+        (None, remote(az_send.at[1], az_recv.at[0], 2, a_hi)),
+        (None, remote(az_send.at[0], az_recv.at[1], 3, a_lo)),
+        (has_x_hi, remote(x_send.at[1], x_recv.at[0, pl.ds(0, n_kx)], 4, x_hi)),
+        (has_x_lo, remote(x_send.at[0], x_recv.at[1, pl.ds(0, n_kx)], 5, x_lo)),
+    ]
+    recvs = [
+        (has_r_lo, remote(e.at[:, :, pl.ds(rows, 2)], e.at[:, :, pl.ds(0, 2)], 0, r_lo)),
+        (has_r_hi, remote(e.at[:, :, pl.ds(2, 2)], e.at[:, :, pl.ds(rows + 2, 2)], 1, r_hi)),
+        (None, remote(az_send.at[1], az_recv.at[0], 2, a_lo)),
+        (None, remote(az_send.at[0], az_recv.at[1], 3, a_hi)),
+        (has_x_lo, remote(x_send.at[1], x_recv.at[0, pl.ds(0, n_kx)], 4, x_lo)),
+        (has_x_hi, remote(x_send.at[0], x_recv.at[1, pl.ds(0, n_kx)], 5, x_hi)),
+    ]
+
+    def when(cond, fn):
+        if cond is None:
+            fn()
+        else:
+            pl.when(cond)(fn)
+
+    for cond, c in sends:
+        when(cond, c.start)
+
+    @pl.when(jnp.logical_not(has_r_lo))
+    def _():
+        e[:, :, 0:2] = jnp.zeros((2, fields, 2, n_a, n_x), jnp.float32)
+
+    @pl.when(jnp.logical_not(has_r_hi))
+    def _():
+        e[:, :, rows + 2:rows + 4] = jnp.zeros((2, fields, 2, n_a, n_x), jnp.float32)
+
+    @pl.when(jnp.logical_not(has_x_lo))
+    def _():
+        x_recv[0, 0:n_kx, :] = jnp.zeros((n_kx, x_recv.shape[2]), jnp.float32)
+
+    @pl.when(jnp.logical_not(has_x_hi))
+    def _():
+        x_recv[1, 0:n_kx, :] = jnp.zeros((n_kx, x_recv.shape[2]), jnp.float32)
+
+    for cond, c in recvs:
+        when(cond, c.wait_recv)
+
+    for side in range(2):
+        xt[side] = x_recv[side].T
+        for k in range(2):
+            for f in range(fields):
+                for r in range(rows):
+                    row = ((k * fields + f) * rows + r) * 2
+                    az_exp[side, r, k * fields + f, 0:2, :] = az_recv[side, row:row + 2, :]
+
     sub = lax.broadcasted_iota(jnp.int32, (n_a, n_x), 0)
     lane = lax.broadcasted_iota(jnp.int32, (n_a, n_x), 1)
 
@@ -165,43 +256,45 @@
                         jnp.where(sub == n_a - 2, jnp.broadcast_to(hi[0:1], u.shape), pltpu.roll(u, n_a - 2, 0)))
         return um2, um1, u, up1, up2
 
-    def shifted_ax(u, lo, hi):
-        um1 = jnp.where(lane == 0, jnp.broadcast_to(lo[:, 1:2], u.shape), pltpu.roll(u, 1, 1))
-        um2 = jnp.where(lane == 0, jnp.broadcast_to(lo[:, 0:1], u.shape),
-                        jnp.where(lane == 1, jnp.broadcast_to(lo[:, 1:2], u.shape), pltpu.roll(u, 2, 1)))
-        up1 = jnp.where(lane == n_x - 1, jnp.broadcast_to(hi[:, 0:1], u.shape), pltpu.roll(u, n_x - 1, 1))
-        up2 = jnp.where(lane == n_x - 1, jnp.broadcast_to(hi[:, 1:2], u.shape),
-                        jnp.where(lane == n_x - 2, jnp.broadcast_to(hi[:, 0:1], u.shape), pltpu.roll(u, n_x - 2, 1)))
+    def shifted_ax(u, lo0, lo1, hi0, hi1):
+        um1 = jnp.where(lane == 0, jnp.broadcast_to(lo1, u.shape), pltpu.roll(u, 1, 1))
+        um2 = jnp.where(lane == 0, jnp.broadcast_to(lo0, u.shape),
+                        jnp.where(lane == 1, jnp.broadcast_to(lo1, u.shape), pltpu.roll(u, 2, 1)))
+        up1 = jnp.where(lane == n_x - 1, jnp.broadcast_to(hi0, u.shape), pltpu.roll(u, n_x - 1, 1))
+        up2 = jnp.where(lane == n_x - 1, jnp.broadcast_to(hi1, u.shape),
+                        jnp.where(lane == n_x - 2, jnp.broadcast_to(hi0, u.shape), pltpu.roll(u, n_x - 2, 1)))
         return um2, um1, u, up1, up2
 
-    def row(r, carry):
-        balance = None
-        weight = None
-        lo_s, hi_s = [], []
-        w = []
+    def row_body(r, carry):
+        base = pl.multiple_of(r * n_a, n_a)
+        xlo = xt[0, pl.ds(base, n_a), :]
+        xhi = xt[1, pl.ds(base, n_a), :]
+        lo_s, hi_s, w = [], [], []
         for f in range(fields):
-            e = [ep[f, r + k] for k in range(5)]
-            lo, hi = faces(*e)
+            lo, hi = faces(*[e[0, f, r + k] for k in range(5)])
             lo_s.append(lo)
             hi_s.append(hi)
-            w.append(fourth(*[ea[f, r + k] for k in range(5)]))
+            w.append(fourth(*[e[1, f, r + k] for k in range(5)]))
         balance = flux_pair(lo_s, hi_s, 0)
         weight = w
         lo_s, hi_s, w = [], [], []
         for f in range(fields):
-            lo, hi = faces(*shifted_azi(ep[f, r + 2], al[0, f, r], ah[0, f, r]))
+            lo, hi = faces(*shifted_azi(e[0, f, r + 2], az_exp[0, r, f], az_exp[1, r, f]))
             lo_s.append(lo)
             hi_s.append(hi)
-            w.append(fourth(*shifted_azi(ea[f, r + 2], al[1, f, r], ah[1, f, r])))
+            w.append(fourth(*shifted_azi(e[1, f, r + 2], az_exp[0, r, fields + f], az_exp[1, r, fields + f])))
         part = flux_pair(lo_s, hi_s, 1)
         balance = [b + p for b, p in zip(balance, part)]
         weight = [a + b for a, b in zip(weight, w)]
         lo_s, hi_s, w = [], [], []
         for f in range(fields):
-            lo, hi = faces(*shifted_ax(ep[f, r + 2], xl[0, f, r], xh[0, f, r]))
+            cp, ca = 2 * f, 2 * (fields + f)
+            lo, hi = faces(*shifted_ax(e[0, f, r + 2], xlo[:, cp:cp + 1], xlo[:, cp + 1:cp + 2],
+                                       xhi[:, cp:cp + 1], xhi[:, cp + 1:cp + 2]))
             lo_s.append(lo)
             hi_s.append(hi)
-            w.append(fourth(*shifted_ax(ea[f, r + 2], xl[1, f, r], xh[1, f, r])))
+            w.append(fourth(*shifted_ax(e[1, f, r + 2], xlo[:, ca:ca + 1], xlo[:, ca + 1:ca + 2],
+                                        xhi[:, ca:ca + 1], xhi[:, ca + 1:ca + 2])))
         part = flux_pair(lo_s, hi_s, 2)
         balance = [b + p for b, p in zip(balance, part)]
         weight = [a + b for a, b in zip(weight, w)]
@@ -211,36 +304,40 @@
         out_ref[r] = jnp.abs(total)
         return carry
 
-    lax.fori_loop(0, rows, row, 0)
-
-
-def stencil(primal, adjoint, rl, rh, al, ah, xl, xh):
+    lax.fori_loop(0, rows, row_body, 0)
+
+    for cond, c in sends:
+        when(cond, c.wait_send)
+
+
+def stencil(primal, adjoint):
     fields, rows, n_a, n_x = primal.shape
-    vmem = pl.BlockSpec(memory_space=pltpu.VMEM)
     anywhere = pl.BlockSpec(memory_space=pl.ANY)
     return pl.pallas_call(
         stencil_kernel,
         out_shape=jax.ShapeDtypeStruct((rows, n_a, n_x), jnp.float32),
-        in_specs=[anywhere, anywhere] + [vmem] * 6,
-        out_specs=vmem,
+        in_specs=[anywhere, anywhere],
+        out_specs=pl.BlockSpec(memory_space=pltpu.VMEM),
         scratch_shapes=[
-            pltpu.VMEM((fields, rows + 4, n_a, n_x), jnp.float32),
-            pltpu.VMEM((fields, rows + 4, n_a, n_x), jnp.float32),
+            pltpu.VMEM((2, fields, rows + 4, n_a, n_x), jnp.float32),
+            pltpu.VMEM((2, 2 * fields * rows * 2, n_x), jnp.float32),
+            pltpu.VMEM((2, 2 * fields * rows * 2, n_x), jnp.float32),
+            pltpu.VMEM((2, rows, 2 * fields, 8, n_x), jnp.float32),
+            pltpu.VMEM((2, -(-4 * fields // 8) * 8, rows * n_a), jnp.float32),
+            pltpu.VMEM((2, 128, rows * n_a), jnp.float32),
+            pltpu.VMEM((2, rows * n_a, 128), jnp.float32),
             pltpu.SemaphoreType.DMA((2,)),
+            pltpu.SemaphoreType.DMA((6,)),
+            pltpu.SemaphoreType.DMA((6,)),
         ],
-        compiler_params=pltpu.CompilerParams(vmem_limit_bytes=48 * 1024 * 1024),
-    )(primal, adjoint, rl, rh, al, ah, xl, xh)
+        compiler_params=pltpu.CompilerParams(
+            collective_id=2, has_side_effects=True, vmem_limit_bytes=48 * 1024 * 1024
+        ),
+    )(primal, adjoint)
 
 
 def on_device(primal, adjoint, refine_flag, owner_map, migrate_weight, neighbor_list):
-    both = jnp.stack([primal, adjoint])
-    rl, rh = exchange(both[:, :, -2:], both[:, :, :2], "rad", False)
-    al, ah = exchange(both[:, :, :, -2:], both[:, :, :, :2], "azi", True)
-    xl, xh = exchange(
-        jnp.swapaxes(both[..., -2:], -1, -2), jnp.swapaxes(both[..., :2], -1, -2), "ax", False
-    )
-    xl, xh = jnp.swapaxes(xl, -1, -2), jnp.swapaxes(xh, -1, -2)
-    indicator = stencil(primal, adjoint, rl, rh, al, ah, xl, xh)
+    indicator = stencil(primal, adjoint)
     rows_rad, rows_azi, rows_ax = indicator.shape
     per_rad = rows_rad // BLK
     per_azi = rows_azi // BLK

time: 103 us -> 73.8 us (0.72)
  local copies, waits for them, and re-layouts: 21.1 us -> 6.65 us
  starting transfers between devices: 12.6 us -> 0 us
  other arithmetic: 11 us -> 2.6 us
  Pallas kernels: 55.5 us -> 61.8 us
    ppermute x6 -> x0, starting transfers between devices: 12.6 us -> none  [the longest x3 10 us: exchange(): low = lax.ppermute(dense(tail), axis, forward).reshape(tail.shape)]
    reshape x6 -> x0, local copies, waits for them, and re-layouts: 10.4 us -> none  [the longest x2 4.66 us: exchange(): high = lax.ppermute(dense(head), axis, backward).reshape(head.shape)]
    pallas_call x1, Pallas kernels: 12.1 us -> 21.5 us  [stencil(): pl.pallas_call(stencil_kernel, out_shape=jax.ShapeDtypeStruct((rows, n_a,...]
    transpose x1 -> x0, other arithmetic: 5.68 us -> none  [on_device(): jnp.swapaxes(both[..., :2], -1, -2)]
    transpose x2 -> x0, local copies, waits for them, and re-layouts: 5.61 us -> none  [the longest x1 3.03 us: on_device(): jnp.swapaxes(both[..., :2], -1, -2)]
    pallas_call x2, Pallas kernels: 43.4 us -> 40.3 us  [gather_all(): pl.pallas_call(functools.partial(gather_kernel, (n_r, n_a, n_x)), out_sha...]
    slice x2 -> x0, other arithmetic: 1.8 us -> none  [the longest x1 0.94 us: on_device(): rl, rh = exchange(both[:, :, -2:], both[:, :, :2], 'rad', False)]
    unnamed x17 -> x16, local copies, waits for them, and re-layouts: 1.85 us -> 3.45 us
  transfers between devices with their start and end apart: 6 -> 0, of which waited for: 0 -> 0; matrix products, arithmetic and copies ran while one was open for 14% -> 0% of each run, Pallas kernels for 0% -> 0%
where the time goes in v3:
time: 73.8 us; the launch traced here: 73.6 us
  Pallas kernels  61.8 us (84%)
  local copies, waits for them, and re-layouts  6.65 us (9%)
  other arithmetic  2.6 us (4%)
  between operations  2.54 us (3%)
    pallas_call x2, Pallas kernels, gather_all(): pl.pallas_call(functools.partial(gather_kernel, (n_r, n_a, n_x)), out_sha...  40.3 us
    pallas_call x1, Pallas kernels, stencil(): pl.pallas_call(stencil_kernel, out_shape=jax.ShapeDtypeStruct((rows, n_a,...  21.5 us
    unnamed x16, local copies, waits for them, and re-layouts  3.45 us
    reduce_sum x1, other arithmetic, on_device(): jnp.sum(jnp.where(owner_all == own_index.astype(jnp.float32), cost_all, 0...  1.69 us

profile of v3, /device:TPU:1, one launch (start us, length us, event | category | flops | bytes accessed | tf_op | source)
XLA Modules:
  0.0 73.6 jit_solution(10824498565188354827)
XLA Ops:
  0.6 0.0 copy-start
  0.6 1.3 %copy-done = f32[5,16,32,128]{3,2,1,0:T(8,128)S(1)} copy-done((f32[5,16,32,128]{3,2,1,0:T(8,128)S(1)}, f32[5,16,32,128]{3,2,1,0:T(8,128)}, u32[]{:S(2)}) %copy-start) | copy-done | bytes 1310744
  2.0 0.0 copy-start.1
  2.0 1.3 %copy-done.1 = f32[5,16,32,128]{3,2,1,0:T(8,128)S(1)} copy-done((f32[5,16,32,128]{3,2,1,0:T(8,128)S(1)}, f32[5,16,32,128]{3,2,1,0:T(8,128)}, u32[]{:S(2)}) %copy-start.1) | copy-done | bytes 1310744
  3.3 0.0 copy-start.2
  3.3 21.5 %shard_map.85 = f32[16,32,128]{2,1,0:T(8,128)S(1)} custom-call(f32[5,16,32,128]{3,2,1,0:T(8,128)S(1)} %copy-done, f32[5,16,32,128]{3,2,1,0:T(8,128)S(1)} %copy-done.1), custom_call_target="tpu_custom_call" | custom-call | tf_op jit(solution)/shard_map/pallas_call | solution.py:316
  24.8 0.1 reduce_sum.35
  24.9 0.1 reduce_sum.36
  25.0 0.6 div.67.x_ref
  25.6 23.2 %shard_map.86 = f32[8,8,4,16]{3,2,1,0:T(4,128)} custom-call(f32[1,1,1,16]{3,2,1,0:T(1,128)} %div.67.x_ref), custom_call_target="tpu_custom_call" | custom-call | tf_op jit(solution)/shard_map/pallas_call | solution.py:85
  48.8 1.0 %reshape.80 = f32[4096]{0:T(1024)S(1)} reshape(f32[8,8,4,16]{3,2,1,0:T(4,128)} %shard_map.86) | data formatting | bytes 32768 | tf_op jit(solution)/shard_map/reshape | solution.py:97
  49.9 0.0 copy-done.2
  49.9 0.1 copy.17
  50.0 0.1 reshape.86
  50.1 0.0 copy-start.3
  50.1 0.0 copy-start.4
  50.1 0.0 copy-start.5
  50.2 1.1 %gather_fusion = f32[96]{0:T(128)S(1)} fusion(f32[4096]{0:T(1024)S(1)} %reshape.80, s32[1024]{0:T(1024)S(1)} %pad_clamp_fusion), kind=kCustom, calls=%fused_computation | custom fusion | bytes 1152 | tf_op jit(solution)/shard_map/jit(_take)/gather | solution.py:360
  51.3 0.1 reshape.85
  51.4 0.1 select_reduce_fusion
  51.5 0.0 copy-done.3
  51.5 0.0 copy-done.4
  51.5 0.0 copy-done.5
  51.5 0.0 copy-start.6
  51.6 0.1 reshape.81
  51.6 0.1 convert_element_type.19
  51.7 0.6 maximum_bitcast_fusion.x_ref
  52.3 17.1 %shard_map.87 = f32[8,8,4,32]{3,2,1,0:T(4,128)} custom-call(f32[1,1,1,32]{3,2,1,0:T(1,128)} %maximum_bitcast_fusion.x_ref), custom_call_target="tpu_custom_call" | custom-call | tf_op jit(solution)/shard_map/pallas_call | solution.py:85
  69.4 1.7 %fusion = f32[]{:T(128)} fusion(f32[256,32]{1,0:T(8,128)} %bitcast.10, f32[]{:T(128)S(6)} %convert_element_type.20), kind=kLoop, calls=%fused_computation.2 | loop fusion | flops 12287 | bytes 32776 | tf_op jit(solution)/shard_map/reduce_sum | solution.py:375
  71.7 0.7 copy.22
  72.4 0.0 copy-done.6
  (6 shorter events, 0.1 us)
Async XLA Ops:
  0.6 1.3 %copy-start = (f32[5,16,32,128]{3,2,1,0:T(8,128)S(1)}, f32[5,16,32,128]{3,2,1,0:T(8,128)}, u32[]{:S(2)}) copy-start(f32[5,16,32,128]{3,2,1,0:T(8,128)} %p_hbm.1) | copy-start | bytes 3932164
  2.0 1.3 %copy-start.1 = (f32[5,16,32,128]{3,2,1,0:T(8,128)S(1)}, f32[5,16,32,128]{3,2,1,0:T(8,128)}, u32[]{:S(2)}) copy-start(f32[5,16,32,128]{3,2,1,0:T(8,128)} %a_hbm.1) | copy-start | bytes 3932164
  3.3 46.6 %copy-start.2 = (s32[1,2,8,6]{2,1,3,0:T(2,128)S(1)}, s32[1,2,8,6]{2,1,3,0:T(2,128)}, u32[]{:S(2)}) copy-start(s32[1,2,8,6]{2,1,3,0:T(2,128)} %param.11) | copy-start | bytes 1156
  50.1 1.4 %copy-start.3 = (s32[1,2,8]{2,1,0:T(2,128)S(1)}, s32[1,2,8]{2,1,0:T(2,128)}, u32[]{:S(2)}) copy-start(s32[1,2,8]{2,1,0:T(2,128)} %param.9) | copy-start | bytes 196
  50.1 1.4 %copy-start.4 = (s32[1,2,8]{2,1,0:T(2,128)S(1)}, s32[1,2,8]{2,1,0:T(2,128)}, u32[]{:S(2)}) copy-start(s32[1,2,8]{2,1,0:T(2,128)} %param.10) | copy-start | bytes 196
  50.1 1.4 %copy-start.5 = (s32[1,2,8]{2,1,0:T(2,128)S(1)}, s32[1,2,8]{2,1,0:T(2,128)}, u32[]{:S(2)}) copy-start(s32[1,2,8]{2,1,0:T(2,128)} %param.8) | copy-start | bytes 196
  51.5 20.9 %copy-start.6 = (f32[1,2,8]{2,1,0:T(2,128)}, f32[1,2,8]{2,1,0:T(2,128)S(1)}, u32[]{:S(2)}) copy-start(f32[1,2,8]{2,1,0:T(2,128)S(1)} %fusion.21) | copy-start | bytes 196

commit v4 on v3

--- a/solution.py
+++ b/solution.py
@@ -25,13 +25,6 @@
         (n_a, lambda k: at(r, lax.rem(a + k, n_a), x), lambda k: at(r, lax.rem(a + n_a - k, n_a), x)),
         (n_r, lambda k: at(lax.rem(r + k, n_r), a, x), lambda k: at(lax.rem(r + n_r - k, n_r), a, x)),
     ]
-    barrier = pltpu.get_barrier_semaphore()
-    count = 0
-    for n, to, _ in stages:
-        for k in range(1, n):
-            pl.semaphore_signal(barrier, 1, device_id=to(k), device_id_type=MESH)
-            count += 1
-    pl.semaphore_wait(barrier, count)
 
     def region(stage, dev):
         rr, aa, xx = dev
@@ -92,7 +85,7 @@
             pltpu.SemaphoreType.DMA((links,)),
             pltpu.SemaphoreType.DMA((links,)),
         ],
-        compiler_params=pltpu.CompilerParams(collective_id=cid, has_side_effects=True),
+        compiler_params=pltpu.CompilerParams(has_side_effects=True),
     )(values.reshape(1, 1, 1, width))
     return out.reshape(-1)
 

time: 73.8 us -> 91 us (1.23)
  Pallas kernels: 61.8 us -> 79 us
    pallas_call x2, Pallas kernels: 40.3 us -> 57.5 us  [gather_all(): pl.pallas_call(functools.partial(gather_kernel, (n_r, n_a, n_x)), out_sha...]
where the time goes in v4:
time: 91 us; the launch traced here: 90.7 us
  Pallas kernels  79 us (87%)
  local copies, waits for them, and re-layouts  6.65 us (7%)
  other arithmetic  2.6 us (3%)
  between operations  2.54 us (3%)
    pallas_call x2, Pallas kernels, gather_all(): pl.pallas_call(functools.partial(gather_kernel, (n_r, n_a, n_x)), out_sha...  57.5 us
    pallas_call x1, Pallas kernels, stencil(): pl.pallas_call(stencil_kernel, out_shape=jax.ShapeDtypeStruct((rows, n_a,...  21.5 us
    unnamed x16, local copies, waits for them, and re-layouts  3.45 us

profile of v4, /device:TPU:1, one launch (start us, length us, event | category | flops | bytes accessed | tf_op | source)
XLA Modules:
  0.0 90.7 jit_solution(3081298811784838970)
XLA Ops:
  0.6 0.0 copy-start
  0.6 1.3 %copy-done = f32[5,16,32,128]{3,2,1,0:T(8,128)S(1)} copy-done((f32[5,16,32,128]{3,2,1,0:T(8,128)S(1)}, f32[5,16,32,128]{3,2,1,0:T(8,128)}, u32[]{:S(2)}) %copy-start) | copy-done | bytes 1310744
  2.0 0.0 copy-start.1
  2.0 1.3 %copy-done.1 = f32[5,16,32,128]{3,2,1,0:T(8,128)S(1)} copy-done((f32[5,16,32,128]{3,2,1,0:T(8,128)S(1)}, f32[5,16,32,128]{3,2,1,0:T(8,128)}, u32[]{:S(2)}) %copy-start.1) | copy-done | bytes 1310744
  3.3 0.0 copy-start.2
  3.3 21.5 %shard_map.85 = f32[16,32,128]{2,1,0:T(8,128)S(1)} custom-call(f32[5,16,32,128]{3,2,1,0:T(8,128)S(1)} %copy-done, f32[5,16,32,128]{3,2,1,0:T(8,128)S(1)} %copy-done.1), custom_call_target="tpu_custom_call" | custom-call | tf_op jit(solution)/shard_map/pallas_call | solution.py:309
  24.8 0.1 reduce_sum.35
  24.9 0.1 reduce_sum.36
  25.0 0.6 div.67.x_ref
  25.6 33.8 %shard_map.86 = f32[8,8,4,16]{3,2,1,0:T(4,128)} custom-call(f32[1,1,1,16]{3,2,1,0:T(1,128)} %div.67.x_ref), custom_call_target="tpu_custom_call" | custom-call | tf_op jit(solution)/shard_map/pallas_call | solution.py:78
  59.4 1.0 %reshape.80 = f32[4096]{0:T(1024)S(1)} reshape(f32[8,8,4,16]{3,2,1,0:T(4,128)} %shard_map.86) | data formatting | bytes 32768 | tf_op jit(solution)/shard_map/reshape | solution.py:90
  60.5 0.0 copy-done.2
  60.5 0.1 copy.17
  60.6 0.1 reshape.86
  60.7 0.0 copy-start.3
  60.7 0.0 copy-start.4
  60.7 0.0 copy-start.5
  60.7 1.1 %gather_fusion = f32[96]{0:T(128)S(1)} fusion(f32[4096]{0:T(1024)S(1)} %reshape.80, s32[1024]{0:T(1024)S(1)} %pad_clamp_fusion), kind=kCustom, calls=%fused_computation | custom fusion | bytes 1152 | tf_op jit(solution)/shard_map/jit(_take)/gather | solution.py:353
  61.9 0.1 reshape.85
  62.0 0.1 select_reduce_fusion
  62.1 0.0 copy-done.3
  62.1 0.0 copy-done.4
  62.1 0.0 copy-done.5
  62.1 0.0 copy-start.6
  62.1 0.1 reshape.81
  62.2 0.1 convert_element_type.19
  62.3 0.6 maximum_bitcast_fusion.x_ref
  62.9 23.6 %shard_map.87 = f32[8,8,4,32]{3,2,1,0:T(4,128)} custom-call(f32[1,1,1,32]{3,2,1,0:T(1,128)} %maximum_bitcast_fusion.x_ref), custom_call_target="tpu_custom_call" | custom-call | tf_op jit(solution)/shard_map/pallas_call | solution.py:78
  86.6 1.7 %fusion = f32[]{:T(128)} fusion(f32[256,32]{1,0:T(8,128)} %bitcast.10, f32[]{:T(128)S(6)} %convert_element_type.20), kind=kLoop, calls=%fused_computation.2 | loop fusion | flops 12287 | bytes 32776 | tf_op jit(solution)/shard_map/reduce_sum | solution.py:368
  88.9 0.7 copy.22
  89.6 0.0 copy-done.6
  (6 shorter events, 0.1 us)
Async XLA Ops:
  0.6 1.3 %copy-start = (f32[5,16,32,128]{3,2,1,0:T(8,128)S(1)}, f32[5,16,32,128]{3,2,1,0:T(8,128)}, u32[]{:S(2)}) copy-start(f32[5,16,32,128]{3,2,1,0:T(8,128)} %p_hbm.1) | copy-start | bytes 3932164
  2.0 1.3 %copy-start.1 = (f32[5,16,32,128]{3,2,1,0:T(8,128)S(1)}, f32[5,16,32,128]{3,2,1,0:T(8,128)}, u32[]{:S(2)}) copy-start(f32[5,16,32,128]{3,2,1,0:T(8,128)} %a_hbm.1) | copy-start | bytes 3932164
  3.3 57.2 %copy-start.2 = (s32[1,2,8,6]{2,1,3,0:T(2,128)S(1)}, s32[1,2,8,6]{2,1,3,0:T(2,128)}, u32[]{:S(2)}) copy-start(s32[1,2,8,6]{2,1,3,0:T(2,128)} %param.11) | copy-start | bytes 1156
  60.7 1.4 %copy-start.3 = (s32[1,2,8]{2,1,0:T(2,128)S(1)}, s32[1,2,8]{2,1,0:T(2,128)}, u32[]{:S(2)}) copy-start(s32[1,2,8]{2,1,0:T(2,128)} %param.9) | copy-start | bytes 196
  60.7 1.4 %copy-start.4 = (s32[1,2,8]{2,1,0:T(2,128)S(1)}, s32[1,2,8]{2,1,0:T(2,128)}, u32[]{:S(2)}) copy-start(s32[1,2,8]{2,1,0:T(2,128)} %param.10) | copy-start | bytes 196
  60.7 1.4 %copy-start.5 = (s32[1,2,8]{2,1,0:T(2,128)S(1)}, s32[1,2,8]{2,1,0:T(2,128)}, u32[]{:S(2)}) copy-start(s32[1,2,8]{2,1,0:T(2,128)} %param.8) | copy-start | bytes 196
  62.1 27.5 %copy-start.6 = (f32[1,2,8]{2,1,0:T(2,128)}, f32[1,2,8]{2,1,0:T(2,128)S(1)}, u32[]{:S(2)}) copy-start(f32[1,2,8]{2,1,0:T(2,128)S(1)} %fusion.21) | copy-start | bytes 196

commit v5 on v4

--- a/solution.py
+++ b/solution.py
@@ -11,83 +11,165 @@
 MESH = pl.DeviceIdType.MESH
 
 
-def gather_kernel(sizes, x_ref, o_ref, lsem, ssem, rsem):
+def gather_stages(sizes, pairs, local_sem, ssem, rsem):
     n_r, n_a, n_x = sizes
     r = lax.axis_index("rad")
     a = lax.axis_index("azi")
     x = lax.axis_index("ax")
-
-    def at(rr, aa, xx):
-        return (rr, aa, xx)
-
     stages = [
-        (n_x, lambda k: at(r, a, lax.rem(x + k, n_x)), lambda k: at(r, a, lax.rem(x + n_x - k, n_x))),
-        (n_a, lambda k: at(r, lax.rem(a + k, n_a), x), lambda k: at(r, lax.rem(a + n_a - k, n_a), x)),
-        (n_r, lambda k: at(lax.rem(r + k, n_r), a, x), lambda k: at(lax.rem(r + n_r - k, n_r), a, x)),
+        (n_x, lambda k: (r, a, lax.rem(x + k, n_x)), lambda k: (r, a, lax.rem(x + n_x - k, n_x))),
+        (n_a, lambda k: (r, lax.rem(a + k, n_a), x), lambda k: (r, lax.rem(a + n_a - k, n_a), x)),
+        (n_r, lambda k: (lax.rem(r + k, n_r), a, x), lambda k: (lax.rem(r + n_r - k, n_r), a, x)),
     ]
 
-    def region(stage, dev):
+    def region(dst, stage, dev):
         rr, aa, xx = dev
         if stage == 0:
-            return o_ref.at[pl.ds(rr, 1), pl.ds(aa, 1), pl.ds(xx, 1)]
+            return dst.at[pl.ds(rr, 1), pl.ds(aa, 1), pl.ds(xx, 1)]
         if stage == 1:
-            return o_ref.at[pl.ds(rr, 1), pl.ds(aa, 1)]
-        return o_ref.at[pl.ds(rr, 1)]
-
-    local = pltpu.make_async_copy(x_ref, region(0, (r, a, x)), lsem)
-    local.start()
+            return dst.at[pl.ds(rr, 1), pl.ds(aa, 1)]
+        return dst.at[pl.ds(rr, 1)]
+
+    locals_ = []
+    for i, (src, dst) in enumerate(pairs):
+        c = pltpu.make_async_copy(src, region(dst, 0, (r, a, x)), local_sem.at[i])
+        c.start()
+        locals_.append(c)
     sends = []
     slot = 0
     for stage, (n, to, frm) in enumerate(stages):
-        src = x_ref if stage == 0 else region(stage, (r, a, x))
         first = slot
-        for k in range(1, n):
-            copy = pltpu.make_async_remote_copy(
-                src_ref=src,
-                dst_ref=region(stage, (r, a, x)),
-                send_sem=ssem.at[slot],
-                recv_sem=rsem.at[slot],
-                device_id=to(k),
-                device_id_type=MESH,
-            )
-            copy.start()
-            sends.append(copy)
-            slot += 1
+        for src, dst in pairs:
+            s = src if stage == 0 else region(dst, stage, (r, a, x))
+            for k in range(1, n):
+                copy = pltpu.make_async_remote_copy(
+                    src_ref=s, dst_ref=region(dst, stage, (r, a, x)),
+                    send_sem=ssem.at[slot], recv_sem=rsem.at[slot],
+                    device_id=to(k), device_id_type=MESH,
+                )
+                copy.start()
+                sends.append(copy)
+                slot += 1
         slot = first
-        for k in range(1, n):
-            incoming = pltpu.make_async_remote_copy(
-                src_ref=src,
-                dst_ref=region(stage, frm(k)),
-                send_sem=ssem.at[slot],
-                recv_sem=rsem.at[slot],
-                device_id=frm(k),
-                device_id_type=MESH,
-            )
-            incoming.wait_recv()
-            slot += 1
+        for src, dst in pairs:
+            s = src if stage == 0 else region(dst, stage, (r, a, x))
+            for k in range(1, n):
+                incoming = pltpu.make_async_remote_copy(
+                    src_ref=s, dst_ref=region(dst, stage, frm(k)),
+                    send_sem=ssem.at[slot], recv_sem=rsem.at[slot],
+                    device_id=frm(k), device_id_type=MESH,
+                )
+                incoming.wait_recv()
+                slot += 1
         if stage == 0:
-            local.wait()
-    for copy in sends:
-        copy.wait_send()
-
-
-def gather_all(values, cid):
-    n_r, n_a, n_x = (lax.axis_size(ax) for ax in AXES)
-    width = values.shape[0]
-    links = (n_r - 1) + (n_a - 1) + (n_x - 1)
-    out = pl.pallas_call(
-        functools.partial(gather_kernel, (n_r, n_a, n_x)),
-        out_shape=jax.ShapeDtypeStruct((n_r, n_a, n_x, width), jnp.float32),
-        in_specs=[pl.BlockSpec(memory_space=pltpu.VMEM)],
-        out_specs=pl.BlockSpec(memory_space=pltpu.VMEM),
+            for c in locals_:
+                c.wait()
+    return sends
+
+
+def peer_barrier(sizes):
+    n_r, n_a, n_x = sizes
+    r = lax.axis_index("rad")
+    a = lax.axis_index("azi")
+    x = lax.axis_index("ax")
+    barrier = pltpu.get_barrier_semaphore()
+    count = 0
+    for k in range(1, n_x):
+        pl.semaphore_signal(barrier, 1, device_id=(r, a, lax.rem(x + k, n_x)), device_id_type=MESH)
+        count += 1
+    for k in range(1, n_a):
+        pl.semaphore_signal(barrier, 1, device_id=(r, lax.rem(a + k, n_a), x), device_id_type=MESH)
+        count += 1
+    for k in range(1, n_r):
+        pl.semaphore_signal(barrier, 1, device_id=(lax.rem(r + k, n_r), a, x), device_id_type=MESH)
+        count += 1
+    pl.semaphore_wait(barrier, count)
+
+
+def post_kernel(sizes, blocks, bm_ref, nl_ref, rf_ref, mw_ref, ow_ref, cost_out, load_out,
+                g_mean, g_mean_s, sums_s, sums_v, pay_c, pay_o, g_cost, g_own, lsem, ssem, rsem):
+    n_r, n_a, n_x = sizes
+    per_rad, per_azi, per_ax = blocks
+    n_links = (n_r - 1) + (n_a - 1) + (n_x - 1)
+    peer_barrier(sizes)
+    sends = gather_stages(sizes, [(bm_ref, g_mean)], lsem.at[0:1], ssem.at[0:n_links], rsem.at[0:n_links])
+    to_smem = pltpu.make_async_copy(g_mean, g_mean_s, lsem.at[1])
+    to_smem.start()
+    to_smem.wait()
+    blocks_azi = per_azi * n_a
+    blocks_ax = per_ax * n_x
+    width = per_rad * per_azi * per_ax
+    for b in range(width):
+        total = None
+        for k in range(6):
+            v = nl_ref[b * 6 + k]
+            br = v // (blocks_azi * blocks_ax)
+            ba = v // blocks_ax % blocks_azi
+            bx = v % blocks_ax
+            local = (br % per_rad * per_azi + ba % per_azi) * per_ax + bx % per_ax
+            val = g_mean_s[br // per_rad, ba // per_azi, bx // per_ax, local]
+            total = val if total is None else total + val
+        sums_s[0, b] = total
+    to_vmem = pltpu.make_async_copy(sums_s, sums_v, lsem.at[2])
+    to_vmem.start()
+    to_vmem.wait()
+    me = (lax.axis_index("rad") * n_a + lax.axis_index("azi")) * n_x + lax.axis_index("ax")
+    me_f = me.astype(jnp.float32)
+    bm = bm_ref[0, 0]
+    owner = ow_ref[...]
+    smooth = 0.5 * bm + 0.5 * (sums_v[...] / 6.0)
+    moved = jnp.where(owner != me_f, 1.0, 0.0)
+    cost = smooth * (1.0 + 7.0 * rf_ref[...]) + 0.25 * mw_ref[...] * moved
+    cost_out[...] = cost
+    pay_c[0, 0] = cost
+    pay_o[0, 0] = owner
+    sends += gather_stages(
+        sizes, [(pay_c, g_cost), (pay_o, g_own)], lsem.at[3:5],
+        ssem.at[n_links:3 * n_links], rsem.at[n_links:3 * n_links],
+    )
+    costs = g_cost[...]
+    owners = g_own[...]
+    picked = jnp.where(owners == me_f, costs, 0.0)
+    part = jnp.sum(picked, axis=(0, 1))
+    total = jnp.sum(part, axis=0, keepdims=True)
+    total = jnp.sum(total, axis=1, keepdims=True)
+    load_out[...] = (total / float(width)).reshape(1, 1, 1)
+    for c in sends:
+        c.wait_send()
+
+
+def post(block_mean, neighbor_list, refine_flag, migrate_weight, owner_map, blocks):
+    sizes = tuple(lax.axis_size(ax) for ax in AXES)
+    n_r, n_a, n_x = sizes
+    width = block_mean.size
+    n_links = (n_r - 1) + (n_a - 1) + (n_x - 1)
+    vmem = pl.BlockSpec(memory_space=pltpu.VMEM)
+    smem = pl.BlockSpec(memory_space=pltpu.SMEM)
+    row = lambda v: v.reshape(1, width).astype(jnp.float32)
+    cost, load = pl.pallas_call(
+        functools.partial(post_kernel, sizes, blocks),
+        out_shape=(jax.ShapeDtypeStruct((1, width), jnp.float32), jax.ShapeDtypeStruct((1, 1, 1), jnp.float32)),
+        in_specs=[vmem, smem, vmem, vmem, vmem],
+        out_specs=(vmem, vmem),
         scratch_shapes=[
-            pltpu.SemaphoreType.DMA(()),
-            pltpu.SemaphoreType.DMA((links,)),
-            pltpu.SemaphoreType.DMA((links,)),
+            pltpu.VMEM((n_r, n_a, n_x, width), jnp.float32),
+            pltpu.SMEM((n_r, n_a, n_x, width), jnp.float32),
+            pltpu.SMEM((1, width), jnp.float32),
+            pltpu.VMEM((1, width), jnp.float32),
+            pltpu.VMEM((1, 1, 1, width), jnp.float32),
+            pltpu.VMEM((1, 1, 1, width), jnp.float32),
+            pltpu.VMEM((n_r, n_a, n_x, width), jnp.float32),
+            pltpu.VMEM((n_r, n_a, n_x, width), jnp.float32),
+            pltpu.SemaphoreType.DMA((5,)),
+            pltpu.SemaphoreType.DMA((3 * n_links,)),
+            pltpu.SemaphoreType.DMA((3 * n_links,)),
         ],
-        compiler_params=pltpu.CompilerParams(has_side_effects=True),
-    )(values.reshape(1, 1, 1, width))
-    return out.reshape(-1)
+        compiler_params=pltpu.CompilerParams(collective_id=0, has_side_effects=True),
+    )(
+        block_mean.reshape(1, 1, 1, width), neighbor_list.reshape(-1),
+        row(refine_flag), row(migrate_weight), row(owner_map),
+    )
+    return cost.reshape(refine_flag.shape), load
 
 
 def dense(x):
@@ -336,37 +418,7 @@
     per_azi = rows_azi // BLK
     per_ax = rows_ax // BLK
     block_mean = indicator.reshape(per_rad, BLK, per_azi, BLK, per_ax, BLK).mean(axis=(1, 3, 5))
-    all_means = gather_all(block_mean.reshape(-1), 0)
-    size_rad = lax.axis_size("rad")
-    size_azi = lax.axis_size("azi")
-    size_ax = lax.axis_size("ax")
-    blocks_azi = per_azi * size_azi
-    blocks_ax = per_ax * size_ax
-    block_rad = neighbor_list // (blocks_azi * blocks_ax)
-    block_azi = neighbor_list // blocks_ax % blocks_azi
-    block_ax = neighbor_list % blocks_ax
-    owner_dev = (
-        block_rad // per_rad * size_azi + block_azi // per_azi
-    ) * size_ax + block_ax // per_ax
-    local_pos = (block_rad % per_rad * per_azi + block_azi % per_azi) * per_ax + block_ax % per_ax
-    position = owner_dev * (per_rad * per_azi * per_ax) + local_pos
-    beside_all = jnp.mean(jnp.take(all_means, position), axis=-1)
-    smooth = 0.5 * block_mean + 0.5 * beside_all
-    own_index = (
-        lax.axis_index("rad") * size_azi + lax.axis_index("azi")
-    ) * size_ax + lax.axis_index("ax")
-    moved = (owner_map != own_index).astype(jnp.float32)
-    block_cost = (
-        smooth * (1.0 + 7.0 * refine_flag.astype(jnp.float32))
-        + 0.25 * migrate_weight.astype(jnp.float32) * moved
-    )
-    width = block_cost.size
-    payload = jnp.concatenate([block_cost.reshape(-1), owner_map.reshape(-1).astype(jnp.float32)])
-    gathered = gather_all(payload, 1).reshape(-1, 2 * width)
-    cost_all = gathered[:, :width]
-    owner_all = gathered[:, width:]
-    total = jnp.sum(jnp.where(owner_all == own_index.astype(jnp.float32), cost_all, 0.0))
-    owner_load = (total / (per_rad * per_azi * per_ax)).reshape(1, 1, 1)
+    block_cost, owner_load = post(block_mean, neighbor_list, refine_flag, migrate_weight, owner_map, (per_rad, per_azi, per_ax))
     return (indicator, block_cost, owner_load)
 
 

time: 91 us -> 78.5 us (0.86)
  Pallas kernels: 79 us -> 66.7 us
  other arithmetic: 2.6 us -> 1.43 us
  local copies, waits for them, and re-layouts: 6.65 us -> 7.73 us
    pallas_call x2 -> x1, Pallas kernels: 57.5 us -> 45 us  [post(): pl.pallas_call(functools.partial(post_kernel, sizes, blocks), out_shape=(...]
    reduce_sum x2 -> x0, other arithmetic: 1.82 us -> none  [the longest x1 1.69 us: on_device(): jnp.sum(jnp.where(owner_all == own_index.astype(jnp.float32), cost_all, 0...]
    convert_element_type x1 -> x3, local copies, waits for them, and re-layouts: 0.08 us -> 1.85 us  [post(): row = lambda v: v.reshape(1, width).astype(jnp.float32)]
    pallas_call x0 -> x1, other arithmetic: none -> 1.29 us  [post(): pl.pallas_call(functools.partial(post_kernel, sizes, blocks), out_shape=(...]
    gather x2 -> x0, local copies, waits for them, and re-layouts: 1.23 us -> none  [on_device(): beside_all = jnp.mean(jnp.take(all_means, position), axis=-1)]
    unnamed x16 -> x14, local copies, waits for them, and re-layouts: 3.45 us -> 3.43 us
where the time goes in v5:
time: 78.5 us; the launch traced here: 78.3 us
  Pallas kernels  66.7 us (85%)
  local copies, waits for them, and re-layouts  7.73 us (10%)
  between operations  2.45 us (3%)
  other arithmetic  1.43 us (2%)
    pallas_call x1, Pallas kernels, post(): pl.pallas_call(functools.partial(post_kernel, sizes, blocks), out_shape=(...  45 us
    pallas_call x1, Pallas kernels, stencil(): pl.pallas_call(stencil_kernel, out_shape=jax.ShapeDtypeStruct((rows, n_a,...  21.6 us
    unnamed x14, local copies, waits for them, and re-layouts  3.43 us
    convert_element_type x3, local copies, waits for them, and re-layouts, post(): row = lambda v: v.reshape(1, width).astype(jnp.float32)  1.85 us

profile of v5, /device:TPU:1, one launch (start us, length us, event | category | flops | bytes accessed | tf_op | source)
XLA Modules:
  0.0 78.3 jit_solution(14701432641626507861)
XLA Ops:
  0.6 0.0 copy-start
  0.6 1.3 %copy-done = f32[5,16,32,128]{3,2,1,0:T(8,128)S(1)} copy-done((f32[5,16,32,128]{3,2,1,0:T(8,128)S(1)}, f32[5,16,32,128]{3,2,1,0:T(8,128)}, u32[]{:S(2)}) %copy-start) | copy-done | bytes 1310744
  1.9 0.0 copy-start.1
  2.0 1.3 %copy-done.1 = f32[5,16,32,128]{3,2,1,0:T(8,128)S(1)} copy-done((f32[5,16,32,128]{3,2,1,0:T(8,128)S(1)}, f32[5,16,32,128]{3,2,1,0:T(8,128)}, u32[]{:S(2)}) %copy-start.1) | copy-done | bytes 1310744
  3.3 0.0 copy-start.2
  3.3 0.0 copy-start.3
  3.3 0.0 copy-start.4
  3.3 0.0 copy-start.5
  3.3 21.6 %shard_map.85 = f32[16,32,128]{2,1,0:T(8,128)S(1)} custom-call(f32[5,16,32,128]{3,2,1,0:T(8,128)S(1)} %copy-done, f32[5,16,32,128]{3,2,1,0:T(8,128)S(1)} %copy-done.1), custom_call_target="tpu_custom_call" | custom-call | tf_op jit(solution)/shard_map/pallas_call | solution.py:391
  25.0 0.1 reduce_sum.14
  25.0 0.1 reduce_sum.18
  25.2 0.6 div.6.bm_ref
  25.8 0.0 copy-done.2
  25.8 0.1 copy.11
  25.8 0.6 reshape.73.nl_ref
  26.5 0.0 copy-done.3
  26.5 0.6 convert_element_type.16.rf_ref
  27.1 0.0 copy-done.4
  27.1 0.7 convert_element_type.18.mw_ref
  27.7 0.0 copy-done.5
  27.7 0.6 convert_element_type.20.ow_ref
  28.3 45.0 %shard_map.86 = (f32[1,16]{1,0:T(1,128)}, f32[1,1,1]{2,1,0:T(1,128)}) custom-call(f32[1,1,1,16]{3,2,1,0:T(1,128)} %div.6.bm_ref, s32[96]{0:T(128)} %reshape.73.nl_ref, f32[1,16]{1,0:T(1,128)} %convert_element_type.16.rf_ref, f32[1,16]{1,0:T(1,128)} %convert_element_type.18.mw_ref, f32[1,16]{1,0:T(1,128)} %convert_element_type.20.ow_ref), custom_call_target="tpu_custom_call" | custom-call | tf_op jit(solution)/shard_map/pallas_call | solution.py:149
  73.4 0.5 broadcast.20
  73.9 1.3 %reduce.6 = f32[16]{0:T(128)S(1)} reduce(f32[1,16]{1,0:T(1,128)} %get-tuple-element.5, f32[]{:T(128)} %broadcast.20), dimensions={0}, to_apply=%get-tuple-element.5.reduce_sub_computation.3 | reduce | bytes 132 | tf_op jit(solution)/shard_map/pallas_call | solution.py:149
  75.2 0.6 reshape.74
  75.8 0.7 copy.14
  (5 shorter events, 0.0 us)
Async XLA Ops:
  0.6 1.3 %copy-start = (f32[5,16,32,128]{3,2,1,0:T(8,128)S(1)}, f32[5,16,32,128]{3,2,1,0:T(8,128)}, u32[]{:S(2)}) copy-start(f32[5,16,32,128]{3,2,1,0:T(8,128)} %p_hbm.1) | copy-start | bytes 3932164
  1.9 1.3 %copy-start.1 = (f32[5,16,32,128]{3,2,1,0:T(8,128)S(1)}, f32[5,16,32,128]{3,2,1,0:T(8,128)}, u32[]{:S(2)}) copy-start(f32[5,16,32,128]{3,2,1,0:T(8,128)} %a_hbm.1) | copy-start | bytes 3932164
  3.3 22.5 %copy-start.2 = (s32[1,2,8,6]{2,1,3,0:T(2,128)S(1)}, s32[1,2,8,6]{2,1,3,0:T(2,128)}, u32[]{:S(2)}) copy-start(s32[1,2,8,6]{2,1,3,0:T(2,128)} %param.11) | copy-start | bytes 1156
  3.3 23.2 %copy-start.3 = (s32[1,2,8]{2,1,0:T(2,128)S(1)}, s32[1,2,8]{2,1,0:T(2,128)}, u32[]{:S(2)}) copy-start(s32[1,2,8]{2,1,0:T(2,128)} %param.8) | copy-start | bytes 196
  3.3 23.8 %copy-start.4 = (s32[1,2,8]{2,1,0:T(2,128)S(1)}, s32[1,2,8]{2,1,0:T(2,128)}, u32[]{:S(2)}) copy-start(s32[1,2,8]{2,1,0:T(2,128)} %param.10) | copy-start | bytes 196
  3.3 24.5 %copy-start.5 = (s32[1,2,8]{2,1,0:T(2,128)S(1)}, s32[1,2,8]{2,1,0:T(2,128)}, u32[]{:S(2)}) copy-start(s32[1,2,8]{2,1,0:T(2,128)} %param.9) | copy-start | bytes 196

commit v6 on v3

--- a/solution.py
+++ b/solution.py
@@ -1,4 +1,5 @@
 import functools
+import itertools
 import jax
 import jax.numpy as jnp
 from jax import lax
@@ -11,87 +12,83 @@
 MESH = pl.DeviceIdType.MESH
 
 
-def gather_kernel(sizes, x_ref, o_ref, lsem, ssem, rsem):
-    n_r, n_a, n_x = sizes
-    r = lax.axis_index("rad")
-    a = lax.axis_index("azi")
-    x = lax.axis_index("ax")
-
-    def at(rr, aa, xx):
-        return (rr, aa, xx)
-
-    stages = [
-        (n_x, lambda k: at(r, a, lax.rem(x + k, n_x)), lambda k: at(r, a, lax.rem(x + n_x - k, n_x))),
-        (n_a, lambda k: at(r, lax.rem(a + k, n_a), x), lambda k: at(r, lax.rem(a + n_a - k, n_a), x)),
-        (n_r, lambda k: at(lax.rem(r + k, n_r), a, x), lambda k: at(lax.rem(r + n_r - k, n_r), a, x)),
-    ]
+def stage_plan(sizes, groups):
+    plan = []
+    for axes in groups:
+        offs = [o for o in itertools.product(*[range(sizes[i]) for i in axes]) if any(o)]
+        plan.append((axes, offs))
+    return plan
+
+
+def gen_gather_kernel(sizes, groups, x_ref, o_ref, lsem, ssem, rsem):
+    me = tuple(lax.axis_index(a) for a in AXES)
+    plan = stage_plan(sizes, groups)
+
+    def shift(off_axes, off, sign):
+        dev = list(me)
+        for i, o in zip(off_axes, off):
+            dev[i] = lax.rem(me[i] + (o if sign > 0 else sizes[i] - o), sizes[i])
+        return tuple(dev)
+
     barrier = pltpu.get_barrier_semaphore()
     count = 0
-    for n, to, _ in stages:
-        for k in range(1, n):
-            pl.semaphore_signal(barrier, 1, device_id=to(k), device_id_type=MESH)
+    for axes, offs in plan:
+        for off in offs:
+            pl.semaphore_signal(barrier, 1, device_id=shift(axes, off, 1), device_id_type=MESH)
             count += 1
     pl.semaphore_wait(barrier, count)
 
-    def region(stage, dev):
-        rr, aa, xx = dev
-        if stage == 0:
-            return o_ref.at[pl.ds(rr, 1), pl.ds(aa, 1), pl.ds(xx, 1)]
-        if stage == 1:
-            return o_ref.at[pl.ds(rr, 1), pl.ds(aa, 1)]
-        return o_ref.at[pl.ds(rr, 1)]
-
-    local = pltpu.make_async_copy(x_ref, region(0, (r, a, x)), lsem)
+    covered = set()
+
+    def region(dev):
+        idx = []
+        for i in range(3):
+            if i in covered:
+                break
+            idx.append(pl.ds(dev[i], 1))
+        return o_ref.at[tuple(idx)] if idx else o_ref
+
+    def region_full(dev):
+        n_fixed = 3 - len(covered)
+        return o_ref.at[tuple(pl.ds(dev[i], 1) for i in range(n_fixed))]
+
+    local = pltpu.make_async_copy(x_ref, o_ref.at[tuple(pl.ds(m, 1) for m in me)], lsem)
     local.start()
     sends = []
     slot = 0
-    for stage, (n, to, frm) in enumerate(stages):
-        src = x_ref if stage == 0 else region(stage, (r, a, x))
+    for stage, (axes, offs) in enumerate(plan):
+        src = x_ref if stage == 0 else region_full(me)
         first = slot
-        for k in range(1, n):
-            copy = pltpu.make_async_remote_copy(
-                src_ref=src,
-                dst_ref=region(stage, (r, a, x)),
-                send_sem=ssem.at[slot],
-                recv_sem=rsem.at[slot],
-                device_id=to(k),
-                device_id_type=MESH,
-            )
-            copy.start()
-            sends.append(copy)
+        for off in offs:
+            c = pltpu.make_async_remote_copy(src_ref=src, dst_ref=region_full(me), send_sem=ssem.at[slot],
+                                             recv_sem=rsem.at[slot], device_id=shift(axes, off, 1), device_id_type=MESH)
+            c.start()
+            sends.append(c)
             slot += 1
         slot = first
-        for k in range(1, n):
-            incoming = pltpu.make_async_remote_copy(
-                src_ref=src,
-                dst_ref=region(stage, frm(k)),
-                send_sem=ssem.at[slot],
-                recv_sem=rsem.at[slot],
-                device_id=frm(k),
-                device_id_type=MESH,
-            )
-            incoming.wait_recv()
+        for off in offs:
+            frm = shift(axes, off, -1)
+            c = pltpu.make_async_remote_copy(src_ref=src, dst_ref=region_full(frm), send_sem=ssem.at[slot],
+                                             recv_sem=rsem.at[slot], device_id=frm, device_id_type=MESH)
+            c.wait_recv()
             slot += 1
         if stage == 0:
             local.wait()
-    for copy in sends:
-        copy.wait_send()
-
-
-def gather_all(values, cid):
-    n_r, n_a, n_x = (lax.axis_size(ax) for ax in AXES)
+        covered.update(axes)
+    for c in sends:
+        c.wait_send()
+
+
+def gather_all(values, cid, groups=((2, 1), (0,))):
+    sizes = tuple(lax.axis_size(a) for a in AXES)
     width = values.shape[0]
-    links = (n_r - 1) + (n_a - 1) + (n_x - 1)
+    links = sum(len(offs) for _, offs in stage_plan(sizes, groups))
     out = pl.pallas_call(
-        functools.partial(gather_kernel, (n_r, n_a, n_x)),
-        out_shape=jax.ShapeDtypeStruct((n_r, n_a, n_x, width), jnp.float32),
+        functools.partial(gen_gather_kernel, sizes, groups),
+        out_shape=jax.ShapeDtypeStruct(sizes + (width,), jnp.float32),
         in_specs=[pl.BlockSpec(memory_space=pltpu.VMEM)],
         out_specs=pl.BlockSpec(memory_space=pltpu.VMEM),
-        scratch_shapes=[
-            pltpu.SemaphoreType.DMA(()),
-            pltpu.SemaphoreType.DMA((links,)),
-            pltpu.SemaphoreType.DMA((links,)),
-        ],
+        scratch_shapes=[pltpu.SemaphoreType.DMA(()), pltpu.SemaphoreType.DMA((links,)), pltpu.SemaphoreType.DMA((links,))],
         compiler_params=pltpu.CompilerParams(collective_id=cid, has_side_effects=True),
     )(values.reshape(1, 1, 1, width))
     return out.reshape(-1)
@@ -312,7 +309,7 @@
 
 def stencil(primal, adjoint):
     fields, rows, n_a, n_x = primal.shape
-    anywhere = pl.BlockSpec(memory_space=pl.ANY)
+    anywhere = pl.BlockSpec(memory_space=pltpu.HBM)
     return pl.pallas_call(
         stencil_kernel,
         out_shape=jax.ShapeDtypeStruct((rows, n_a, n_x), jnp.float32),
@@ -331,7 +328,7 @@
             pltpu.SemaphoreType.DMA((6,)),
         ],
         compiler_params=pltpu.CompilerParams(
-            collective_id=2, has_side_effects=True, vmem_limit_bytes=48 * 1024 * 1024
+            collective_id=2, has_side_effects=True, vmem_limit_bytes=67043328
         ),
     )(primal, adjoint)
 

time: 73.8 us -> 69.8 us (0.946)
  Pallas kernels: 61.8 us -> 58.8 us
  local copies, waits for them, and re-layouts: 6.65 us -> 4.71 us
  other arithmetic: 2.6 us -> 3.55 us
    pallas_call x2, Pallas kernels: 40.3 us -> 36.6 us  [gather_all(): pl.pallas_call(functools.partial(gen_gather_kernel, sizes, groups), out_s...]
    unnamed x16 -> x12, local copies, waits for them, and re-layouts: 3.45 us -> 1.51 us
    reduce_sum x2, other arithmetic: 0.13 us -> 1.08 us  [on_device(): indicator.reshape(per_rad, BLK, per_azi, BLK, per_ax, BLK)]
where the time goes in v6:
time: 69.8 us; the launch traced here: 69.6 us
  Pallas kernels  58.8 us (84%)
  local copies, waits for them, and re-layouts  4.71 us (7%)
  other arithmetic  3.55 us (5%)
  between operations  2.54 us (4%)
    pallas_call x2, Pallas kernels, gather_all(): pl.pallas_call(functools.partial(gen_gather_kernel, sizes, groups), out_s...  36.6 us
    pallas_call x1, Pallas kernels, stencil(): pl.pallas_call(stencil_kernel, out_shape=jax.ShapeDtypeStruct((rows, n_a,...  22.2 us
    reduce_sum x1, other arithmetic, on_device(): jnp.sum(jnp.where(owner_all == own_index.astype(jnp.float32), cost_all, 0...  1.69 us
    unnamed x12, local copies, waits for them, and re-layouts  1.51 us

profile of v6, /device:TPU:1, one launch (start us, length us, event | category | flops | bytes accessed | tf_op | source)
XLA Modules:
  0.0 69.6 jit_solution(12652115407387692558)
XLA Ops:
  0.6 22.2 %shard_map.85 = f32[16,32,128]{2,1,0:T(8,128)} custom-call(f32[5,16,32,128]{3,2,1,0:T(8,128)} %p_hbm.1, f32[5,16,32,128]{3,2,1,0:T(8,128)} %a_hbm.1), custom_call_target="tpu_custom_call" | custom-call | tf_op jit(solution)/shard_map/pallas_call | solution.py:313
  22.8 1.0 %reduce_sum.34 = f32[32,128]{1,0:T(8,128)S(1)} reduce(f32[16,32,128]{2,1,0:T(8,128)} %shard_map.85, f32[]{:T(128)} %constant.131.clone.1), dimensions={0}, to_apply=%region_0.0 | reduce | flops 61440 | bytes 278532 | tf_op jit(solution)/shard_map/reduce_sum | solution.py:342
  23.8 0.1 reduce_sum.35
  23.9 0.1 reduce_sum.36
  24.0 0.6 div.67.x_ref
  24.6 21.5 %shard_map.86 = f32[8,8,4,16]{3,2,1,0:T(4,128)} custom-call(f32[1,1,1,16]{3,2,1,0:T(1,128)} %div.67.x_ref), custom_call_target="tpu_custom_call" | custom-call | tf_op jit(solution)/shard_map/pallas_call | solution.py:86
  46.1 1.0 %reshape.80 = f32[4096]{0:T(1024)S(1)} reshape(f32[8,8,4,16]{3,2,1,0:T(4,128)} %shard_map.86) | data formatting | bytes 32768 | tf_op jit(solution)/shard_map/reshape | solution.py:94
  47.1 0.8 %copy.17 = s32[1,2,8,6]{3,2,1,0:T(8,128)S(1)} copy(s32[1,2,8,6]{2,1,3,0:T(2,128)} %param.11) | data formatting | bytes 768 | tf_op args[5]
  47.9 0.1 reshape.86
  48.0 0.0 copy-start.1
  48.0 0.0 copy-start.2
  48.0 0.0 copy-start.3
  48.1 0.0 copy-start
  48.1 1.1 %gather_fusion = f32[96]{0:T(128)S(1)} fusion(f32[4096]{0:T(1024)S(1)} %reshape.80, s32[1024]{0:T(1024)S(1)} %pad_clamp_fusion), kind=kCustom, calls=%fused_computation | custom fusion | bytes 1152 | tf_op jit(solution)/shard_map/jit(_take)/gather | solution.py:357
  49.2 0.1 reshape.85
  49.3 0.1 select_reduce_fusion
  49.4 0.0 copy-done.1
  49.4 0.0 copy-done.2
  49.4 0.0 copy-done.3
  49.5 0.0 copy-start.4
  49.5 0.1 reshape.81
  49.6 0.1 convert_element_type.19
  49.6 0.6 maximum_bitcast_fusion.x_ref
  50.2 15.1 %shard_map.87 = f32[8,8,4,32]{3,2,1,0:T(4,128)} custom-call(f32[1,1,1,32]{3,2,1,0:T(1,128)} %maximum_bitcast_fusion.x_ref), custom_call_target="tpu_custom_call" | custom-call | tf_op jit(solution)/shard_map/pallas_call | solution.py:86
  65.4 1.7 %fusion = f32[]{:T(128)} fusion(f32[256,32]{1,0:T(8,128)} %bitcast.10, f32[]{:T(128)S(6)} %convert_element_type.20), kind=kLoop, calls=%fused_computation.2 | loop fusion | flops 12287 | bytes 32776 | tf_op jit(solution)/shard_map/reduce_sum | solution.py:372
  67.7 0.0 copy-done
  67.7 0.7 %copy.22 = f32[16,32,128]{2,1,0:T(8,128)} copy(f32[16,32,128]{2,1,0:T(8,128)S(1)} %copy-done) | data formatting | bytes 524288
  68.4 0.0 copy-done.4
  (5 shorter events, 0.1 us)
Async XLA Ops:
  48.0 1.4 %copy-start.1 = (s32[1,2,8]{2,1,0:T(2,128)S(1)}, s32[1,2,8]{2,1,0:T(2,128)}, u32[]{:S(2)}) copy-start(s32[1,2,8]{2,1,0:T(2,128)} %param.9) | copy-start | bytes 196
  48.0 1.4 %copy-start.2 = (s32[1,2,8]{2,1,0:T(2,128)S(1)}, s32[1,2,8]{2,1,0:T(2,128)}, u32[]{:S(2)}) copy-start(s32[1,2,8]{2,1,0:T(2,128)} %param.10) | copy-start | bytes 196
  48.0 1.4 %copy-start.3 = (s32[1,2,8]{2,1,0:T(2,128)S(1)}, s32[1,2,8]{2,1,0:T(2,128)}, u32[]{:S(2)}) copy-start(s32[1,2,8]{2,1,0:T(2,128)} %param.8) | copy-start | bytes 196
  48.1 19.7 %copy-start = (f32[16,32,128]{2,1,0:T(8,128)S(1)}, f32[16,32,128]{2,1,0:T(8,128)}, u32[]{:S(2)}) copy-start(f32[16,32,128]{2,1,0:T(8,128)} %shard_map.85) | copy-start | bytes 786436
  49.5 19.0 %copy-start.4 = (f32[1,2,8]{2,1,0:T(2,128)}, f32[1,2,8]{2,1,0:T(2,128)S(1)}, u32[]{:S(2)}) copy-start(f32[1,2,8]{2,1,0:T(2,128)S(1)} %fusion.21) | copy-start | bytes 196

commit v7 on v6

--- a/solution.py
+++ b/solution.py
@@ -20,7 +20,7 @@
     return plan
 
 
-def gen_gather_kernel(sizes, groups, x_ref, o_ref, lsem, ssem, rsem):
+def gen_gather_kernel(sizes, groups, x_ref, o_ref, lsem, ssem, rsem, with_barrier=True):
     me = tuple(lax.axis_index(a) for a in AXES)
     plan = stage_plan(sizes, groups)
 
@@ -30,13 +30,14 @@
             dev[i] = lax.rem(me[i] + (o if sign > 0 else sizes[i] - o), sizes[i])
         return tuple(dev)
 
-    barrier = pltpu.get_barrier_semaphore()
-    count = 0
-    for axes, offs in plan:
-        for off in offs:
-            pl.semaphore_signal(barrier, 1, device_id=shift(axes, off, 1), device_id_type=MESH)
-            count += 1
-    pl.semaphore_wait(barrier, count)
+    if with_barrier:
+        barrier = pltpu.get_barrier_semaphore()
+        count = 0
+        for axes, offs in plan:
+            for off in offs:
+                pl.semaphore_signal(barrier, 1, device_id=shift(axes, off, 1), device_id_type=MESH)
+                count += 1
+        pl.semaphore_wait(barrier, count)
 
     covered = set()
 
@@ -75,7 +76,11 @@
         if stage == 0:
             local.wait()
         covered.update(axes)
-    for c in sends:
+    return sends
+
+
+def gather_kernel(sizes, groups, x_ref, o_ref, lsem, ssem, rsem):
+    for c in gen_gather_kernel(sizes, groups, x_ref, o_ref, lsem, ssem, rsem):
         c.wait_send()
 
 
@@ -84,7 +89,7 @@
     width = values.shape[0]
     links = sum(len(offs) for _, offs in stage_plan(sizes, groups))
     out = pl.pallas_call(
-        functools.partial(gen_gather_kernel, sizes, groups),
+        functools.partial(gather_kernel, sizes, groups),
         out_shape=jax.ShapeDtypeStruct(sizes + (width,), jnp.float32),
         in_specs=[pl.BlockSpec(memory_space=pltpu.VMEM)],
         out_specs=pl.BlockSpec(memory_space=pltpu.VMEM),
@@ -135,7 +140,8 @@
     return (zm2 - 4.0 * zm1 + 6.0 * z - 4.0 * zp1 + zp2) / 12.0
 
 
-def stencil_kernel(p_hbm, a_hbm, out_ref, e, az_send, az_recv, az_exp, x_send, x_recv, xt, sems, ssem, rsem):
+def stencil_kernel(groups, p_hbm, a_hbm, out_ref, g_out, e, az_send, az_recv, az_exp, x_send, x_recv, xt, sems, ssem, rsem,
+                   pay, glsem, gssem, grsem):
     _, fields, ext_rows, n_a, n_x = e.shape
     rows = ext_rows - 4
     n_r_dev, n_a_dev, n_x_dev = (lax.axis_size(ax) for ax in AXES)
@@ -154,15 +160,18 @@
     for c in loads:
         c.start()
 
+    sizes = (n_r_dev, n_a_dev, n_x_dev)
+    me = (me_r, me_a, me_x)
     barrier = pltpu.get_barrier_semaphore()
-    for cond, dev in ((has_r_lo, r_lo), (has_r_hi, r_hi), (has_x_lo, x_lo), (has_x_hi, x_hi)):
-        @pl.when(cond)
-        def _():
-            pl.semaphore_signal(barrier, 1, device_id=dev, device_id_type=MESH)
-    pl.semaphore_signal(barrier, 1, device_id=a_lo, device_id_type=MESH)
-    pl.semaphore_signal(barrier, 1, device_id=a_hi, device_id_type=MESH)
-    count = 2 + sum(c.astype(jnp.int32) for c in (has_r_lo, has_r_hi, has_x_lo, has_x_hi))
-    pl.semaphore_wait(barrier, count)
+    n_peers = 0
+    for axes, offs in stage_plan(sizes, groups):
+        for off in offs:
+            dev = list(me)
+            for i, o in zip(axes, off):
+                dev[i] = lax.rem(me[i] + o, sizes[i])
+            pl.semaphore_signal(barrier, 1, device_id=tuple(dev), device_id_type=MESH)
+            n_peers += 1
+    pl.semaphore_wait(barrier, n_peers)
 
     x_recv[:, x_send.shape[1]:, :] = jnp.zeros((2, x_recv.shape[1] - x_send.shape[1], x_recv.shape[2]), jnp.float32)
     x_send[:, 4 * fields:, :] = jnp.zeros((2, x_send.shape[1] - 4 * fields, x_send.shape[2]), jnp.float32)
@@ -298,23 +307,41 @@
         total = weight[0] * balance[0]
         for f in range(1, fields):
             total = total + weight[f] * balance[f]
-        out_ref[r] = jnp.abs(total)
-        return carry
-
-    lax.fori_loop(0, rows, row_body, 0)
+        value = jnp.abs(total)
+        out_ref[r] = value
+        return carry + value
+
+    acc = lax.fori_loop(0, rows, row_body, jnp.zeros((n_a, n_x), jnp.float32))
+    per_azi, per_ax = n_a // BLK, n_x // BLK
+    width = per_azi * per_ax
+    lane_l = lax.broadcasted_iota(jnp.int32, (n_x, width), 0)
+    col_j = lax.broadcasted_iota(jnp.int32, (n_x, width), 1)
+    means = None
+    for ba in range(per_azi):
+        half = jnp.sum(acc[ba * BLK:(ba + 1) * BLK], axis=0, keepdims=True)
+        pick = jnp.where((col_j // per_ax == ba) & (lane_l // BLK == col_j % per_ax), 1.0, 0.0)
+        part = jnp.dot(half, pick, precision=lax.Precision.HIGHEST, preferred_element_type=jnp.float32)
+        means = part if means is None else means + part
+    pay[0, 0] = means / float(rows * BLK * BLK)
+    sends_g = gen_gather_kernel(sizes, groups, pay, g_out, glsem, gssem, grsem, with_barrier=False)
 
     for cond, c in sends:
         when(cond, c.wait_send)
-
-
-def stencil(primal, adjoint):
+    for c in sends_g:
+        c.wait_send()
+
+
+def stencil(primal, adjoint, groups=((2, 1), (0,))):
     fields, rows, n_a, n_x = primal.shape
     anywhere = pl.BlockSpec(memory_space=pltpu.HBM)
+    sizes = tuple(lax.axis_size(a) for a in AXES)
+    width = (n_a // BLK) * (n_x // BLK)
+    links = sum(len(offs) for _, offs in stage_plan(sizes, groups))
     return pl.pallas_call(
-        stencil_kernel,
-        out_shape=jax.ShapeDtypeStruct((rows, n_a, n_x), jnp.float32),
+        functools.partial(stencil_kernel, groups),
+        out_shape=(jax.ShapeDtypeStruct((rows, n_a, n_x), jnp.float32), jax.ShapeDtypeStruct(sizes + (width,), jnp.float32)),
         in_specs=[anywhere, anywhere],
-        out_specs=pl.BlockSpec(memory_space=pltpu.VMEM),
+        out_specs=(pl.BlockSpec(memory_space=pltpu.VMEM), pl.BlockSpec(memory_space=pltpu.VMEM)),
         scratch_shapes=[
             pltpu.VMEM((2, fields, rows + 4, n_a, n_x), jnp.float32),
             pltpu.VMEM((2, 2 * fields * rows * 2, n_x), jnp.float32),
@@ -326,6 +353,10 @@
             pltpu.SemaphoreType.DMA((2,)),
             pltpu.SemaphoreType.DMA((6,)),
             pltpu.SemaphoreType.DMA((6,)),
+            pltpu.VMEM((1, 1, 1, width), jnp.float32),
+            pltpu.SemaphoreType.DMA(()),
+            pltpu.SemaphoreType.DMA((links,)),
+            pltpu.SemaphoreType.DMA((links,)),
         ],
         compiler_params=pltpu.CompilerParams(
             collective_id=2, has_side_effects=True, vmem_limit_bytes=67043328
@@ -334,13 +365,14 @@
 
 
 def on_device(primal, adjoint, refine_flag, owner_map, migrate_weight, neighbor_list):
-    indicator = stencil(primal, adjoint)
+    indicator, gathered_means = stencil(primal, adjoint)
     rows_rad, rows_azi, rows_ax = indicator.shape
     per_rad = rows_rad // BLK
     per_azi = rows_azi // BLK
     per_ax = rows_ax // BLK
-    block_mean = indicator.reshape(per_rad, BLK, per_azi, BLK, per_ax, BLK).mean(axis=(1, 3, 5))
-    all_means = gather_all(block_mean.reshape(-1), 0)
+    all_means = gathered_means.reshape(-1)
+    me_dev = (lax.axis_index("rad") * lax.axis_size("azi") + lax.axis_index("azi")) * lax.axis_size("ax") + lax.axis_index("ax")
+    block_mean = lax.dynamic_slice_in_dim(all_means, me_dev * (per_rad * per_azi * per_ax), per_rad * per_azi * per_ax).reshape(per_rad, per_azi, per_ax)
     size_rad = lax.axis_size("rad")
     size_azi = lax.axis_size("azi")
     size_ax = lax.axis_size("ax")

time: 69.8 us -> 65.7 us (0.941)
  Pallas kernels: 58.8 us -> 56.3 us
  other arithmetic: 3.55 us -> 2.54 us
    pallas_call x3 -> x2, Pallas kernels: 58.8 us -> 56.3 us  [the longest x1 41 us: stencil(): pl.pallas_call(functools.partial(stencil_kernel, groups), out_shape=(jax....]
    reduce_sum x2 -> x0, other arithmetic: 1.08 us -> none  [on_device(): indicator.reshape(per_rad, BLK, per_azi, BLK, per_ax, BLK)]
where the time goes in v7:
time: 65.7 us; the launch traced here: 65.4 us
  Pallas kernels  56.3 us (86%)
  local copies, waits for them, and re-layouts  4.11 us (6%)
  other arithmetic  2.54 us (4%)
  between operations  2.52 us (4%)
    pallas_call x1, Pallas kernels, stencil(): pl.pallas_call(functools.partial(stencil_kernel, groups), out_shape=(jax....  41 us
    pallas_call x1, Pallas kernels, gather_all(): pl.pallas_call(functools.partial(gather_kernel, sizes, groups), out_shape...  15.2 us
    reduce_sum x1, other arithmetic, on_device(): jnp.sum(jnp.where(owner_all == own_index.astype(jnp.float32), cost_all, 0...  1.69 us
    unnamed x12, local copies, waits for them, and re-layouts  1.51 us

profile of v7, /device:TPU:1, one launch (start us, length us, event | category | flops | bytes accessed | tf_op | source)
XLA Modules:
  0.0 65.4 jit_solution(4579144208746775326)
XLA Ops:
  0.6 41.0 %shard_map.85 = (f32[16,32,128]{2,1,0:T(8,128)}, f32[8,8,4,16]{3,2,1,0:T(4,128)}) custom-call(f32[5,16,32,128]{3,2,1,0:T(8,128)} %p_hbm.1, f32[5,16,32,128]{3,2,1,0:T(8,128)} %a_hbm.1), custom_call_target="tpu_custom_call" | custom-call | tf_op jit(solution)/shard_map/pallas_call | solution.py:340
  41.7 1.0 %reshape.66 = f32[4096]{0:T(1024)S(1)} reshape(f32[8,8,4,16]{3,2,1,0:T(4,128)} %get-tuple-element.6) | data formatting | bytes 32768 | tf_op jit(solution)/shard_map/reshape | solution.py:373
  42.7 0.1 dynamic-slice_multiply_fusion
  42.8 0.1 mul.78
  42.9 0.8 %copy.13 = s32[1,2,8,6]{3,2,1,0:T(8,128)S(1)} copy(s32[1,2,8,6]{2,1,3,0:T(2,128)} %param.11) | data formatting | bytes 768 | tf_op args[5]
  43.7 0.1 reshape.72
  43.8 0.0 copy-start.1
  43.8 0.0 copy-start.2
  43.8 0.0 copy-start.3
  43.8 0.0 copy-start
  43.8 1.1 %gather_fusion = f32[96]{0:T(128)S(1)} fusion(f32[4096]{0:T(1024)S(1)} %reshape.66, s32[1024]{0:T(1024)S(1)} %pad_clamp_fusion), kind=kCustom, calls=%fused_computation | custom fusion | bytes 1152 | tf_op jit(solution)/shard_map/jit(_take)/gather | solution.py:389
  45.0 0.1 reshape.71
  45.1 0.1 select_reduce_fusion
  45.2 0.0 copy-done.1
  45.2 0.0 copy-done.2
  45.2 0.0 copy-done.3
  45.2 0.0 copy-start.4
  45.3 0.1 reshape.67
  45.3 0.1 convert_element_type.19
  45.4 0.6 maximum_bitcast_fusion.x_ref
  46.0 15.2 %shard_map.86 = f32[8,8,4,32]{3,2,1,0:T(4,128)} custom-call(f32[1,1,1,32]{3,2,1,0:T(1,128)} %maximum_bitcast_fusion.x_ref), custom_call_target="tpu_custom_call" | custom-call | tf_op jit(solution)/shard_map/pallas_call | solution.py:91
  61.2 1.7 %fusion = f32[]{:T(128)} fusion(f32[256,32]{1,0:T(8,128)} %bitcast.12, f32[]{:T(128)S(6)} %convert_element_type.20), kind=kLoop, calls=%fused_computation.2 | loop fusion | flops 12287 | bytes 32776 | tf_op jit(solution)/shard_map/reduce_sum | solution.py:404
  63.6 0.0 copy-done
  63.6 0.7 %copy.18 = f32[16,32,128]{2,1,0:T(8,128)} copy(f32[16,32,128]{2,1,0:T(8,128)S(1)} %copy-done) | data formatting | bytes 524288
  64.3 0.0 copy-done.4
  (4 shorter events, 0.1 us)
Async XLA Ops:
  43.8 1.4 %copy-start.1 = (s32[1,2,8]{2,1,0:T(2,128)S(1)}, s32[1,2,8]{2,1,0:T(2,128)}, u32[]{:S(2)}) copy-start(s32[1,2,8]{2,1,0:T(2,128)} %param.9) | copy-start | bytes 196
  43.8 1.4 %copy-start.2 = (s32[1,2,8]{2,1,0:T(2,128)S(1)}, s32[1,2,8]{2,1,0:T(2,128)}, u32[]{:S(2)}) copy-start(s32[1,2,8]{2,1,0:T(2,128)} %param.10) | copy-start | bytes 196
  43.8 1.4 %copy-start.3 = (s32[1,2,8]{2,1,0:T(2,128)S(1)}, s32[1,2,8]{2,1,0:T(2,128)}, u32[]{:S(2)}) copy-start(s32[1,2,8]{2,1,0:T(2,128)} %param.8) | copy-start | bytes 196
  43.8 19.8 %copy-start = (f32[16,32,128]{2,1,0:T(8,128)S(1)}, f32[16,32,128]{2,1,0:T(8,128)}, u32[]{:S(2)}) copy-start(f32[16,32,128]{2,1,0:T(8,128)} %get-tuple-element.10) | copy-start | bytes 786436
  45.2 19.1 %copy-start.4 = (f32[1,2,8]{2,1,0:T(2,128)}, f32[1,2,8]{2,1,0:T(2,128)S(1)}, u32[]{:S(2)}) copy-start(f32[1,2,8]{2,1,0:T(2,128)S(1)} %fusion.21) | copy-start | bytes 196

commit v8 on v7

--- a/solution.py
+++ b/solution.py
@@ -178,18 +178,6 @@
     for c in loads:
         c.wait()
 
-    for k in range(2):
-        for f in range(fields):
-            for r in range(rows):
-                row = ((k * fields + f) * rows + r) * 2
-                az_send[0, row:row + 2, :] = e[k, f, 2 + r, 0:2, :]
-                az_send[1, row:row + 2, :] = e[k, f, 2 + r, n_a - 2:n_a, :]
-            plane = e[k, f, 2:2 + rows].reshape(rows * n_a, n_x)
-            cols = plane.T
-            row = (k * fields + f) * 2
-            x_send[0, row:row + 2, :] = cols[0:2]
-            x_send[1, row:row + 2, :] = cols[n_x - 2:n_x]
-
     def remote(src, dst, i, dev):
         return pltpu.make_async_remote_copy(
             src_ref=src, dst_ref=dst, send_sem=ssem.at[i], recv_sem=rsem.at[i],
@@ -220,7 +208,22 @@
         else:
             pl.when(cond)(fn)
 
-    for cond, c in sends:
+    for cond, c in sends[:2]:
+        when(cond, c.start)
+
+    for k in range(2):
+        for f in range(fields):
+            for r in range(rows):
+                row = ((k * fields + f) * rows + r) * 2
+                az_send[0, row:row + 2, :] = e[k, f, 2 + r, 0:2, :]
+                az_send[1, row:row + 2, :] = e[k, f, 2 + r, n_a - 2:n_a, :]
+            plane = e[k, f, 2:2 + rows].reshape(rows * n_a, n_x)
+            cols = plane.T
+            row = (k * fields + f) * 2
+            x_send[0, row:row + 2, :] = cols[0:2]
+            x_send[1, row:row + 2, :] = cols[n_x - 2:n_x]
+
+    for cond, c in sends[2:]:
         when(cond, c.start)
 
     @pl.when(jnp.logical_not(has_r_lo))
@@ -239,7 +242,7 @@
     def _():
         x_recv[1, 0:n_kx, :] = jnp.zeros((n_kx, x_recv.shape[2]), jnp.float32)
 
-    for cond, c in recvs:
+    for cond, c in recvs[2:]:
         when(cond, c.wait_recv)
 
     for side in range(2):
@@ -311,7 +314,11 @@
         out_ref[r] = value
         return carry + value
 
-    acc = lax.fori_loop(0, rows, row_body, jnp.zeros((n_a, n_x), jnp.float32))
+    acc = lax.fori_loop(2, rows - 2, row_body, jnp.zeros((n_a, n_x), jnp.float32))
+    for cond, c in recvs[:2]:
+        when(cond, c.wait_recv)
+    acc = lax.fori_loop(0, 2, row_body, acc)
+    acc = lax.fori_loop(rows - 2, rows, row_body, acc)
     per_azi, per_ax = n_a // BLK, n_x // BLK
     width = per_azi * per_ax
     lane_l = lax.broadcasted_iota(jnp.int32, (n_x, width), 0)

time: 65.7 us -> 62.1 us (0.945)
  Pallas kernels: 56.3 us -> 52.7 us
    pallas_call x1, Pallas kernels: 41 us -> 35.7 us  [stencil(): pl.pallas_call(functools.partial(stencil_kernel, groups), out_shape=(jax....]
    pallas_call x1, Pallas kernels: 15.2 us -> 17.1 us  [gather_all(): pl.pallas_call(functools.partial(gather_kernel, sizes, groups), out_shape...]
where the time goes in v8:
time: 62.1 us; the launch traced here: 61.9 us
  Pallas kernels  52.7 us (85%)
  local copies, waits for them, and re-layouts  4.11 us (7%)
  other arithmetic  2.54 us (4%)
  between operations  2.52 us (4%)
    pallas_call x1, Pallas kernels, stencil(): pl.pallas_call(functools.partial(stencil_kernel, groups), out_shape=(jax....  35.7 us
    pallas_call x1, Pallas kernels, gather_all(): pl.pallas_call(functools.partial(gather_kernel, sizes, groups), out_shape...  17.1 us
    reduce_sum x1, other arithmetic, on_device(): jnp.sum(jnp.where(owner_all == own_index.astype(jnp.float32), cost_all, 0...  1.69 us
    unnamed x12, local copies, waits for them, and re-layouts  1.51 us

profile of v8, /device:TPU:1, one launch (start us, length us, event | category | flops | bytes accessed | tf_op | source)
XLA Modules:
  0.0 61.9 jit_solution(14714450456484869418)
XLA Ops:
  0.6 35.7 %shard_map.85 = (f32[16,32,128]{2,1,0:T(8,128)}, f32[8,8,4,16]{3,2,1,0:T(4,128)}) custom-call(f32[5,16,32,128]{3,2,1,0:T(8,128)} %p_hbm.1, f32[5,16,32,128]{3,2,1,0:T(8,128)} %a_hbm.1), custom_call_target="tpu_custom_call" | custom-call | tf_op jit(solution)/shard_map/pallas_call | solution.py:347
  36.3 1.0 %reshape.66 = f32[4096]{0:T(1024)S(1)} reshape(f32[8,8,4,16]{3,2,1,0:T(4,128)} %get-tuple-element.6) | data formatting | bytes 32768 | tf_op jit(solution)/shard_map/reshape | solution.py:380
  37.3 0.1 dynamic-slice_multiply_fusion
  37.4 0.1 mul.78
  37.5 0.8 %copy.13 = s32[1,2,8,6]{3,2,1,0:T(8,128)S(1)} copy(s32[1,2,8,6]{2,1,3,0:T(2,128)} %param.11) | data formatting | bytes 768 | tf_op args[5]
  38.3 0.1 reshape.72
  38.4 0.0 copy-start.1
  38.4 0.0 copy-start.2
  38.4 0.0 copy-start.3
  38.5 0.0 copy-start
  38.5 1.1 %gather_fusion = f32[96]{0:T(128)S(1)} fusion(f32[4096]{0:T(1024)S(1)} %reshape.66, s32[1024]{0:T(1024)S(1)} %pad_clamp_fusion), kind=kCustom, calls=%fused_computation | custom fusion | bytes 1152 | tf_op jit(solution)/shard_map/jit(_take)/gather | solution.py:396
  39.6 0.1 reshape.71
  39.7 0.1 select_reduce_fusion
  39.8 0.0 copy-done.1
  39.8 0.0 copy-done.2
  39.8 0.0 copy-done.3
  39.9 0.0 copy-start.4
  39.9 0.1 reshape.67
  40.0 0.1 convert_element_type.19
  40.0 0.6 maximum_bitcast_fusion.x_ref
  40.6 17.1 %shard_map.86 = f32[8,8,4,32]{3,2,1,0:T(4,128)} custom-call(f32[1,1,1,32]{3,2,1,0:T(1,128)} %maximum_bitcast_fusion.x_ref), custom_call_target="tpu_custom_call" | custom-call | tf_op jit(solution)/shard_map/pallas_call | solution.py:91
  57.7 1.7 %fusion = f32[]{:T(128)} fusion(f32[256,32]{1,0:T(8,128)} %bitcast.12, f32[]{:T(128)S(6)} %convert_element_type.20), kind=kLoop, calls=%fused_computation.2 | loop fusion | flops 12287 | bytes 32776 | tf_op jit(solution)/shard_map/reduce_sum | solution.py:411
  60.0 0.0 copy-done
  60.1 0.7 %copy.18 = f32[16,32,128]{2,1,0:T(8,128)} copy(f32[16,32,128]{2,1,0:T(8,128)S(1)} %copy-done) | data formatting | bytes 524288
  60.8 0.0 copy-done.4
  (4 shorter events, 0.1 us)
Async XLA Ops:
  38.4 1.4 %copy-start.1 = (s32[1,2,8]{2,1,0:T(2,128)S(1)}, s32[1,2,8]{2,1,0:T(2,128)}, u32[]{:S(2)}) copy-start(s32[1,2,8]{2,1,0:T(2,128)} %param.9) | copy-start | bytes 196
  38.4 1.4 %copy-start.2 = (s32[1,2,8]{2,1,0:T(2,128)S(1)}, s32[1,2,8]{2,1,0:T(2,128)}, u32[]{:S(2)}) copy-start(s32[1,2,8]{2,1,0:T(2,128)} %param.10) | copy-start | bytes 196
  38.4 1.4 %copy-start.3 = (s32[1,2,8]{2,1,0:T(2,128)S(1)}, s32[1,2,8]{2,1,0:T(2,128)}, u32[]{:S(2)}) copy-start(s32[1,2,8]{2,1,0:T(2,128)} %param.8) | copy-start | bytes 196
  38.5 21.6 %copy-start = (f32[16,32,128]{2,1,0:T(8,128)S(1)}, f32[16,32,128]{2,1,0:T(8,128)}, u32[]{:S(2)}) copy-start(f32[16,32,128]{2,1,0:T(8,128)} %get-tuple-element.10) | copy-start | bytes 786436
  39.9 20.9 %copy-start.4 = (f32[1,2,8]{2,1,0:T(2,128)}, f32[1,2,8]{2,1,0:T(2,128)S(1)}, u32[]{:S(2)}) copy-start(f32[1,2,8]{2,1,0:T(2,128)S(1)} %fusion.21) | copy-start | bytes 196

commit v9 on v8

--- a/solution.py
+++ b/solution.py
@@ -82,6 +82,40 @@
 def gather_kernel(sizes, groups, x_ref, o_ref, lsem, ssem, rsem):
     for c in gen_gather_kernel(sizes, groups, x_ref, o_ref, lsem, ssem, rsem):
         c.wait_send()
+
+
+def load_kernel(sizes, groups, width, x_ref, load_out, o_ref, lsem, ssem, rsem):
+    sends = gen_gather_kernel(sizes, groups, x_ref, o_ref, lsem, ssem, rsem)
+    me = (lax.axis_index("rad") * sizes[1] + lax.axis_index("azi")) * sizes[2] + lax.axis_index("ax")
+    values = o_ref[...]
+    owners = pltpu.roll(values, values.shape[-1] - width, 3)
+    lane = lax.broadcasted_iota(jnp.int32, values.shape, 3)
+    picked = jnp.where((lane < width) & (owners == me.astype(jnp.float32)), values, 0.0)
+    part = jnp.sum(picked, axis=(0, 1))
+    total = jnp.sum(part, axis=0, keepdims=True)
+    total = jnp.sum(total, axis=1, keepdims=True)
+    load_out[...] = (total / float(width)).reshape(1, 1, 1)
+    for c in sends:
+        c.wait_send()
+
+
+def load_gather(payload, width, groups=((2, 1), (0,))):
+    sizes = tuple(lax.axis_size(a) for a in AXES)
+    lanes = payload.shape[0]
+    links = sum(len(offs) for _, offs in stage_plan(sizes, groups))
+    return pl.pallas_call(
+        functools.partial(load_kernel, sizes, groups, width),
+        out_shape=jax.ShapeDtypeStruct((1, 1, 1), jnp.float32),
+        in_specs=[pl.BlockSpec(memory_space=pltpu.VMEM)],
+        out_specs=pl.BlockSpec(memory_space=pltpu.VMEM),
+        scratch_shapes=[
+            pltpu.VMEM(sizes + (lanes,), jnp.float32),
+            pltpu.SemaphoreType.DMA(()),
+            pltpu.SemaphoreType.DMA((links,)),
+            pltpu.SemaphoreType.DMA((links,)),
+        ],
+        compiler_params=pltpu.CompilerParams(collective_id=1, has_side_effects=True),
+    )(payload.reshape(1, 1, 1, lanes))
 
 
 def gather_all(values, cid, groups=((2, 1), (0,))):
@@ -377,9 +411,10 @@
     per_rad = rows_rad // BLK
     per_azi = rows_azi // BLK
     per_ax = rows_ax // BLK
-    all_means = gathered_means.reshape(-1)
-    me_dev = (lax.axis_index("rad") * lax.axis_size("azi") + lax.axis_index("azi")) * lax.axis_size("ax") + lax.axis_index("ax")
-    block_mean = lax.dynamic_slice_in_dim(all_means, me_dev * (per_rad * per_azi * per_ax), per_rad * per_azi * per_ax).reshape(per_rad, per_azi, per_ax)
+    block_mean = lax.dynamic_slice(
+        gathered_means, (lax.axis_index("rad"), lax.axis_index("azi"), lax.axis_index("ax"), 0),
+        (1, 1, 1, gathered_means.shape[3]),
+    ).reshape(per_rad, per_azi, per_ax)
     size_rad = lax.axis_size("rad")
     size_azi = lax.axis_size("azi")
     size_ax = lax.axis_size("ax")
@@ -392,8 +427,10 @@
         block_rad // per_rad * size_azi + block_azi // per_azi
     ) * size_ax + block_ax // per_ax
     local_pos = (block_rad % per_rad * per_azi + block_azi % per_azi) * per_ax + block_ax % per_ax
-    position = owner_dev * (per_rad * per_azi * per_ax) + local_pos
-    beside_all = jnp.mean(jnp.take(all_means, position), axis=-1)
+    dev_rad = owner_dev // (size_azi * size_ax)
+    dev_azi = owner_dev // size_ax % size_azi
+    dev_ax = owner_dev % size_ax
+    beside_all = jnp.mean(gathered_means[dev_rad, dev_azi, dev_ax, local_pos], axis=-1)
     smooth = 0.5 * block_mean + 0.5 * beside_all
     own_index = (
         lax.axis_index("rad") * size_azi + lax.axis_index("azi")
@@ -404,12 +441,11 @@
         + 0.25 * migrate_weight.astype(jnp.float32) * moved
     )
     width = block_cost.size
-    payload = jnp.concatenate([block_cost.reshape(-1), owner_map.reshape(-1).astype(jnp.float32)])
-    gathered = gather_all(payload, 1).reshape(-1, 2 * width)
-    cost_all = gathered[:, :width]
-    owner_all = gathered[:, width:]
-    total = jnp.sum(jnp.where(owner_all == own_index.astype(jnp.float32), cost_all, 0.0))
-    owner_load = (total / (per_rad * per_azi * per_ax)).reshape(1, 1, 1)
+    payload = jnp.concatenate([
+        block_cost.reshape(-1), owner_map.reshape(-1).astype(jnp.float32),
+        jnp.zeros((128 - 2 * width,), jnp.float32),
+    ])
+    owner_load = load_gather(payload, width)
     return (indicator, block_cost, owner_load)
 
 

time: 62.1 us -> 61.8 us (level)
  local copies, waits for them, and re-layouts: 4.11 us -> 3.07 us
    reduce_sum x2 -> x1, other arithmetic: 1.82 us -> 0.09 us  [on_device(): jnp.mean(gathered_means[dev_rad, dev_azi, dev_ax, local_pos], axis=-1)]
    broadcast_in_dim x0 -> x2, other arithmetic: none -> 1.56 us  [on_device(): gathered_means[dev_rad, dev_azi, dev_ax, local_pos]]
    reshape x1 -> x0, local copies, waits for them, and re-layouts: 1.04 us -> none  [on_device(): all_means = gathered_means.reshape(-1)]
    unnamed x12 -> x13, local copies, waits for them, and re-layouts: 1.51 us -> 0.74 us
    mul x1, other arithmetic: 0.08 us -> 0.76 us  [on_device(): smooth = 0.5 * block_mean + 0.5 * beside_all]
    gather x2, local copies, waits for them, and re-layouts: 1.23 us -> 1.9 us  [on_device(): gathered_means[dev_rad, dev_azi, dev_ax, local_pos]]
where the time goes in v9:
time: 61.8 us; the launch traced here: 61.6 us
  Pallas kernels  52.9 us (86%)
  local copies, waits for them, and re-layouts  3.07 us (5%)
  other arithmetic  3.05 us (5%)
  between operations  2.59 us (4%)
    pallas_call x1, Pallas kernels, stencil(): pl.pallas_call(functools.partial(stencil_kernel, groups), out_shape=(jax....  35.7 us
    pallas_call x1, Pallas kernels, load_gather(): pl.pallas_call(functools.partial(load_kernel, sizes, groups, width), out_...  17.2 us
    gather x2, local copies, waits for them, and re-layouts, on_device(): gathered_means[dev_rad, dev_azi, dev_ax, local_pos]  1.9 us
    broadcast_in_dim x2, other arithmetic, on_device(): gathered_means[dev_rad, dev_azi, dev_ax, local_pos]  1.56 us

profile of v9, /device:TPU:1, one launch (start us, length us, event | category | flops | bytes accessed | tf_op | source)
XLA Modules:
  0.0 61.6 jit_solution(9052600104457084835)
XLA Ops:
  0.6 35.7 %shard_map.85 = (f32[16,32,128]{2,1,0:T(8,128)}, f32[8,8,4,16]{3,2,1,0:T(4,128)}) custom-call(f32[5,16,32,128]{3,2,1,0:T(8,128)} %p_hbm.1, f32[5,16,32,128]{3,2,1,0:T(8,128)} %a_hbm.1), custom_call_target="tpu_custom_call" | custom-call | tf_op jit(solution)/shard_map/pallas_call | solution.py:381
  36.3 0.0 copy-start
  36.3 0.8 %multiply_reduce_fusion = f32[16]{0:T(128)S(1)} fusion(f32[8,8,4,16]{3,2,1,0:T(4,128)} %get-tuple-element.6, s32[]{:T(128)S(6)} %select_n.74, s32[]{:T(128)S(6)} %select_n.75, s32[]{:T(128)S(6)} %select_n.76), kind=kLoop, calls=%fused_computation.74 | loop fusion | flops 16 | bytes 140 | tf_op jit(solution)/shard_map/mul | solution.py:434
  37.1 0.1 mul.63
  37.2 0.8 %fusion.6 = (s32[1,2,8,6,1]{2,1,3,4,0:T(2,128)S(1)}, s32[1,2,8,6]{2,1,3,0:T(2,128)S(1)}, s32[1,2,8,6]{2,1,3,0:T(2,128)S(1)}) fusion(s32[1,2,8,6]{2,1,3,0:T(2,128)} %param.11), kind=kLoop, calls=%fused_computation.44 | loop fusion | flops 8832 | bytes 1536 | tf_op jit(solution)/shard_map/broadcast_in_dim | solution.py:433
  38.0 0.8 %fusion.7 = (s32[1,2,8,6,1]{2,1,3,4,0:T(2,128)S(1)}, s32[1,2,8,6,1]{2,1,3,4,0:T(2,128)S(1)}, s32[1,2,8,6,1]{2,1,3,4,0:T(2,128)S(1)}) fusion(s32[1,2,8,6]{2,1,3,0:T(2,128)S(1)} %get-tuple-element.8, s32[1,2,8,6]{2,1,3,0:T(2,128)} %param.11, s32[1,2,8,6]{2,1,3,0:T(2,128)S(1)} %get-tuple-element.9), kind=kLoop, calls=%fused_computation.45 | loop fusion | flops 7104 | bytes 2304 | tf_op jit(solution)/shard_map/broadcast_in_dim | solution.py:433
  38.8 0.1 copy.10
  38.9 0.1 reshape.51
  39.0 0.0 copy-done
  39.0 0.0 copy-start.2
  39.0 0.0 copy-start.3
  39.0 0.0 copy-start.4
  39.0 0.0 copy-start.1
  39.0 1.8 %gather_fusion = f32[96]{0:T(128)S(1)} fusion(f32[8,8,4,16]{3,2,1,0:T(4,128)S(1)} %copy-done, s32[96]{0:T(128)S(1)} %reshape.51), kind=kCustom, calls=%fused_computation | custom fusion | bytes 2304 | tf_op jit(solution)/shard_map/gather | solution.py:433
  40.9 0.1 reshape.54
  40.9 0.1 reduce.1
  41.0 0.0 copy-done.2
  41.0 0.0 copy-done.3
  41.0 0.0 copy-done.4
  41.1 0.0 copy-start.5
  41.1 0.1 reshape.47
  41.2 0.1 convert_element_type.16
  41.2 0.6 maximum_bitcast_fusion.x_ref
  41.8 17.2 %shard_map.86 = f32[1,1,1]{2,1,0:T(1,128)} custom-call(f32[1,1,1,128]{3,2,1,0:T(1,128)} %maximum_bitcast_fusion.x_ref), custom_call_target="tpu_custom_call" | custom-call | tf_op jit(solution)/shard_map/pallas_call | solution.py:106
  59.0 0.0 copy-done.1
  59.1 0.7 %copy.13 = f32[16,32,128]{2,1,0:T(8,128)} copy(f32[16,32,128]{2,1,0:T(8,128)S(1)} %copy-done.1) | data formatting | bytes 524288
  60.5 0.0 copy-done.5
  (5 shorter events, 0.1 us)
Async XLA Ops:
  36.3 2.6 %copy-start = (f32[8,8,4,16]{3,2,1,0:T(4,128)S(1)}, f32[8,8,4,16]{3,2,1,0:T(4,128)}, u32[]{:S(2)}) copy-start(f32[8,8,4,16]{3,2,1,0:T(4,128)} %get-tuple-element.6) | copy-start | bytes 49156
  39.0 2.0 %copy-start.2 = (s32[1,2,8]{2,1,0:T(2,128)S(1)}, s32[1,2,8]{2,1,0:T(2,128)}, u32[]{:S(2)}) copy-start(s32[1,2,8]{2,1,0:T(2,128)} %param.9) | copy-start | bytes 196
  39.0 2.0 %copy-start.3 = (s32[1,2,8]{2,1,0:T(2,128)S(1)}, s32[1,2,8]{2,1,0:T(2,128)}, u32[]{:S(2)}) copy-start(s32[1,2,8]{2,1,0:T(2,128)} %param.10) | copy-start | bytes 196
  39.0 2.0 %copy-start.4 = (s32[1,2,8]{2,1,0:T(2,128)S(1)}, s32[1,2,8]{2,1,0:T(2,128)}, u32[]{:S(2)}) copy-start(s32[1,2,8]{2,1,0:T(2,128)} %param.8) | copy-start | bytes 196
  39.0 20.0 %copy-start.1 = (f32[16,32,128]{2,1,0:T(8,128)S(1)}, f32[16,32,128]{2,1,0:T(8,128)}, u32[]{:S(2)}) copy-start(f32[16,32,128]{2,1,0:T(8,128)} %get-tuple-element.16) | copy-start | bytes 786436
  41.1 19.4 %copy-start.5 = (f32[1,2,8]{2,1,0:T(2,128)}, f32[1,2,8]{2,1,0:T(2,128)S(1)}, u32[]{:S(2)}) copy-start(f32[1,2,8]{2,1,0:T(2,128)S(1)} %fusion.17) | copy-start | bytes 196

commit v10 on v9

--- a/solution.py
+++ b/solution.py
@@ -205,7 +205,6 @@
                 dev[i] = lax.rem(me[i] + o, sizes[i])
             pl.semaphore_signal(barrier, 1, device_id=tuple(dev), device_id_type=MESH)
             n_peers += 1
-    pl.semaphore_wait(barrier, n_peers)
 
     x_recv[:, x_send.shape[1]:, :] = jnp.zeros((2, x_recv.shape[1] - x_send.shape[1], x_recv.shape[2]), jnp.float32)
     x_send[:, 4 * fields:, :] = jnp.zeros((2, x_send.shape[1] - 4 * fields, x_send.shape[2]), jnp.float32)
@@ -242,9 +241,6 @@
         else:
             pl.when(cond)(fn)
 
-    for cond, c in sends[:2]:
-        when(cond, c.start)
-
     for k in range(2):
         for f in range(fields):
             for r in range(rows):
@@ -257,7 +253,8 @@
             x_send[0, row:row + 2, :] = cols[0:2]
             x_send[1, row:row + 2, :] = cols[n_x - 2:n_x]
 
-    for cond, c in sends[2:]:
+    pl.semaphore_wait(barrier, n_peers)
+    for cond, c in sends:
         when(cond, c.start)
 
     @pl.when(jnp.logical_not(has_r_lo))

time: 61.8 us -> 60.8 us (0.984)
  Pallas kernels: 52.9 us -> 51.8 us
    pallas_call x1, Pallas kernels: 35.7 us -> 34.7 us  [stencil(): pl.pallas_call(functools.partial(stencil_kernel, groups), out_shape=(jax....]
where the time goes in v10:
time: 60.8 us; the launch traced here: 60.5 us
  Pallas kernels  51.8 us (85%)
  local copies, waits for them, and re-layouts  3.07 us (5%)
  other arithmetic  3.05 us (5%)
  between operations  2.59 us (4%)
    pallas_call x1, Pallas kernels, stencil(): pl.pallas_call(functools.partial(stencil_kernel, groups), out_shape=(jax....  34.7 us
    pallas_call x1, Pallas kernels, load_gather(): pl.pallas_call(functools.partial(load_kernel, sizes, groups, width), out_...  17.1 us
    gather x2, local copies, waits for them, and re-layouts, on_device(): gathered_means[dev_rad, dev_azi, dev_ax, local_pos]  1.9 us
    broadcast_in_dim x2, other arithmetic, on_device(): gathered_means[dev_rad, dev_azi, dev_ax, local_pos]  1.56 us

profile of v10, /device:TPU:1, one launch (start us, length us, event | category | flops | bytes accessed | tf_op | source)
XLA Modules:
  0.0 60.5 jit_solution(10176162825851051748)
XLA Ops:
  0.6 34.7 %shard_map.85 = (f32[16,32,128]{2,1,0:T(8,128)}, f32[8,8,4,16]{3,2,1,0:T(4,128)}) custom-call(f32[5,16,32,128]{3,2,1,0:T(8,128)} %p_hbm.1, f32[5,16,32,128]{3,2,1,0:T(8,128)} %a_hbm.1), custom_call_target="tpu_custom_call" | custom-call | tf_op jit(solution)/shard_map/pallas_call | solution.py:378
  35.4 0.0 copy-start
  35.4 0.8 %multiply_reduce_fusion = f32[16]{0:T(128)S(1)} fusion(f32[8,8,4,16]{3,2,1,0:T(4,128)} %get-tuple-element.6, s32[]{:T(128)S(6)} %select_n.74, s32[]{:T(128)S(6)} %select_n.75, s32[]{:T(128)S(6)} %select_n.76), kind=kLoop, calls=%fused_computation.74 | loop fusion | flops 16 | bytes 140 | tf_op jit(solution)/shard_map/mul | solution.py:431
  36.2 0.1 mul.63
  36.2 0.8 %fusion.6 = (s32[1,2,8,6,1]{2,1,3,4,0:T(2,128)S(1)}, s32[1,2,8,6]{2,1,3,0:T(2,128)S(1)}, s32[1,2,8,6]{2,1,3,0:T(2,128)S(1)}) fusion(s32[1,2,8,6]{2,1,3,0:T(2,128)} %param.11), kind=kLoop, calls=%fused_computation.44 | loop fusion | flops 8832 | bytes 1536 | tf_op jit(solution)/shard_map/broadcast_in_dim | solution.py:430
  37.0 0.8 %fusion.7 = (s32[1,2,8,6,1]{2,1,3,4,0:T(2,128)S(1)}, s32[1,2,8,6,1]{2,1,3,4,0:T(2,128)S(1)}, s32[1,2,8,6,1]{2,1,3,4,0:T(2,128)S(1)}) fusion(s32[1,2,8,6]{2,1,3,0:T(2,128)S(1)} %get-tuple-element.8, s32[1,2,8,6]{2,1,3,0:T(2,128)} %param.11, s32[1,2,8,6]{2,1,3,0:T(2,128)S(1)} %get-tuple-element.9), kind=kLoop, calls=%fused_computation.45 | loop fusion | flops 7104 | bytes 2304 | tf_op jit(solution)/shard_map/broadcast_in_dim | solution.py:430
  37.9 0.1 copy.10
  37.9 0.1 reshape.51
  38.0 0.0 copy-done
  38.0 0.0 copy-start.2
  38.0 0.0 copy-start.3
  38.1 0.0 copy-start.4
  38.1 0.0 copy-start.1
  38.1 1.8 %gather_fusion = f32[96]{0:T(128)S(1)} fusion(f32[8,8,4,16]{3,2,1,0:T(4,128)S(1)} %copy-done, s32[96]{0:T(128)S(1)} %reshape.51), kind=kCustom, calls=%fused_computation | custom fusion | bytes 2304 | tf_op jit(solution)/shard_map/gather | solution.py:430
  39.9 0.1 reshape.54
  40.0 0.1 reduce.1
  40.1 0.0 copy-done.2
  40.1 0.0 copy-done.3
  40.1 0.0 copy-done.4
  40.1 0.0 copy-start.5
  40.1 0.1 reshape.47
  40.2 0.1 convert_element_type.16
  40.3 0.6 maximum_bitcast_fusion.x_ref
  40.9 17.1 %shard_map.86 = f32[1,1,1]{2,1,0:T(1,128)} custom-call(f32[1,1,1,128]{3,2,1,0:T(1,128)} %maximum_bitcast_fusion.x_ref), custom_call_target="tpu_custom_call" | custom-call | tf_op jit(solution)/shard_map/pallas_call | solution.py:106
  58.0 0.0 copy-done.1
  58.0 0.7 %copy.13 = f32[16,32,128]{2,1,0:T(8,128)} copy(f32[16,32,128]{2,1,0:T(8,128)S(1)} %copy-done.1) | data formatting | bytes 524288
  59.4 0.0 copy-done.5
  (5 shorter events, 0.1 us)
Async XLA Ops:
  35.4 2.6 %copy-start = (f32[8,8,4,16]{3,2,1,0:T(4,128)S(1)}, f32[8,8,4,16]{3,2,1,0:T(4,128)}, u32[]{:S(2)}) copy-start(f32[8,8,4,16]{3,2,1,0:T(4,128)} %get-tuple-element.6) | copy-start | bytes 49156
  38.0 2.0 %copy-start.2 = (s32[1,2,8]{2,1,0:T(2,128)S(1)}, s32[1,2,8]{2,1,0:T(2,128)}, u32[]{:S(2)}) copy-start(s32[1,2,8]{2,1,0:T(2,128)} %param.9) | copy-start | bytes 196
  38.0 2.0 %copy-start.3 = (s32[1,2,8]{2,1,0:T(2,128)S(1)}, s32[1,2,8]{2,1,0:T(2,128)}, u32[]{:S(2)}) copy-start(s32[1,2,8]{2,1,0:T(2,128)} %param.10) | copy-start | bytes 196
  38.1 2.0 %copy-start.4 = (s32[1,2,8]{2,1,0:T(2,128)S(1)}, s32[1,2,8]{2,1,0:T(2,128)}, u32[]{:S(2)}) copy-start(s32[1,2,8]{2,1,0:T(2,128)} %param.8) | copy-start | bytes 196
  38.1 19.9 %copy-start.1 = (f32[16,32,128]{2,1,0:T(8,128)S(1)}, f32[16,32,128]{2,1,0:T(8,128)}, u32[]{:S(2)}) copy-start(f32[16,32,128]{2,1,0:T(8,128)} %get-tuple-element.16) | copy-start | bytes 786436
  40.1 19.3 %copy-start.5 = (f32[1,2,8]{2,1,0:T(2,128)}, f32[1,2,8]{2,1,0:T(2,128)S(1)}, u32[]{:S(2)}) copy-start(f32[1,2,8]{2,1,0:T(2,128)S(1)} %fusion.17) | copy-start | bytes 196

commit v11 on v10

--- a/solution.py
+++ b/solution.py
@@ -116,6 +116,101 @@
         ],
         compiler_params=pltpu.CompilerParams(collective_id=1, has_side_effects=True),
     )(payload.reshape(1, 1, 1, lanes))
+
+
+def cost_load_kernel(sizes, groups, blocks, nl_ref, gm_ref, aux_ref, cost_out, load_out,
+                     gm_s, sums_s, sums_v, pay, o_ref, csem, lsem, ssem, rsem):
+    n_r, n_a, n_x = sizes
+    per_rad, per_azi, per_ax = blocks
+    width = per_rad * per_azi * per_ax
+    me = tuple(lax.axis_index(a) for a in AXES)
+    barrier = pltpu.get_barrier_semaphore()
+    n_peers = 0
+    for axes, offs in stage_plan(sizes, groups):
+        for off in offs:
+            dev = list(me)
+            for i, o in zip(axes, off):
+                dev[i] = lax.rem(me[i] + o, sizes[i])
+            pl.semaphore_signal(barrier, 1, device_id=tuple(dev), device_id_type=MESH)
+            n_peers += 1
+    to_smem = pltpu.make_async_copy(gm_ref, gm_s, csem.at[0])
+    to_smem.start()
+
+    def clear(i, carry):
+        sums_s[0, i] = 0.0
+        sums_s[1, i] = 0.0
+        return carry
+
+    lax.fori_loop(0, sums_s.shape[1], clear, 0)
+    to_smem.wait()
+    blocks_azi = per_azi * n_a
+    blocks_ax = per_ax * n_x
+    for b in range(width):
+        total = None
+        for k in range(6):
+            v = nl_ref[b * 6 + k]
+            br = v // (blocks_azi * blocks_ax)
+            ba = v // blocks_ax % blocks_azi
+            bx = v % blocks_ax
+            local = (br % per_rad * per_azi + ba % per_azi) * per_ax + bx % per_ax
+            val = gm_s[br // per_rad, ba // per_azi, bx // per_ax, local]
+            total = val if total is None else total + val
+        sums_s[0, b] = total
+        sums_s[1, b] = gm_s[me[0], me[1], me[2], b]
+    to_vmem = pltpu.make_async_copy(sums_s, sums_v, csem.at[1])
+    to_vmem.start()
+    to_vmem.wait()
+    me_f = ((me[0] * n_a + me[1]) * n_x + me[2]).astype(jnp.float32)
+    both = sums_v[...]
+    aux = aux_ref[...]
+    refine, migrate, owner = aux[0:1], aux[1:2], aux[2:3]
+    smooth = 0.5 * both[1:2] + 0.5 * (both[0:1] / 6.0)
+    moved = jnp.where(owner != me_f, 1.0, 0.0)
+    cost = smooth * (1.0 + 7.0 * refine) + 0.25 * migrate * moved
+    cost_out[...] = cost
+    lane = lax.broadcasted_iota(jnp.int32, cost.shape, 1)
+    pay[0, 0] = jnp.where(lane < width, cost, pltpu.roll(owner, width, 1))
+    pl.semaphore_wait(barrier, n_peers)
+    sends = gen_gather_kernel(sizes, groups, pay, o_ref, lsem, ssem, rsem, with_barrier=False)
+    values = o_ref[...]
+    owners = pltpu.roll(values, values.shape[-1] - width, 3)
+    lane4 = lax.broadcasted_iota(jnp.int32, values.shape, 3)
+    picked = jnp.where((lane4 < width) & (owners == me_f), values, 0.0)
+    part = jnp.sum(picked, axis=(0, 1))
+    total = jnp.sum(part, axis=0, keepdims=True)
+    total = jnp.sum(total, axis=1, keepdims=True)
+    load_out[...] = (total / float(width)).reshape(1, 1, 1)
+    for c in sends:
+        c.wait_send()
+
+
+def cost_load(gathered_means, neighbor_list, refine_flag, migrate_weight, owner_map, blocks, groups=((2, 1), (0,))):
+    sizes = tuple(lax.axis_size(a) for a in AXES)
+    width = refine_flag.size
+    lanes = 128
+    links = sum(len(offs) for _, offs in stage_plan(sizes, groups))
+    aux = jnp.stack([refine_flag.reshape(-1), migrate_weight.reshape(-1), owner_map.reshape(-1)]).astype(jnp.float32)
+    aux = jnp.pad(aux, ((0, 0), (0, lanes - width)))
+    vmem = pl.BlockSpec(memory_space=pltpu.VMEM)
+    cost, load = pl.pallas_call(
+        functools.partial(cost_load_kernel, sizes, groups, blocks),
+        out_shape=(jax.ShapeDtypeStruct((1, lanes), jnp.float32), jax.ShapeDtypeStruct((1, 1, 1), jnp.float32)),
+        in_specs=[pl.BlockSpec(memory_space=pltpu.SMEM), vmem, vmem],
+        out_specs=(vmem, vmem),
+        scratch_shapes=[
+            pltpu.SMEM(gathered_means.shape, jnp.float32),
+            pltpu.SMEM((2, lanes), jnp.float32),
+            pltpu.VMEM((2, lanes), jnp.float32),
+            pltpu.VMEM((1, 1, 1, lanes), jnp.float32),
+            pltpu.VMEM(sizes + (lanes,), jnp.float32),
+            pltpu.SemaphoreType.DMA((2,)),
+            pltpu.SemaphoreType.DMA(()),
+            pltpu.SemaphoreType.DMA((links,)),
+            pltpu.SemaphoreType.DMA((links,)),
+        ],
+        compiler_params=pltpu.CompilerParams(collective_id=1, has_side_effects=True),
+    )(neighbor_list.reshape(-1), gathered_means, aux)
+    return cost[0, :width].reshape(refine_flag.shape), load
 
 
 def gather_all(values, cid, groups=((2, 1), (0,))):
@@ -408,41 +503,7 @@
     per_rad = rows_rad // BLK
     per_azi = rows_azi // BLK
     per_ax = rows_ax // BLK
-    block_mean = lax.dynamic_slice(
-        gathered_means, (lax.axis_index("rad"), lax.axis_index("azi"), lax.axis_index("ax"), 0),
-        (1, 1, 1, gathered_means.shape[3]),
-    ).reshape(per_rad, per_azi, per_ax)
-    size_rad = lax.axis_size("rad")
-    size_azi = lax.axis_size("azi")
-    size_ax = lax.axis_size("ax")
-    blocks_azi = per_azi * size_azi
-    blocks_ax = per_ax * size_ax
-    block_rad = neighbor_list // (blocks_azi * blocks_ax)
-    block_azi = neighbor_list // blocks_ax % blocks_azi
-    block_ax = neighbor_list % blocks_ax
-    owner_dev = (
-        block_rad // per_rad * size_azi + block_azi // per_azi
-    ) * size_ax + block_ax // per_ax
-    local_pos = (block_rad % per_rad * per_azi + block_azi % per_azi) * per_ax + block_ax % per_ax
-    dev_rad = owner_dev // (size_azi * size_ax)
-    dev_azi = owner_dev // size_ax % size_azi
-    dev_ax = owner_dev % size_ax
-    beside_all = jnp.mean(gathered_means[dev_rad, dev_azi, dev_ax, local_pos], axis=-1)
-    smooth = 0.5 * block_mean + 0.5 * beside_all
-    own_index = (
-        lax.axis_index("rad") * size_azi + lax.axis_index("azi")
-    ) * size_ax + lax.axis_index("ax")
-    moved = (owner_map != own_index).astype(jnp.float32)
-    block_cost = (
-        smooth * (1.0 + 7.0 * refine_flag.astype(jnp.float32))
-        + 0.25 * migrate_weight.astype(jnp.float32) * moved
-    )
-    width = block_cost.size
-    payload = jnp.concatenate([
-        block_cost.reshape(-1), owner_map.reshape(-1).astype(jnp.float32),
-        jnp.zeros((128 - 2 * width,), jnp.float32),
-    ])
-    owner_load = load_gather(payload, width)
+    block_cost, owner_load = cost_load(gathered_means, neighbor_list, refine_flag, migrate_weight, owner_map, (per_rad, per_azi, per_ax))
     return (indicator, block_cost, owner_load)
 
 

time: 60.8 us -> 63.8 us (1.049)
  local copies, waits for them, and re-layouts: 3.07 us -> 7.18 us
  other arithmetic: 3.05 us -> 0.01 us
  Pallas kernels: 51.8 us -> 53.9 us
    another operation x0 -> x4, local copies, waits for them, and re-layouts: none -> 2.92 us  [the longest x3 2.28 us: cost_load(): jnp.stack([refine_flag.reshape(-1), migrate_weight.reshape(-1), owner_map...]
    pallas_call x1, Pallas kernels: 17.1 us -> 19.5 us  [cost_load(): pl.pallas_call(functools.partial(cost_load_kernel, sizes, groups, blocks)...]
    gather x2 -> x0, local copies, waits for them, and re-layouts: 1.9 us -> none  [on_device(): gathered_means[dev_rad, dev_azi, dev_ax, local_pos]]
    unnamed x13 -> x2, local copies, waits for them, and re-layouts: 0.74 us -> 2.44 us
    broadcast_in_dim x2 -> x0, other arithmetic: 1.56 us -> none  [on_device(): gathered_means[dev_rad, dev_azi, dev_ax, local_pos]]
    mul x1 -> x0, other arithmetic: 0.76 us -> none  [on_device(): smooth = 0.5 * block_mean + 0.5 * beside_all]
where the time goes in v11:
time: 63.8 us; the launch traced here: 63.5 us
  Pallas kernels  53.9 us (84%)
  local copies, waits for them, and re-layouts  7.18 us (11%)
  between operations  2.4 us (4%)
    pallas_call x1, Pallas kernels, stencil(): pl.pallas_call(functools.partial(stencil_kernel, groups), out_shape=(jax....  34.4 us
    pallas_call x1, Pallas kernels, cost_load(): pl.pallas_call(functools.partial(cost_load_kernel, sizes, groups, blocks)...  19.5 us
    unnamed x2, local copies, waits for them, and re-layouts  2.44 us
    another operation x3, local copies, waits for them, and re-layouts, cost_load(): jnp.stack([refine_flag.reshape(-1), migrate_weight.reshape(-1), owner_map...  2.28 us

profile of v11, /device:TPU:1, one launch (start us, length us, event | category | flops | bytes accessed | tf_op | source)
XLA Modules:
  0.0 63.5 jit_solution(13158452589687681570)
XLA Ops:
  0.6 0.8 %stack_reshape.9 = s32[1,16]{1,0:T(1,128)S(1)} reshape(s32[1,2,8]{2,1,0:T(2,128)} %param.8) | data formatting | bytes 128 | tf_op jit(solution)/shard_map/stack;reshape | solution.py:192
  1.4 0.8 %stack_reshape.11 = s32[1,16]{1,0:T(1,128)S(1)} reshape(s32[1,2,8]{2,1,0:T(2,128)} %param.9) | data formatting | bytes 128 | tf_op jit(solution)/shard_map/stack;reshape | solution.py:192
  2.1 0.8 %stack_reshape.10 = s32[1,16]{1,0:T(1,128)S(1)} reshape(s32[1,2,8]{2,1,0:T(2,128)} %param.10) | data formatting | bytes 128 | tf_op jit(solution)/shard_map/stack;reshape | solution.py:192
  2.9 0.6 pad.4.aux_ref
  3.5 0.8 %copy.10 = s32[1,2,8,6]{3,2,1,0:T(8,128)S(1)} copy(s32[1,2,8,6]{2,1,3,0:T(2,128)} %param.11) | data formatting | bytes 768 | tf_op args[5]
  4.3 0.6 reshape.9.nl_ref
  4.9 34.4 %shard_map.85 = (f32[16,32,128]{2,1,0:T(8,128)}, f32[8,8,4,16]{3,2,1,0:T(4,128)}) custom-call(f32[5,16,32,128]{3,2,1,0:T(8,128)} %p_hbm.1, f32[5,16,32,128]{3,2,1,0:T(8,128)} %a_hbm.1), custom_call_target="tpu_custom_call" | custom-call | tf_op jit(solution)/shard_map/pallas_call | solution.py:473
  39.3 19.5 %shard_map.86 = (f32[1,128]{1,0:T(1,128)}, f32[1,1,1]{2,1,0:T(1,128)}) custom-call(s32[96]{0:T(128)} %reshape.9.nl_ref, f32[8,8,4,16]{3,2,1,0:T(4,128)} %get-tuple-element.8.gm_ref, f32[3,128]{1,0:T(4,128)} %pad.4.aux_ref), custom_call_target="tpu_custom_call" | custom-call | tf_op jit(solution)/shard_map/pallas_call | solution.py:195
  58.8 0.6 slice_reduce_fusion
  59.4 0.6 %reshape_squeeze.3 = f32[1,2,8]{2,1,0:T(2,128)} reshape(f32[16]{0:T(128)S(1)} %slice_reduce_fusion) | data formatting | bytes 128 | tf_op jit(solution)/shard_map/reshape;squeeze | solution.py:213
  60.1 1.7 %copy.13 = f32[16,32,128]{2,1,0:T(8,128)} copy(f32[16,32,128]{2,1,0:T(8,128)} %get-tuple-element.14) | data formatting | bytes 524288
  (1 shorter events, 0.0 us)

commit v12 on v11

--- a/solution.py
+++ b/solution.py
@@ -118,7 +118,7 @@
     )(payload.reshape(1, 1, 1, lanes))
 
 
-def cost_load_kernel(sizes, groups, blocks, nl_ref, gm_ref, aux_ref, cost_out, load_out,
+def cost_load_kernel(sizes, groups, blocks, nl_ref, gm_ref, rf_ref, mw_ref, ow_ref, cost_out, load_out,
                      gm_s, sums_s, sums_v, pay, o_ref, csem, lsem, ssem, rsem):
     n_r, n_a, n_x = sizes
     per_rad, per_azi, per_ax = blocks
@@ -157,19 +157,22 @@
             total = val if total is None else total + val
         sums_s[0, b] = total
         sums_s[1, b] = gm_s[me[0], me[1], me[2], b]
+    me_i = (me[0] * n_a + me[1]) * n_x + me[2]
+    me_f = me_i.astype(jnp.float32)
+    for b in range(width):
+        i0, i1 = b // per_ax, b % per_ax
+        smooth = 0.5 * sums_s[1, b] + 0.5 * (sums_s[0, b] * (1.0 / 6.0))
+        own = ow_ref[0, i0, i1]
+        gain = 1.0 + 7.0 * rf_ref[0, i0, i1].astype(jnp.float32)
+        extra = jnp.where(own != me_i, 0.25 * mw_ref[0, i0, i1].astype(jnp.float32), 0.0)
+        c = smooth * gain + extra
+        cost_out[0, i0, i1] = c
+        sums_s[0, b] = c
+        sums_s[0, width + b] = own.astype(jnp.float32)
     to_vmem = pltpu.make_async_copy(sums_s, sums_v, csem.at[1])
     to_vmem.start()
     to_vmem.wait()
-    me_f = ((me[0] * n_a + me[1]) * n_x + me[2]).astype(jnp.float32)
-    both = sums_v[...]
-    aux = aux_ref[...]
-    refine, migrate, owner = aux[0:1], aux[1:2], aux[2:3]
-    smooth = 0.5 * both[1:2] + 0.5 * (both[0:1] / 6.0)
-    moved = jnp.where(owner != me_f, 1.0, 0.0)
-    cost = smooth * (1.0 + 7.0 * refine) + 0.25 * migrate * moved
-    cost_out[...] = cost
-    lane = lax.broadcasted_iota(jnp.int32, cost.shape, 1)
-    pay[0, 0] = jnp.where(lane < width, cost, pltpu.roll(owner, width, 1))
+    pay[0, 0] = sums_v[0:1]
     pl.semaphore_wait(barrier, n_peers)
     sends = gen_gather_kernel(sizes, groups, pay, o_ref, lsem, ssem, rsem, with_barrier=False)
     values = o_ref[...]
@@ -189,14 +192,13 @@
     width = refine_flag.size
     lanes = 128
     links = sum(len(offs) for _, offs in stage_plan(sizes, groups))
-    aux = jnp.stack([refine_flag.reshape(-1), migrate_weight.reshape(-1), owner_map.reshape(-1)]).astype(jnp.float32)
-    aux = jnp.pad(aux, ((0, 0), (0, lanes - width)))
+    smem = pl.BlockSpec(memory_space=pltpu.SMEM)
     vmem = pl.BlockSpec(memory_space=pltpu.VMEM)
     cost, load = pl.pallas_call(
         functools.partial(cost_load_kernel, sizes, groups, blocks),
-        out_shape=(jax.ShapeDtypeStruct((1, lanes), jnp.float32), jax.ShapeDtypeStruct((1, 1, 1), jnp.float32)),
-        in_specs=[pl.BlockSpec(memory_space=pltpu.SMEM), vmem, vmem],
-        out_specs=(vmem, vmem),
+        out_shape=(jax.ShapeDtypeStruct(refine_flag.shape, jnp.float32), jax.ShapeDtypeStruct((1, 1, 1), jnp.float32)),
+        in_specs=[smem, vmem, smem, smem, smem],
+        out_specs=(smem, vmem),
         scratch_shapes=[
             pltpu.SMEM(gathered_means.shape, jnp.float32),
             pltpu.SMEM((2, lanes), jnp.float32),
@@ -209,8 +211,8 @@
             pltpu.SemaphoreType.DMA((links,)),
         ],
         compiler_params=pltpu.CompilerParams(collective_id=1, has_side_effects=True),
-    )(neighbor_list.reshape(-1), gathered_means, aux)
-    return cost[0, :width].reshape(refine_flag.shape), load
+    )(neighbor_list.reshape(-1), gathered_means, refine_flag, migrate_weight, owner_map)
+    return cost, load
 
 
 def gather_all(values, cid, groups=((2, 1), (0,))):

time: 63.8 us -> 61 us (0.956)
  local copies, waits for them, and re-layouts: 7.18 us -> 4.29 us
    another operation x4 -> x0, local copies, waits for them, and re-layouts: 2.92 us -> none  [the longest x3 2.28 us: cost_load(): jnp.stack([refine_flag.reshape(-1), migrate_weight.reshape(-1), owner_map...]
    unnamed x2 -> x3, local copies, waits for them, and re-layouts: 2.44 us -> 3.69 us
where the time goes in v12:
time: 61 us; the launch traced here: 60.8 us
  Pallas kernels  54.2 us (89%)
  local copies, waits for them, and re-layouts  4.29 us (7%)
  between operations  2.35 us (4%)
    pallas_call x1, Pallas kernels, stencil(): pl.pallas_call(functools.partial(stencil_kernel, groups), out_shape=(jax....  34.7 us
    pallas_call x1, Pallas kernels, cost_load(): pl.pallas_call(functools.partial(cost_load_kernel, sizes, groups, blocks)...  19.4 us
    unnamed x3, local copies, waits for them, and re-layouts  3.69 us

profile of v12, /device:TPU:1, one launch (start us, length us, event | category | flops | bytes accessed | tf_op | source)
XLA Modules:
  0.0 60.8 jit_solution(16378616270948439809)
XLA Ops:
  0.6 34.7 %shard_map.85 = (f32[16,32,128]{2,1,0:T(8,128)}, f32[8,8,4,16]{3,2,1,0:T(4,128)}) custom-call(f32[5,16,32,128]{3,2,1,0:T(8,128)} %p_hbm.1, f32[5,16,32,128]{3,2,1,0:T(8,128)} %a_hbm.1), custom_call_target="tpu_custom_call" | custom-call | tf_op jit(solution)/shard_map/pallas_call | solution.py:475
  35.4 0.8 %copy.10 = s32[1,2,8,6]{3,2,1,0:T(8,128)S(1)} copy(s32[1,2,8,6]{2,1,3,0:T(2,128)} %param.11) | data formatting | bytes 768 | tf_op args[5]
  36.1 0.6 reshape.9.nl_ref
  36.7 19.4 %shard_map.86 = (f32[1,2,8]{2,1,0:T(2,128)}, f32[1,1,1]{2,1,0:T(1,128)}) custom-call(s32[96]{0:T(128)} %reshape.9.nl_ref, f32[8,8,4,16]{3,2,1,0:T(4,128)} %get-tuple-element.8.gm_ref, s32[1,2,8]{2,1,0:T(2,128)} %rf_ref.1, s32[1,2,8]{2,1,0:T(2,128)} %mw_ref.1, s32[1,2,8]{2,1,0:T(2,128)} %ow_ref.1), custom_call_target="tpu_custom_call" | custom-call | tf_op jit(solution)/shard_map/pallas_call | solution.py:197
  56.2 1.7 %copy.14 = f32[16,32,128]{2,1,0:T(8,128)} copy(f32[16,32,128]{2,1,0:T(8,128)} %get-tuple-element.14) | data formatting | bytes 524288
  57.8 1.2 %copy.15 = f32[1,2,8]{2,1,0:T(2,128)} copy(f32[1,2,8]{2,1,0:T(2,128)} %get-tuple-element.15) | data formatting | bytes 128

commit v13 on v10

--- a/solution.py
+++ b/solution.py
@@ -305,18 +305,10 @@
                         jnp.where(lane == n_x - 2, jnp.broadcast_to(hi0, u.shape), pltpu.roll(u, n_x - 2, 1)))
         return um2, um1, u, up1, up2
 
-    def row_body(r, carry):
+    def row_rest(r, balance, weight):
         base = pl.multiple_of(r * n_a, n_a)
         xlo = xt[0, pl.ds(base, n_a), :]
         xhi = xt[1, pl.ds(base, n_a), :]
-        lo_s, hi_s, w = [], [], []
-        for f in range(fields):
-            lo, hi = faces(*[e[0, f, r + k] for k in range(5)])
-            lo_s.append(lo)
-            hi_s.append(hi)
-            w.append(fourth(*[e[1, f, r + k] for k in range(5)]))
-        balance = flux_pair(lo_s, hi_s, 0)
-        weight = w
         lo_s, hi_s, w = [], [], []
         for f in range(fields):
             lo, hi = faces(*shifted_azi(e[0, f, r + 2], az_exp[0, r, f], az_exp[1, r, f]))
@@ -343,9 +335,27 @@
             total = total + weight[f] * balance[f]
         value = jnp.abs(total)
         out_ref[r] = value
-        return carry + value
-
-    acc = lax.fori_loop(2, rows - 2, row_body, jnp.zeros((n_a, n_x), jnp.float32))
+        return value
+
+    def radial_weight(r):
+        return [fourth(*[e[1, f, r + k] for k in range(5)]) for f in range(fields)]
+
+    def row_body(r, carry):
+        lo_s, hi_s = [], []
+        for f in range(fields):
+            lo, hi = faces(*[e[0, f, r + k] for k in range(5)])
+            lo_s.append(lo)
+            hi_s.append(hi)
+        return carry + row_rest(r, flux_pair(lo_s, hi_s, 0), radial_weight(r))
+
+    def row_body_carry(r, carry):
+        acc, flux_lo = carry
+        flux_hi = euler_flux([faces(*[e[0, f, r + k] for k in range(5)])[1] for f in range(fields)], 0)
+        balance = [h - l for h, l in zip(flux_hi, flux_lo)]
+        return acc + row_rest(r, balance, radial_weight(r)), flux_hi
+
+    first_lo = euler_flux([faces(*[e[0, f, 2 + k] for k in range(5)])[0] for f in range(fields)], 0)
+    acc, _ = lax.fori_loop(2, rows - 2, row_body_carry, (jnp.zeros((n_a, n_x), jnp.float32), first_lo))
     for cond, c in recvs[:2]:
         when(cond, c.wait_recv)
     acc = lax.fori_loop(0, 2, row_body, acc)

time: 60.8 us -> 60.4 us (level)
  no operation moved by 1% of the time
where the time goes in v13:
time: 60.4 us; the launch traced here: 60.1 us
  Pallas kernels  51.4 us (85%)
  local copies, waits for them, and re-layouts  3.07 us (5%)
  other arithmetic  3.05 us (5%)
  between operations  2.59 us (4%)
    pallas_call x1, Pallas kernels, stencil(): pl.pallas_call(functools.partial(stencil_kernel, groups), out_shape=(jax....  34.4 us
    pallas_call x1, Pallas kernels, load_gather(): pl.pallas_call(functools.partial(load_kernel, sizes, groups, width), out_...  17.1 us
    gather x2, local copies, waits for them, and re-layouts, on_device(): gathered_means[dev_rad, dev_azi, dev_ax, local_pos]  1.9 us
    broadcast_in_dim x2, other arithmetic, on_device(): gathered_means[dev_rad, dev_azi, dev_ax, local_pos]  1.56 us

profile of v13, /device:TPU:1, one launch (start us, length us, event | category | flops | bytes accessed | tf_op | source)
XLA Modules:
  0.0 60.1 jit_solution(1274342877646623857)
XLA Ops:
  0.6 34.4 %shard_map.85 = (f32[16,32,128]{2,1,0:T(8,128)}, f32[8,8,4,16]{3,2,1,0:T(4,128)}) custom-call(f32[5,16,32,128]{3,2,1,0:T(8,128)} %p_hbm.1, f32[5,16,32,128]{3,2,1,0:T(8,128)} %a_hbm.1), custom_call_target="tpu_custom_call" | custom-call | tf_op jit(solution)/shard_map/pallas_call | solution.py:388
  35.0 0.0 copy-start
  35.0 0.8 %multiply_reduce_fusion = f32[16]{0:T(128)S(1)} fusion(f32[8,8,4,16]{3,2,1,0:T(4,128)} %get-tuple-element.6, s32[]{:T(128)S(6)} %select_n.74, s32[]{:T(128)S(6)} %select_n.75, s32[]{:T(128)S(6)} %select_n.76), kind=kLoop, calls=%fused_computation.74 | loop fusion | flops 16 | bytes 140 | tf_op jit(solution)/shard_map/mul | solution.py:441
  35.8 0.1 mul.63
  35.9 0.8 %fusion.6 = (s32[1,2,8,6,1]{2,1,3,4,0:T(2,128)S(1)}, s32[1,2,8,6]{2,1,3,0:T(2,128)S(1)}, s32[1,2,8,6]{2,1,3,0:T(2,128)S(1)}) fusion(s32[1,2,8,6]{2,1,3,0:T(2,128)} %param.11), kind=kLoop, calls=%fused_computation.44 | loop fusion | flops 8832 | bytes 1536 | tf_op jit(solution)/shard_map/broadcast_in_dim | solution.py:440
  36.7 0.8 %fusion.7 = (s32[1,2,8,6,1]{2,1,3,4,0:T(2,128)S(1)}, s32[1,2,8,6,1]{2,1,3,4,0:T(2,128)S(1)}, s32[1,2,8,6,1]{2,1,3,4,0:T(2,128)S(1)}) fusion(s32[1,2,8,6]{2,1,3,0:T(2,128)S(1)} %get-tuple-element.8, s32[1,2,8,6]{2,1,3,0:T(2,128)} %param.11, s32[1,2,8,6]{2,1,3,0:T(2,128)S(1)} %get-tuple-element.9), kind=kLoop, calls=%fused_computation.45 | loop fusion | flops 7104 | bytes 2304 | tf_op jit(solution)/shard_map/broadcast_in_dim | solution.py:440
  37.5 0.1 copy.10
  37.6 0.1 reshape.51
  37.7 0.0 copy-done
  37.7 0.0 copy-start.2
  37.7 0.0 copy-start.3
  37.7 0.0 copy-start.4
  37.7 0.0 copy-start.1
  37.7 1.8 %gather_fusion = f32[96]{0:T(128)S(1)} fusion(f32[8,8,4,16]{3,2,1,0:T(4,128)S(1)} %copy-done, s32[96]{0:T(128)S(1)} %reshape.51), kind=kCustom, calls=%fused_computation | custom fusion | bytes 2304 | tf_op jit(solution)/shard_map/gather | solution.py:440
  39.5 0.1 reshape.54
  39.6 0.1 reduce.1
  39.7 0.0 copy-done.2
  39.7 0.0 copy-done.3
  39.7 0.0 copy-done.4
  39.7 0.0 copy-start.5
  39.8 0.1 reshape.47
  39.8 0.1 convert_element_type.16
  39.9 0.6 maximum_bitcast_fusion.x_ref
  40.5 17.1 %shard_map.86 = f32[1,1,1]{2,1,0:T(1,128)} custom-call(f32[1,1,1,128]{3,2,1,0:T(1,128)} %maximum_bitcast_fusion.x_ref), custom_call_target="tpu_custom_call" | custom-call | tf_op jit(solution)/shard_map/pallas_call | solution.py:106
  57.6 0.0 copy-done.1
  57.6 0.7 %copy.13 = f32[16,32,128]{2,1,0:T(8,128)} copy(f32[16,32,128]{2,1,0:T(8,128)S(1)} %copy-done.1) | data formatting | bytes 524288
  59.0 0.0 copy-done.5
  (5 shorter events, 0.1 us)
Async XLA Ops:
  35.0 2.6 %copy-start = (f32[8,8,4,16]{3,2,1,0:T(4,128)S(1)}, f32[8,8,4,16]{3,2,1,0:T(4,128)}, u32[]{:S(2)}) copy-start(f32[8,8,4,16]{3,2,1,0:T(4,128)} %get-tuple-element.6) | copy-start | bytes 49156
  37.7 2.0 %copy-start.2 = (s32[1,2,8]{2,1,0:T(2,128)S(1)}, s32[1,2,8]{2,1,0:T(2,128)}, u32[]{:S(2)}) copy-start(s32[1,2,8]{2,1,0:T(2,128)} %param.9) | copy-start | bytes 196
  37.7 2.0 %copy-start.3 = (s32[1,2,8]{2,1,0:T(2,128)S(1)}, s32[1,2,8]{2,1,0:T(2,128)}, u32[]{:S(2)}) copy-start(s32[1,2,8]{2,1,0:T(2,128)} %param.10) | copy-start | bytes 196
  37.7 2.0 %copy-start.4 = (s32[1,2,8]{2,1,0:T(2,128)S(1)}, s32[1,2,8]{2,1,0:T(2,128)}, u32[]{:S(2)}) copy-start(s32[1,2,8]{2,1,0:T(2,128)} %param.8) | copy-start | bytes 196
  37.7 19.9 %copy-start.1 = (f32[16,32,128]{2,1,0:T(8,128)S(1)}, f32[16,32,128]{2,1,0:T(8,128)}, u32[]{:S(2)}) copy-start(f32[16,32,128]{2,1,0:T(8,128)} %get-tuple-element.16) | copy-start | bytes 786436
  39.7 19.3 %copy-start.5 = (f32[1,2,8]{2,1,0:T(2,128)}, f32[1,2,8]{2,1,0:T(2,128)S(1)}, u32[]{:S(2)}) copy-start(f32[1,2,8]{2,1,0:T(2,128)S(1)} %fusion.17) | copy-start | bytes 196

commit v14 on v12

--- a/solution.py
+++ b/solution.py
@@ -119,20 +119,21 @@
 
 
 def cost_load_kernel(sizes, groups, blocks, nl_ref, gm_ref, rf_ref, mw_ref, ow_ref, cost_out, load_out,
-                     gm_s, sums_s, sums_v, pay, o_ref, csem, lsem, ssem, rsem):
+                     gm_s, sums_s, sums_v, pay, o_ref, csem, lsem, ssem, rsem, with_barrier=True):
     n_r, n_a, n_x = sizes
     per_rad, per_azi, per_ax = blocks
     width = per_rad * per_azi * per_ax
     me = tuple(lax.axis_index(a) for a in AXES)
-    barrier = pltpu.get_barrier_semaphore()
-    n_peers = 0
-    for axes, offs in stage_plan(sizes, groups):
-        for off in offs:
-            dev = list(me)
-            for i, o in zip(axes, off):
-                dev[i] = lax.rem(me[i] + o, sizes[i])
-            pl.semaphore_signal(barrier, 1, device_id=tuple(dev), device_id_type=MESH)
-            n_peers += 1
+    if with_barrier:
+        barrier = pltpu.get_barrier_semaphore()
+        n_peers = 0
+        for axes, offs in stage_plan(sizes, groups):
+            for off in offs:
+                dev = list(me)
+                for i, o in zip(axes, off):
+                    dev[i] = lax.rem(me[i] + o, sizes[i])
+                pl.semaphore_signal(barrier, 1, device_id=tuple(dev), device_id_type=MESH)
+                n_peers += 1
     to_smem = pltpu.make_async_copy(gm_ref, gm_s, csem.at[0])
     to_smem.start()
 
@@ -173,7 +174,8 @@
     to_vmem.start()
     to_vmem.wait()
     pay[0, 0] = sums_v[0:1]
-    pl.semaphore_wait(barrier, n_peers)
+    if with_barrier:
+        pl.semaphore_wait(barrier, n_peers)
     sends = gen_gather_kernel(sizes, groups, pay, o_ref, lsem, ssem, rsem, with_barrier=False)
     values = o_ref[...]
     owners = pltpu.roll(values, values.shape[-1] - width, 3)
@@ -271,8 +273,9 @@
     return (zm2 - 4.0 * zm1 + 6.0 * z - 4.0 * zp1 + zp2) / 12.0
 
 
-def stencil_kernel(groups, p_hbm, a_hbm, out_ref, g_out, e, az_send, az_recv, az_exp, x_send, x_recv, xt, sems, ssem, rsem,
-                   pay, glsem, gssem, grsem):
+def stencil_kernel(groups, p_hbm, a_hbm, nl_ref, rf_ref, mw_ref, ow_ref, out_ref, cost_out, load_out, g_out, e, az_send, az_recv, az_exp, x_send, x_recv, xt, sems, ssem, rsem,
+                   pay, glsem, gssem, grsem,
+                   gm_s, sums_s, sums_v, pay2, o2, csem, lsem2, ssem2, rsem2):
     _, fields, ext_rows, n_a, n_x = e.shape
     rows = ext_rows - 4
     n_r_dev, n_a_dev, n_x_dev = (lax.axis_size(ax) for ax in AXES)
@@ -462,11 +465,13 @@
 
     for cond, c in sends:
         when(cond, c.wait_send)
+    cost_load_kernel(sizes, groups, (rows // BLK, n_a // BLK, n_x // BLK), nl_ref, g_out, rf_ref, mw_ref, ow_ref,
+                     cost_out, load_out, gm_s, sums_s, sums_v, pay2, o2, csem, lsem2, ssem2, rsem2, with_barrier=False)
     for c in sends_g:
         c.wait_send()
 
 
-def stencil(primal, adjoint, groups=((2, 1), (0,))):
+def stencil(primal, adjoint, neighbor_list, refine_flag, migrate_weight, owner_map, groups=((2, 1), (0,))):
     fields, rows, n_a, n_x = primal.shape
     anywhere = pl.BlockSpec(memory_space=pltpu.HBM)
     sizes = tuple(lax.axis_size(a) for a in AXES)
@@ -474,10 +479,19 @@
     links = sum(len(offs) for _, offs in stage_plan(sizes, groups))
     return pl.pallas_call(
         functools.partial(stencil_kernel, groups),
-        out_shape=(jax.ShapeDtypeStruct((rows, n_a, n_x), jnp.float32), jax.ShapeDtypeStruct(sizes + (width,), jnp.float32)),
-        in_specs=[anywhere, anywhere],
-        out_specs=(pl.BlockSpec(memory_space=pltpu.VMEM), pl.BlockSpec(memory_space=pltpu.VMEM)),
+        out_shape=(
+            jax.ShapeDtypeStruct((rows, n_a, n_x), jnp.float32),
+            jax.ShapeDtypeStruct(refine_flag.shape, jnp.float32),
+            jax.ShapeDtypeStruct((1, 1, 1), jnp.float32),
+        ),
+        in_specs=[anywhere, anywhere] + [pl.BlockSpec(memory_space=pltpu.SMEM)] * 4,
+        out_specs=(
+            pl.BlockSpec(memory_space=pltpu.VMEM),
+            pl.BlockSpec(memory_space=pltpu.SMEM),
+            pl.BlockSpec(memory_space=pltpu.VMEM),
+        ),
         scratch_shapes=[
+            pltpu.VMEM(sizes + (width,), jnp.float32),
             pltpu.VMEM((2, fields, rows + 4, n_a, n_x), jnp.float32),
             pltpu.VMEM((2, 2 * fields * rows * 2, n_x), jnp.float32),
             pltpu.VMEM((2, 2 * fields * rows * 2, n_x), jnp.float32),
@@ -492,20 +506,28 @@
             pltpu.SemaphoreType.DMA(()),
             pltpu.SemaphoreType.DMA((links,)),
             pltpu.SemaphoreType.DMA((links,)),
+            pltpu.SMEM(sizes + (width,), jnp.float32),
+            pltpu.SMEM((2, 128), jnp.float32),
+            pltpu.VMEM((2, 128), jnp.float32),
+            pltpu.VMEM((1, 1, 1, 128), jnp.float32),
+            pltpu.VMEM(sizes + (128,), jnp.float32),
+            pltpu.SemaphoreType.DMA((2,)),
+            pltpu.SemaphoreType.DMA(()),
+            pltpu.SemaphoreType.DMA((links,)),
+            pltpu.SemaphoreType.DMA((links,)),
         ],
         compiler_params=pltpu.CompilerParams(
             collective_id=2, has_side_effects=True, vmem_limit_bytes=67043328
         ),
-    )(primal, adjoint)
+    )(primal, adjoint, neighbor_list.reshape(-1), refine_flag, migrate_weight, owner_map)
 
 
 def on_device(primal, adjoint, refine_flag, owner_map, migrate_weight, neighbor_list):
-    indicator, gathered_means = stencil(primal, adjoint)
+    indicator, block_cost, owner_load = stencil(primal, adjoint, neighbor_list, refine_flag, migrate_weight, owner_map)
     rows_rad, rows_azi, rows_ax = indicator.shape
     per_rad = rows_rad // BLK
     per_azi = rows_azi // BLK
     per_ax = rows_ax // BLK
-    block_cost, owner_load = cost_load(gathered_means, neighbor_list, refine_flag, migrate_weight, owner_map, (per_rad, per_azi, per_ax))
     return (indicator, block_cost, owner_load)
 
 

time: 61 us -> 59.7 us (0.979)
  Pallas kernels: 54.2 us -> 52.9 us
    pallas_call x1 -> x0, Pallas kernels: 19.4 us -> none  [cost_load(): pl.pallas_call(functools.partial(cost_load_kernel, sizes, groups, blocks)...]
    pallas_call x1, Pallas kernels: 34.7 us -> 52.9 us  [stencil(): pl.pallas_call(functools.partial(stencil_kernel, groups), out_shape=(jax....]
where the time goes in v14:
time: 59.7 us; the launch traced here: 59.5 us
  Pallas kernels  52.9 us (89%)
  local copies, waits for them, and re-layouts  4.28 us (7%)
  between operations  2.32 us (4%)
    pallas_call x1, Pallas kernels, stencil(): pl.pallas_call(functools.partial(stencil_kernel, groups), out_shape=(jax....  52.9 us
    unnamed x3, local copies, waits for them, and re-layouts  3.68 us

profile of v14, /device:TPU:1, one launch (start us, length us, event | category | flops | bytes accessed | tf_op | source)
XLA Modules:
  0.0 59.5 jit_solution(11992982628696029856)
XLA Ops:
  0.6 0.8 %copy.10 = s32[1,2,8,6]{3,2,1,0:T(8,128)S(1)} copy(s32[1,2,8,6]{2,1,3,0:T(2,128)} %param.11) | data formatting | bytes 768 | tf_op args[5]
  1.4 0.6 %reshape.9.nl_ref = s32[96]{0:T(128)} reshape(s32[1,2,8,6]{3,2,1,0:T(8,128)S(1)} %copy.10) | data formatting | bytes 768 | tf_op jit(solution)/shard_map/reshape | solution.py:522
  2.0 52.9 %shard_map.85 = (f32[16,32,128]{2,1,0:T(8,128)}, f32[1,2,8]{2,1,0:T(2,128)}, f32[1,1,1]{2,1,0:T(1,128)}) custom-call(f32[5,16,32,128]{3,2,1,0:T(8,128)} %p_hbm.1, f32[5,16,32,128]{3,2,1,0:T(8,128)} %a_hbm.1, s32[96]{0:T(128)} %reshape.9.nl_ref, s32[1,2,8]{2,1,0:T(2,128)} %rf_ref.1, s32[1,2,8]{2,1,0:T(2,128)} %mw_ref.1, s32[1,2,8]{2,1,0:T(2,128)} %ow_ref.1), custom_call_target="tpu_custom_call" | custom-call | tf_op jit(solution)/shard_map/pallas_call | solution.py:480
  54.9 1.7 %copy.14 = f32[16,32,128]{2,1,0:T(8,128)} copy(f32[16,32,128]{2,1,0:T(8,128)} %get-tuple-element.6) | data formatting | bytes 524288
  56.6 1.2 %copy.15 = f32[1,2,8]{2,1,0:T(2,128)} copy(f32[1,2,8]{2,1,0:T(2,128)} %get-tuple-element.7) | data formatting | bytes 128
